TPU v7x, 32 devices: a whole 2x2x4 slice. The times are simulated.
32 devices in a mesh: dp: 4 (over y, core), fsdp: 8 (over z, x).
Axes of the slice: x: 2, y: 2, z: 4, core: 2. Of those that a mesh axis runs over, the one named last changes fastest.
Arguments:
- tokens: bfloat16 [32, 1024, 512], P(('dp', 'fsdp')), may hold values from -6 to 6
- cotangent: bfloat16 [32, 1024, 512], P(('dp', 'fsdp')), may hold values from -6 to 6
- dataset_ids: int32 [32], P(('dp', 'fsdp')), may hold values from 0 to 7
- query_counts: int32 [32], P(('dp', 'fsdp')), may hold values from 1 to 128
- learn_rate: float32 [1], replicated, may hold values from 0.0002762136 to 0.00082864077
- momentum_coef: float32 [1], replicated, may hold values from 0.4 to 0.6
- average_decay: float32 [1], replicated, may hold values from 0.2 to 0.95
- step_count: int32 [1], replicated, may hold values from 2 to 20
- attend_weight: float32 [2, 512, 1536], P(None, ('dp', 'fsdp')), may hold values from -0.25 to 0.25
- attend_momentum: float32 [2, 512, 1536], P(None, ('dp', 'fsdp')), may hold values from -112 to 112
- attend_average: float32 [2, 512, 1536], P(None, ('dp', 'fsdp')), may hold values from -0.25 to 0.25
- output_weight: float32 [2, 512, 512], P(None, ('dp', 'fsdp')), may hold values from -1.5 to 1.5
- output_momentum: float32 [2, 512, 512], P(None, ('dp', 'fsdp')), may hold values from -20 to 20
- output_average: float32 [2, 512, 512], P(None, ('dp', 'fsdp')), may hold values from -1.5 to 1.5
- expand_weight: float32 [2, 512, 1024], P(None, ('dp', 'fsdp')), may hold values from -0.25 to 0.25
- expand_momentum: float32 [2, 512, 1024], P(None, ('dp', 'fsdp')), may hold values from -320 to 320
- expand_average: float32 [2, 512, 1024], P(None, ('dp', 'fsdp')), may hold values from -0.25 to 0.25
- shrink_weight: float32 [2, 1024, 512], P(None, ('dp', 'fsdp')), may hold values from -0.1875 to 0.1875
- shrink_momentum: float32 [2, 1024, 512], P(None, ('dp', 'fsdp')), may hold values from -320 to 320
- shrink_average: float32 [2, 1024, 512], P(None, ('dp', 'fsdp')), may hold values from -0.1875 to 0.1875
- norm_gains: float32 [2, 2, 512], P(None, None, ('dp', 'fsdp')), may hold values from 0.5 to 1.5
- gains_momentum: float32 [2, 2, 512], P(None, None, ('dp', 'fsdp')), may hold values from -320 to 320
- gains_average: float32 [2, 2, 512], P(None, None, ('dp', 'fsdp')), may hold values from 0.5 to 1.5
- bias_rows: float32 [2, 8, 512], P(None, None, ('dp', 'fsdp')), may hold values from -3 to 3
- bias_momentum: float32 [2, 8, 512], P(None, None, ('dp', 'fsdp')), may hold values from -320 to 320
- bias_average: float32 [2, 8, 512], P(None, None, ('dp', 'fsdp')), may hold values from -3 to 3
Outputs:
- layer_out: bfloat16 [32, 1024, 512], P(('dp', 'fsdp'))
- input_grad: float32 [32, 1024, 512], P(('dp', 'fsdp'))
- attend_velocity: float32 [2, 512, 1536], P(None, ('dp', 'fsdp'))
- attend_smoothed: float32 [2, 512, 1536], P(None, ('dp', 'fsdp'))
- attend_master: float32 [2, 512, 1536], P(None, ('dp', 'fsdp'))
- attend_copy: bfloat16 [2, 512, 1536], P(None, ('dp', 'fsdp'))
- output_velocity: float32 [2, 512, 512], P(None, ('dp', 'fsdp'))
- output_smoothed: float32 [2, 512, 512], P(None, ('dp', 'fsdp'))
- output_master: float32 [2, 512, 512], P(None, ('dp', 'fsdp'))
- output_copy: bfloat16 [2, 512, 512], P(None, ('dp', 'fsdp'))
- expand_velocity: float32 [2, 512, 1024], P(None, ('dp', 'fsdp'))
- expand_smoothed: float32 [2, 512, 1024], P(None, ('dp', 'fsdp'))
- expand_master: float32 [2, 512, 1024], P(None, ('dp', 'fsdp'))
- expand_copy: bfloat16 [2, 512, 1024], P(None, ('dp', 'fsdp'))
- shrink_velocity: float32 [2, 1024, 512], P(None, ('dp', 'fsdp'))
- shrink_smoothed: float32 [2, 1024, 512], P(None, ('dp', 'fsdp'))
- shrink_master: float32 [2, 1024, 512], P(None, ('dp', 'fsdp'))
- shrink_copy: bfloat16 [2, 1024, 512], P(None, ('dp', 'fsdp'))
- gains_velocity: float32 [2, 2, 512], P(None, None, ('dp', 'fsdp'))
- gains_smoothed: float32 [2, 2, 512], P(None, None, ('dp', 'fsdp'))
- gains_master: float32 [2, 2, 512], P(None, None, ('dp', 'fsdp'))
- gains_copy: bfloat16 [2, 2, 512], P(None, None, ('dp', 'fsdp'))
- bias_velocity: float32 [2, 8, 512], P(None, None, ('dp', 'fsdp'))
- bias_smoothed: float32 [2, 8, 512], P(None, None, ('dp', 'fsdp'))
- bias_master: float32 [2, 8, 512], P(None, None, ('dp', 'fsdp'))
- bias_copy: bfloat16 [2, 8, 512], P(None, None, ('dp', 'fsdp'))
All inputs are finite; a program needn't handle non-finite values.
Results may differ from a plain program's by a relative error of at most 0.02.
The roundings to bfloat16 on the way count: a program that leaves them out, or rounds other values in their place, can miss the bound.
Values may be sent and summed in bfloat16 or wider, within the bound.
No kernel may reach another device: no remote copies, remote signals or barrier semaphores. Data moves between devices by JAX's collectives and lax.ppermute only.
A program may use at most 192 MiB of HBM per device.

v0:
```python
import functools

import jax
import jax.numpy as jnp
import numpy as np
from jax import lax
from jax.experimental import pallas as pl
from jax.experimental.pallas import tpu as pltpu
from jax.sharding import PartitionSpec as P

HEADS = 4
CTX = 896
NDS = 8
EPS = 1e-05
OWNERS = 32
AXES = ("dp", "fsdp")

CHAIN = (0, 4, 2, 6)
SQUARE = (0, 1, 16, 17)
CORE = 8
ORDER = tuple(core ^ side ^ link for core in (0, CORE) for side in SQUARE for link in CHAIN)

FIRST_ROWS = 64
SECOND_ROWS = 96

SCORE_BLOCK = 256
ROW_BLOCK = 256
ROOT_HALF = 0.7071067811865476
PDF_PEAK = 0.3989422804014327
VMEM_LIMIT = 60 * 1024 * 1024
SMALL_LIMIT = 12 * 1024 * 1024
FLOAT = jnp.float32
HALF = jnp.bfloat16
LIKE = jax.ShapeDtypeStruct


def product(left, right, left_dim, right_dim):
    return lax.dot_general(
        left, right, (((left_dim,), (right_dim,)), ((), ())), preferred_element_type=FLOAT
    )


def owner_rows(offset, place, rows):
    return pl.ds(pl.multiple_of((offset ^ place) * rows, rows), rows)


def params(limit=VMEM_LIMIT):
    return pltpu.CompilerParams(vmem_limit_bytes=limit)


def pack_kernel(place_ref, ids_ref, attend_ref, output_ref, expand_ref, shrink_ref, gains_ref,
                bias_ref, near_ref, next_ref, late_ref, small):
    width = near_ref.shape[1]
    each = gains_ref.shape[2]
    lane = lax.broadcasted_iota(jnp.int32, (each, width), 1)
    own = lax.broadcasted_iota(jnp.int32, (each, width), 0) + place_ref[0] * each
    pick = (lane == own).astype(HALF)
    lanes = lax.broadcasted_iota(jnp.int32, (1, width), 1)

    for layer in range(attend_ref.shape[0]):
        first, second, top = (
            (near_ref, next_ref, 0) if layer == 0 else (late_ref, late_ref, FIRST_ROWS)
        )
        gains = product(gains_ref[layer].astype(HALF), pick, 1, 0)
        biases = product(bias_ref[layer].astype(HALF), pick, 1, 0)
        for piece in range(3):
            first[piece * 16 : (piece + 1) * 16, :] = attend_ref[
                layer, :, piece * width : (piece + 1) * width
            ].astype(HALF)
        small[...] = jnp.zeros_like(small)
        small[0:2, :] = biases[0:2, :]
        first[48:64, :] = small[...].astype(HALF)
        second[top : top + 16, :] = output_ref[layer].astype(HALF)
        for piece in range(2):
            second[top + (piece + 1) * 16 : top + (piece + 2) * 16, :] = expand_ref[
                layer, :, piece * width : (piece + 1) * width
            ].astype(HALF)
        second[top + 48 : top + 80, :] = shrink_ref[layer].astype(HALF)
        small[0:2, :] = gains
        small[2:8, :] = biases[2:8, :]
        small[8:9, :] = (lanes == ids_ref[0]).astype(FLOAT)
        second[top + 80 : top + 96, :] = small[...].astype(HALF)


def pack_call(place, ids, masters):
    width = masters[1].shape[2]
    rows = (FIRST_ROWS, SECOND_ROWS, FIRST_ROWS + SECOND_ROWS)
    return pl.pallas_call(
        pack_kernel,
        in_specs=[pl.BlockSpec(memory_space=pltpu.SMEM)] * 2
        + [pl.BlockSpec(memory_space=pltpu.VMEM)] * 6,
        out_specs=[pl.BlockSpec(memory_space=pltpu.VMEM)] * 3,
        out_shape=[LIKE((count, width), HALF) for count in rows],
        scratch_shapes=[pltpu.VMEM((16, width), FLOAT)],
        compiler_params=params(),
        cost_estimate=pl.CostEstimate(flops=0, bytes_accessed=1 << 20, transcendentals=0),
        name="pack",
    )(place, ids, *masters)


def join_kernel(cuts, count, *refs):
    each = refs[count].shape[0] // count
    for at in range(count):
        for to, (start, rows) in enumerate(cuts):
            target = refs[count + to]
            if len(refs[at].shape) == 2:
                target[at] = refs[at][start : start + rows, :]
            else:
                target[at * each : (at + 1) * each] = refs[at][:, start : start + rows, :]


def join_call(blocks, *cuts):
    *head, rows, width = blocks[0].shape
    slots = len(blocks) * (head[0] if head else 1)
    cuts = cuts or ((0, rows),)
    return pl.pallas_call(
        functools.partial(join_kernel, cuts, len(blocks)),
        out_shape=[LIKE((slots, rows, width), HALF) for _, rows in cuts],
        compiler_params=params(SMALL_LIMIT),
        cost_estimate=pl.CostEstimate(flops=0, bytes_accessed=1 << 20, transcendentals=0),
        name="join",
    )(*blocks)


def block_sum(refs):
    total = refs[0][...].astype(FLOAT)
    for ref in refs[1:]:
        total = total + ref[...].astype(FLOAT)
    return total


def core_sum(kept, got):
    return [
        (kept[at : at + 4].astype(FLOAT) + got[at : at + 4].astype(FLOAT)).astype(HALF)
        for at in range(0, 16, 4)
    ]


def square_sum_kernel(rows, *refs):
    outs = refs[4 * len(rows) :]
    start = 0
    for at, count in enumerate(rows):
        total = block_sum(refs[4 * at : 4 * at + 4]).astype(HALF)
        for to in range(4):
            each = 4 // len(outs)
            if each == 1:
                outs[to][start : start + count, :] = total[to]
            else:
                outs[to // each][to % each, start : start + count, :] = total[to]
        start += count


def square_sum_call(*pieces, halves=True):
    rows = tuple(stacks[0].shape[1] for stacks in pieces)
    shape = (sum(rows), pieces[0][0].shape[2])
    return pl.pallas_call(
        functools.partial(square_sum_kernel, rows),
        out_shape=[LIKE((2, *shape), HALF)] * 2 if halves else [LIKE(shape, HALF)] * 4,
        compiler_params=params(SMALL_LIMIT),
        cost_estimate=pl.CostEstimate(flops=0, bytes_accessed=1 << 21, transcendentals=0),
        name="square_sum",
    )(*[stack for stacks in pieces for stack in stacks])


def pair_sum(kept, got):
    return [(kept[at].astype(FLOAT) + got[at].astype(FLOAT)).astype(HALF) for at in range(2)]


def swap(block, offset):
    return lax.ppermute(block, AXES, [(one, one ^ offset) for one in range(OWNERS)])


def swaps(block, offsets):
    return [swap(block, offset) for offset in offsets]


def slot_places(slot_refs):
    for at, offset in enumerate(ORDER):
        yield slot_refs[at // 4], at % 4, offset


def small_rows(slot_refs, start):
    total = None
    for slots in slot_refs:
        for at in range(slots.shape[0]):
            block = slots[at, start : start + 16, :].astype(FLOAT)
            total = block if total is None else total + block
    return total


def attend_kernel(place_ref, x_ref, *refs):
    slot_refs = refs[:8]
    joint_ref, probs_ref, mixed_ref, weight_ref = refs[8:]
    head_size = mixed_ref.shape[1]
    place = place_ref[0]

    for slots, at, offset in slot_places(slot_refs):
        rows = owner_rows(offset, place, 16)
        for piece in range(3):
            weight_ref[0, rows, piece * head_size : (piece + 1) * head_size] = slots[
                at, piece * 16 : (piece + 1) * 16, :
            ]
    zeros = jnp.zeros((1, head_size), FLOAT)
    small = small_rows(slot_refs, 48)
    shift = jnp.concatenate([small[0:1, :], zeros, small[1:2, :]], axis=1)
    joint_ref[0] = (product(x_ref[...], weight_ref[0], 1, 0) + shift).astype(HALF)
    keys = joint_ref[0, :CTX, head_size : 2 * head_size]
    values = joint_ref[0, :CTX, 2 * head_size :]
    values_turned = jnp.transpose(values)
    factor = head_size ** (-0.5) * 1.4426950408889634
    for start in range(0, x_ref.shape[0], SCORE_BLOCK):
        span = slice(start, start + SCORE_BLOCK)
        queries = joint_ref[0, span, :head_size]
        scores = product(keys, queries, 1, 1)
        top = jnp.max(scores, axis=0, keepdims=True)
        grown = jnp.exp2((scores - top) * factor)
        total = jnp.sum(grown, axis=0, keepdims=True)
        probs = (grown * (1.0 / total)).astype(HALF)
        probs_ref[0, :, span] = probs
        mixed_ref[span, :] = jnp.transpose(product(values_turned, probs, 1, 0)).astype(HALF)


def attend_call(place, x, slots):
    rows, width = x.shape
    head_size = width // HEADS
    return pl.pallas_call(
        attend_kernel,
        grid_spec=pltpu.PrefetchScalarGridSpec(
            num_scalar_prefetch=1,
            grid=(HEADS,),
            in_specs=[pl.BlockSpec((rows, width), lambda h, p: (0, 0))]
            + [pl.BlockSpec((part.shape[0], FIRST_ROWS, head_size), lambda h, p: (0, 0, h))
               for part in slots],
            out_specs=[
                pl.BlockSpec((1, rows, 3 * head_size), lambda h, p: (h, 0, 0)),
                pl.BlockSpec((1, CTX, rows), lambda h, p: (h, 0, 0)),
                pl.BlockSpec((rows, head_size), lambda h, p: (0, h)),
                pl.BlockSpec((1, width, 3 * head_size), lambda h, p: (h, 0, 0)),
            ],
        ),
        out_shape=[
            LIKE((HEADS, rows, 3 * head_size), HALF),
            LIKE((HEADS, CTX, rows), HALF),
            LIKE((rows, HEADS * head_size), HALF),
            LIKE((HEADS, width, 3 * head_size), HALF),
        ],
        compiler_params=params(),
        cost_estimate=pl.CostEstimate(
            flops=HEADS * (2 * rows * width * 3 * head_size + 4 * rows * CTX * head_size),
            bytes_accessed=HEADS * 4 * 1024 * 1024,
            transcendentals=HEADS * rows * CTX,
        ),
        name="attend",
    )(place, x, *slots)


def unpack_second(place, slot_refs, output_w, expand_w, shrink_w, vec_ref):
    width = output_w.shape[1]
    for slots, at, offset in slot_places(slot_refs):
        rows = owner_rows(offset, place, 16)
        output_w[rows, :] = slots[at, 0:16, :]
        expand_w[rows, :width] = slots[at, 16:32, :]
        expand_w[rows, width:] = slots[at, 32:48, :]
        shrink_w[owner_rows(offset, place, 32), :] = slots[at, 48:80, :]
    vec_ref[...] = small_rows(slot_refs, 80)


def row_mean(rows):
    return jnp.mean(rows, axis=-1, keepdims=True)


def normalize(rows):
    centred = rows - row_mean(rows)
    inv_std = lax.rsqrt(row_mean(centred * centred) + EPS)
    return (centred * inv_std, inv_std)


def forward_rows(x_ref, mixed_ref, vec_ref, output_w, expand_w, shrink_w):
    attn_out = product(mixed_ref[...], output_w[...], 1, 0) + vec_ref[2:3, :]
    unit_one, inv_one = normalize(x_ref[...].astype(FLOAT) + attn_out)
    first_norm = unit_one * vec_ref[0:1, :] + vec_ref[4:5, :]
    first_low = first_norm.astype(HALF)
    shift = jnp.concatenate([vec_ref[6:7, :], vec_ref[7:8, :]], axis=1)
    hidden = product(first_low, expand_w[...], 1, 0) + shift
    normal_cdf = 0.5 * (1.0 + lax.erf(hidden * ROOT_HALF))
    act_low = (hidden * normal_cdf).astype(HALF)
    slope = normal_cdf + hidden * (jnp.exp(-0.5 * hidden * hidden) * PDF_PEAK)
    branch = product(act_low, shrink_w[...], 1, 0) + vec_ref[3:4, :]
    unit_two, inv_two = normalize(first_norm + branch)
    result = unit_two * vec_ref[1:2, :] + vec_ref[5:6, :]
    return (unit_one, inv_one, first_low, act_low, slope, unit_two, inv_two, result)


def column_sum(rows):
    return jnp.sum(rows, axis=0, keepdims=True)


def backward_rows(grad_rows, mixed_ref, vec_ref, kept, output_w, expand_w, shrink_w,
                  grad_mixed_ref, grad_one_ref, grad_output, grad_expand, grad_shrink, sums):
    unit_one, inv_one, first_low, act_low, slope, unit_two, inv_two = kept
    width = grad_rows.shape[1]

    def layer_norm_back(rows, unit_rows, inv_std, gain):
        scaled = rows * gain
        return inv_std * (scaled - row_mean(scaled) - unit_rows * row_mean(scaled * unit_rows))

    grad_two = layer_norm_back(grad_rows, unit_two, inv_two, vec_ref[1:2, :])
    branch_low = grad_two.astype(HALF)
    grad_shrink[...] += product(act_low, branch_low, 0, 0)
    grad_hidden = (product(branch_low, shrink_w[...], 1, 1) * slope).astype(HALF)
    grad_expand[...] += product(first_low, grad_hidden, 0, 0)
    grad_first = grad_two + product(grad_hidden, expand_w[...], 1, 1)
    grad_one = layer_norm_back(grad_first, unit_one, inv_one, vec_ref[0:1, :])
    attn_low = grad_one.astype(HALF)
    grad_output[...] += product(mixed_ref[...], attn_low, 0, 0)
    grad_mixed_ref[...] = product(attn_low, output_w[...], 1, 1).astype(HALF)
    grad_one_ref[...] = grad_one
    sums[0:1, :] += column_sum(grad_first * unit_one)
    sums[1:2, :] += column_sum(grad_rows * unit_two)
    sums[2:3, :] += column_sum(attn_low.astype(FLOAT))
    sums[3:4, :] += column_sum(branch_low.astype(FLOAT))
    sums[4:5, :] += column_sum(grad_first)
    sums[5:6, :] += column_sum(grad_rows)
    hidden_sum = column_sum(grad_hidden.astype(FLOAT))
    sums[6:7, :] += hidden_sum[:, :width]
    sums[7:8, :] += hidden_sum[:, width:]


def pack_second(place, kept_ref, sent_ref, grad_output, grad_expand, grad_shrink, sums):
    width = grad_output.shape[1]
    small = sums[...].astype(HALF)
    for at, offset in enumerate(ORDER):
        slots_ref = kept_ref if at < 16 else sent_ref
        at = at % 16
        rows = owner_rows(offset, place, 16)
        slots_ref[at, 0:16, :] = grad_output[rows, :].astype(HALF)
        slots_ref[at, 16:32, :] = grad_expand[rows, :width].astype(HALF)
        slots_ref[at, 32:48, :] = grad_expand[rows, width:].astype(HALF)
        slots_ref[at, 48:80, :] = grad_shrink[owner_rows(offset, place, 32), :].astype(HALF)
        slots_ref[at, 80:96, :] = small


def dense_kernel(place_ref, x_ref, mixed_ref, *refs):
    slot_refs = refs[:8]
    (result_ref, unit_one_ref, inv_one_ref, act_ref, slope_ref, unit_two_ref, inv_two_ref, output_w,
     expand_w, shrink_w, vec_ref) = refs[8:]

    @pl.when(pl.program_id(0) == 0)
    def _():
        unpack_second(place_ref[0], slot_refs, output_w, expand_w, shrink_w, vec_ref)

    unit_one, inv_one, _, act_low, slope, unit_two, inv_two, result = forward_rows(
        x_ref, mixed_ref, vec_ref, output_w, expand_w, shrink_w
    )
    result_ref[...] = result.astype(HALF)
    unit_one_ref[...] = unit_one
    inv_one_ref[...] = inv_one
    act_ref[...] = act_low
    slope_ref[...] = slope
    unit_two_ref[...] = unit_two
    inv_two_ref[...] = inv_two


def grad_x_rows(grad_one_ref, grad_joint_ref, weight_ref):
    total = grad_one_ref[...]
    for head in range(weight_ref.shape[0]):
        total = total + product(grad_joint_ref[head], weight_ref[head], 1, 1)
    return total


def clear(*items):
    for item in items:
        item[...] = jnp.zeros_like(item)


def dense_back_kernel(place_ref, grad_one_next, grad_joint_next, weight_next, mixed_ref, *refs):
    (unit_one_ref, inv_one_ref, act_ref, slope_ref, unit_two_ref, inv_two_ref, output_w, expand_w,
     shrink_w, vec_ref, grad_mixed_ref, grad_one_ref, kept_ref, sent_ref, sums, grad_output,
     grad_expand, grad_shrink) = refs

    @pl.when(pl.program_id(0) == 0)
    def _():
        clear(sums, grad_output, grad_expand, grad_shrink)

    unit_one = unit_one_ref[...]
    first_low = (unit_one * vec_ref[0:1, :] + vec_ref[4:5, :]).astype(HALF)
    kept = (unit_one, inv_one_ref[...], first_low, act_ref[...], slope_ref[...], unit_two_ref[...],
            inv_two_ref[...])
    grad_rows = grad_x_rows(grad_one_next, grad_joint_next, weight_next)
    backward_rows(grad_rows, mixed_ref, vec_ref, kept, output_w, expand_w, shrink_w,
                  grad_mixed_ref, grad_one_ref, grad_output, grad_expand, grad_shrink, sums)

    @pl.when(pl.program_id(0) == pl.num_programs(0) - 1)
    def _():
        pack_second(place_ref[0], kept_ref, sent_ref, grad_output, grad_expand, grad_shrink, sums)


def dense_turn_kernel(place_ref, live_ref, ids_ref, x_ref, mixed_ref, *refs):
    slot_refs = refs[:8]
    (cot_ref, result_ref, grad_mixed_ref, grad_one_ref, kept_ref, sent_ref, output_w, expand_w,
     shrink_w, vec_ref, grad_output, grad_expand, grad_shrink, sums) = refs[8:]
    step = pl.program_id(0)

    @pl.when(step == 0)
    def _():
        unpack_second(place_ref[0], slot_refs, output_w, expand_w, shrink_w, vec_ref)
        clear(sums, grad_output, grad_expand, grad_shrink)

    *kept, result = forward_rows(x_ref, mixed_ref, vec_ref, output_w, expand_w, shrink_w)
    result_ref[...] = result.astype(HALF)
    counts = vec_ref[8:9, :]
    lanes = lax.broadcasted_iota(jnp.int32, counts.shape, 1)
    own_count = jnp.sum(jnp.where(lanes == ids_ref[0], counts, 0.0), axis=1, keepdims=True)
    row_weight = jnp.sum(counts, axis=1, keepdims=True) / (NDS * own_count)
    rows = cot_ref.shape[0]
    slot = lax.broadcasted_iota(jnp.int32, (rows, 1), 0) + step * rows
    grad_rows = cot_ref[...].astype(FLOAT) * jnp.where(slot < live_ref[0], row_weight, 0.0)
    backward_rows(grad_rows, mixed_ref, vec_ref, kept, output_w, expand_w, shrink_w,
                  grad_mixed_ref, grad_one_ref, grad_output, grad_expand, grad_shrink, sums)

    @pl.when(step == pl.num_programs(0) - 1)
    def _():
        pack_second(place_ref[0], kept_ref, sent_ref, grad_output, grad_expand, grad_shrink, sums)


def by_rows(width):
    return pl.BlockSpec((ROW_BLOCK, width), lambda i, *p: (i, 0))


def fixed(*shape):
    return pl.BlockSpec(shape, lambda i, *p: (0,) * len(shape))


def joint_rows(grad_joint):
    heads, _, width = grad_joint.shape
    return pl.BlockSpec((heads, ROW_BLOCK, width), lambda i, *p: (0, i, 0))


def weight_shapes(width):
    return [(width, width), (width, 2 * width), (2 * width, width)]


def dense_call(place, x, mixed, slots):
    rows, width = x.shape
    weights = weight_shapes(width)
    return pl.pallas_call(
        dense_kernel,
        grid_spec=pltpu.PrefetchScalarGridSpec(
            num_scalar_prefetch=1,
            grid=(rows // ROW_BLOCK,),
            in_specs=[by_rows(width)] * 2
            + [fixed(*part.shape) for part in slots],
            out_specs=[by_rows(width), by_rows(width), by_rows(1), by_rows(2 * width),
                       by_rows(2 * width), by_rows(width), by_rows(1)]
            + [fixed(*shape) for shape in weights]
            + [fixed(16, width)],
        ),
        out_shape=[LIKE((rows, width), HALF), LIKE((rows, width), FLOAT), LIKE((rows, 1), FLOAT),
                   LIKE((rows, 2 * width), HALF), LIKE((rows, 2 * width), FLOAT),
                   LIKE((rows, width), FLOAT), LIKE((rows, 1), FLOAT)]
        + [LIKE(shape, HALF) for shape in weights]
        + [LIKE((16, width), FLOAT)],
        compiler_params=params(),
        cost_estimate=pl.CostEstimate(
            flops=10 * rows * width * width, bytes_accessed=16 * 1024 * 1024,
            transcendentals=4 * rows * width,
        ),
        name="dense",
    )(place, x, mixed, *slots)


def dense_back_call(place, grad_one, grad_joint, weight, mixed, kept):
    rows, width = grad_one.shape
    weights = weight_shapes(width)
    return pl.pallas_call(
        dense_back_kernel,
        grid_spec=pltpu.PrefetchScalarGridSpec(
            num_scalar_prefetch=1,
            grid=(rows // ROW_BLOCK,),
            in_specs=[by_rows(width), joint_rows(grad_joint), fixed(*weight.shape), by_rows(width)]
            + [by_rows(width), by_rows(1), by_rows(2 * width), by_rows(2 * width), by_rows(width),
               by_rows(1)]
            + [fixed(*shape) for shape in weights]
            + [fixed(16, width)],
            out_specs=[by_rows(width), by_rows(width)] + [fixed(16, SECOND_ROWS, width)] * 2,
            scratch_shapes=[pltpu.VMEM((16, width), FLOAT)]
            + [pltpu.VMEM(shape, FLOAT) for shape in weights],
        ),
        out_shape=[LIKE((rows, width), HALF), LIKE((rows, width), FLOAT)]
        + [LIKE((16, SECOND_ROWS, width), HALF)] * 2,
        compiler_params=params(),
        cost_estimate=pl.CostEstimate(
            flops=26 * rows * width * width, bytes_accessed=20 * 1024 * 1024, transcendentals=0
        ),
        name="dense_back",
    )(place, grad_one, grad_joint, weight, mixed, *kept)


def dense_turn_call(place, live, ids, x, mixed, slots, cotangent):
    rows, width = x.shape
    weights = weight_shapes(width)
    return pl.pallas_call(
        dense_turn_kernel,
        grid_spec=pltpu.PrefetchScalarGridSpec(
            num_scalar_prefetch=3,
            grid=(rows // ROW_BLOCK,),
            in_specs=[by_rows(width)] * 2
            + [fixed(*part.shape) for part in slots]
            + [by_rows(width)],
            out_specs=[by_rows(width)] * 3 + [fixed(16, SECOND_ROWS, width)] * 2,
            scratch_shapes=[pltpu.VMEM(shape, HALF) for shape in weights]
            + [pltpu.VMEM((16, width), FLOAT)]
            + [pltpu.VMEM(shape, FLOAT) for shape in weights]
            + [pltpu.VMEM((16, width), FLOAT)],
        ),
        out_shape=[LIKE((rows, width), HALF), LIKE((rows, width), HALF), LIKE((rows, width), FLOAT)]
        + [LIKE((16, SECOND_ROWS, width), HALF)] * 2,
        compiler_params=params(),
        cost_estimate=pl.CostEstimate(
            flops=30 * rows * width * width, bytes_accessed=16 * 1024 * 1024,
            transcendentals=4 * rows * width,
        ),
        name="dense_turn",
    )(place, live, ids, x, mixed, *slots, cotangent)


def attend_back_kernel(place_ref, x_ref, joint_ref, probs_ref, grad_mixed_ref, *refs):
    kept_ref, sent_ref, grad_joint_ref, x_turned, grad_scores, small = refs[-6:]
    grad_joint = grad_joint_ref.at[0]
    rows = x_ref.shape[0]
    head_size = grad_mixed_ref.shape[1]
    place = place_ref[0]

    @pl.when(pl.program_id(0) == 0)
    def _():
        x_turned[...] = jnp.transpose(x_ref[...])
        clear(small)

    grad_joint[CTX:, head_size:] = jnp.zeros((rows - CTX, 2 * head_size), HALF)
    keys = joint_ref[0, :CTX, head_size : 2 * head_size]
    values = joint_ref[0, :CTX, 2 * head_size :]
    keys_turned = jnp.transpose(keys)
    factor = head_size ** (-0.5)
    for start in range(0, rows, SCORE_BLOCK):
        span = slice(start, start + SCORE_BLOCK)
        grad_probs = product(values, grad_mixed_ref[span, :], 1, 1)
        probs = probs_ref[0, :, span].astype(FLOAT)
        weighted = probs * grad_probs
        grad_low = (factor * (weighted - probs * column_sum(weighted))).astype(HALF)
        grad_scores[:, span] = grad_low
        grad_joint[span, :head_size] = jnp.transpose(product(keys_turned, grad_low, 1, 0)).astype(
            HALF
        )
    grad_joint[:CTX, head_size : 2 * head_size] = product(
        grad_scores[...], joint_ref[0, :, :head_size], 1, 0
    ).astype(HALF)
    grad_joint[:CTX, 2 * head_size :] = product(probs_ref[0], grad_mixed_ref[...], 1, 0).astype(HALF)
    sums = column_sum(grad_joint[...].astype(FLOAT))
    small[0:1, :] = sums[:, :head_size]
    small[1:2, :] = sums[:, 2 * head_size :]
    small_low = small[...].astype(HALF)
    grad_low = product(x_turned[...], grad_joint[...], 1, 0).astype(HALF)
    holder = grad_scores
    holder[: grad_low.shape[0], : 3 * head_size] = grad_low
    for at, offset in enumerate(ORDER):
        slots_ref = kept_ref if at < 16 else sent_ref
        at = at % 16
        span = owner_rows(offset, place, 16)
        for piece in range(3):
            slots_ref[at, piece * 16 : (piece + 1) * 16, :] = holder[
                span, piece * head_size : (piece + 1) * head_size
            ]
        slots_ref[at, 48:64, :] = small_low


def attend_back_call(place, x, joint, probs, grad_mixed, base=0, heads=HEADS, before=()):
    rows, width = x.shape
    head_size = width // HEADS
    return pl.pallas_call(
        attend_back_kernel,
        grid_spec=pltpu.PrefetchScalarGridSpec(
            num_scalar_prefetch=1,
            grid=(heads,),
            in_specs=[
                pl.BlockSpec((rows, width), lambda h, p: (0, 0)),
                pl.BlockSpec((1, rows, 3 * head_size), lambda h, p: (h + base, 0, 0)),
                pl.BlockSpec((1, CTX, rows), lambda h, p: (h + base, 0, 0)),
                pl.BlockSpec((rows, head_size), lambda h, p: (0, h + base)),
            ]
            + [pl.BlockSpec(memory_space=pl.ANY)] * len(before),
            out_specs=[pl.BlockSpec((16, FIRST_ROWS, head_size), lambda h, p: (0, 0, h + base))] * 2
            + [pl.BlockSpec((1, rows, 3 * head_size), lambda h, p: (h + base, 0, 0))],
            scratch_shapes=[pltpu.VMEM((width, rows), HALF), pltpu.VMEM((CTX, rows), HALF),
                            pltpu.VMEM((16, head_size), FLOAT)],
        ),
        out_shape=[LIKE((16, FIRST_ROWS, width), HALF)] * 2
        + [LIKE((HEADS, rows, 3 * head_size), HALF)],
        input_output_aliases={5 + at: at for at in range(len(before))},
        compiler_params=params(),
        cost_estimate=pl.CostEstimate(
            flops=heads * (6 * rows * width * head_size + 8 * rows * CTX * head_size),
            bytes_accessed=heads * 4 * 1024 * 1024, transcendentals=0,
        ),
        name="attend_back",
    )(place, x, joint, probs, grad_mixed, *before)


def grad_x_kernel(grad_one_ref, grad_joint_ref, weight_ref, grad_x_ref):
    grad_x_ref[...] = grad_x_rows(grad_one_ref, grad_joint_ref, weight_ref)


def grad_x_call(grad_one, grad_joint, weight):
    rows, width = grad_one.shape
    return pl.pallas_call(
        grad_x_kernel,
        grid=(rows // ROW_BLOCK,),
        in_specs=[
            by_rows(width),
            joint_rows(grad_joint),
            fixed(*weight.shape),
        ],
        out_specs=by_rows(width),
        out_shape=LIKE((rows, width), FLOAT),
        compiler_params=params(),
        cost_estimate=pl.CostEstimate(
            flops=6 * rows * width * width, bytes_accessed=10 * 1024 * 1024, transcendentals=0
        ),
        name="grad_x",
    )(grad_one, grad_joint, weight)


def advance(master, moment, average, grad, momentum, step_rate, decay_now):
    new_moment = momentum * moment + grad
    new_master = master - step_rate * (grad + momentum * new_moment)
    new_average = decay_now * average + (1.0 - decay_now) * new_master
    return (new_moment, new_average, new_master, new_master.astype(HALF))


def stepper(rates_ref, state_refs, out_refs):
    rates = [rates_ref[at] for at in range(3)]

    def step(weight, where, grad):
        state = [ref[where] for ref in state_refs[3 * weight : 3 * weight + 3]]
        for ref, item in zip(out_refs[4 * weight : 4 * weight + 4], advance(*state, grad, *rates)):
            ref[where] = item

    return step


def second_step_kernel(rates_ref, *refs):
    middle, late = block_sum(refs[:2]), block_sum(refs[2:4])
    state_refs, out_refs, (first_ref, small_ref) = refs[4:13], refs[13:25], refs[25:]
    width = small_ref.shape[2]
    step = stepper(rates_ref, state_refs, out_refs)
    for layer, piece in enumerate((middle[FIRST_ROWS:], late)):
        step(0, (layer,), piece[0:16])
        step(1, (layer, slice(None), slice(0, width)), piece[16:32])
        step(1, (layer, slice(None), slice(width, 2 * width)), piece[32:48])
        step(2, (layer,), piece[48:80])
        small_ref[layer] = piece[80:96]
    first_ref[...] = middle[:FIRST_ROWS]


def step_shapes(masters):
    return [
        LIKE(master.shape, kind) for master in masters for kind in (FLOAT, FLOAT, FLOAT, HALF)
    ]


def step_call(kernel, rates, inputs, out_shape, name):
    return pl.pallas_call(
        kernel,
        in_specs=[pl.BlockSpec(memory_space=pltpu.SMEM)] * len(rates)
        + [pl.BlockSpec(memory_space=pltpu.VMEM)] * len(inputs),
        out_specs=[pl.BlockSpec(memory_space=pltpu.VMEM)] * len(out_shape),
        out_shape=out_shape,
        compiler_params=params(SMALL_LIMIT),
        cost_estimate=pl.CostEstimate(flops=0, bytes_accessed=1 << 22, transcendentals=0),
        name=name,
    )(*rates, *inputs)


def first_step_kernel(place_ref, rates_ref, small_ref, late_ref, *refs):
    blocks, state_refs, out_refs = refs[:4], refs[4:13], refs[13:]
    width = small_ref.shape[2]
    each = out_refs[4].shape[2]
    step = stepper(rates_ref, state_refs, out_refs)
    turn = width - place_ref[0] * each
    for layer, total in enumerate((block_sum(blocks), late_ref[...])):
        for piece in range(3):
            columns = slice(piece * width, (piece + 1) * width)
            step(0, (layer, slice(None), columns), total[piece * 16 : (piece + 1) * 16])
        own_first = pltpu.roll(total[48:64], turn, 1)[:, :each]
        own_second = pltpu.roll(small_ref[layer], turn, 1)[:, :each]
        step(1, (layer,), own_second[0:2])
        step(2, (layer, slice(0, 2)), own_first[0:2])
        step(2, (layer, slice(2, 8)), own_second[2:8])


def wide_to_rows(shard, width):
    return jnp.concatenate(
        [shard[:, at * width : (at + 1) * width] for at in range(shard.shape[1] // width)]
    )


def rows_to_wide(rows, pieces):
    each = rows.shape[0] // pieces
    return jnp.concatenate([rows[at * each : (at + 1) * each] for at in range(pieces)], axis=1)


def gather_rows(shards_by_part, small):
    width = small.shape[1]
    parts = []
    for shard in shards_by_part:
        whole = lax.all_gather(shard, AXES, axis=0, tiled=False)
        parts.append(whole.reshape(OWNERS, -1, width))
    smalls = jnp.broadcast_to(small[None] * (jnp.arange(OWNERS) == 0)[:, None, None].astype(HALF),
                              (OWNERS, *small.shape))
    slots = jnp.concatenate([*parts, smalls], axis=1)[np.array(ORDER)]
    return [slots[4 * at : 4 * at + 4] for at in range(8)]


def scatter_rows(kept, sent, parts):
    slots = jnp.concatenate([kept, sent])[np.argsort(np.array(ORDER))]
    everyone = lax.axis_size(AXES)
    own, start = [], 0
    for rows in parts:
        piece = slots[:, start : start + rows].reshape(everyone, -1, slots.shape[2])
        own.append(lax.psum_scatter(piece, AXES, scatter_dimension=0, tiled=False).astype(FLOAT))
        start += rows
    return own, lax.psum(slots[0, start:].astype(FLOAT), AXES)


def sync(*items):
    return lax.optimization_barrier(items)


def any_size(place, x, cotangent, dataset_ids, live, masters, moments, averages, rates):
    layers = masters[0].shape[0]
    width = x.shape[1]
    position = lax.axis_index(AXES)
    low = lambda item: item.astype(HALF)
    own = low(jnp.concatenate([masters[4], masters[5]], axis=1))
    wide = lax.all_gather(own, AXES, axis=2, tiled=True)
    onehot = (dataset_ids[0] == jnp.arange(width, dtype=jnp.int32)).astype(FLOAT)
    counts = low(lax.psum(onehot, AXES))[None]
    first, second = [], []
    for at in range(layers):
        pad = lambda rows: jnp.pad(rows, ((0, 16 - rows.shape[0]), (0, 0)))
        attend_w = masters[0][at]
        first.append(gather_rows(
            [low(attend_w[:, piece * width : (piece + 1) * width]) for piece in range(3)],
            pad(wide[at, 2:4]),
        ))
        expand_w = masters[2][at]
        second.append(gather_rows(
            [low(masters[1][at]), low(expand_w[:, :width]), low(expand_w[:, width:]),
             low(masters[3][at])],
            pad(jnp.concatenate([wide[at, 0:2], wide[at, 4:10], counts])),
        ))
    current = x
    saved = []
    for at in range(layers):
        joint, probs, mixed, weight = attend_call(place, current, first[at])
        keep = (current, joint, probs, mixed, weight)
        if at + 1 < layers:
            current, *rest = dense_call(place, current, mixed, second[at])
            keep = (*keep, rest)
        saved.append(keep)
    first_grads, second_grads = [None] * layers, [None] * layers
    for at in reversed(range(layers)):
        start, joint, probs, mixed, weight = saved[at][:5]
        if at + 1 == layers:
            result, grad_mixed, grad_one, *slots = dense_turn_call(
                place, live, dataset_ids, start, mixed, second[at], cotangent
            )
        else:
            grad_mixed, grad_one, *slots = dense_back_call(
                place, grad_one, grad_joint, saved[at + 1][4], mixed, saved[at][5]
            )
        second_grads[at] = slots
        *slots, grad_joint = attend_back_call(place, start, joint, probs, grad_mixed)
        first_grads[at] = slots
    grad_rows = grad_x_call(grad_one, grad_joint, weight)
    grads = [[] for _ in range(6)]
    for at in range(layers):
        kept, sent = first_grads[at]
        own, first_small = scatter_rows(kept, sent, (16, 16, 16))
        grads[0].append(jnp.concatenate(own, axis=1))
        own, small = scatter_rows(*second_grads[at], (16, 16, 16, 32))
        grads[1].append(own[0])
        grads[2].append(jnp.concatenate(own[1:3], axis=1))
        grads[3].append(own[3])
        rows = jnp.concatenate([small[0:2], first_small[0:2], small[2:8]])
        lanes = masters[4].shape[2]
        own_rows = lax.dynamic_slice(rows, (0, position * lanes), (10, lanes))
        grads[4].append(own_rows[:2])
        grads[5].append(own_rows[2:])
    outputs = []
    for master, moment, average, grad in zip(masters, moments, averages, grads):
        outputs.extend(
            advance(master, moment, average, jnp.stack(grad), rates[0], rates[1], rates[2])
        )
    return (result, grad_rows, *outputs)


def one_per_owner(place, x, cotangent, dataset_ids, live, masters, moments, averages, rates):
    width = x.shape[1]
    pair = HEADS // 2

    def to_core(stacks):
        return [swap(one, CORE) for one in stacks]

    def square(block):
        return swaps(block, SQUARE[1:])

    def square_back(stacks):
        return [swap(one, offset) for one, offset in zip(stacks[1:], SQUARE[1:])]

    def chain_back(blocks):
        return [swap(one, offset) for one, offset in zip(blocks[1:], CHAIN[1:])]

    near, following, late = pack_call(place, dataset_ids, masters)
    (first_own,) = join_call([near, *swaps(near, CHAIN[1:])])

    first_own, following, late = sync(first_own, following, late)
    first_near = [first_own, *square(first_own)]
    (following_two,) = join_call([following, swap(following, CHAIN[1])])
    (late_two,) = join_call([late, swap(late, CHAIN[1])])
    (second_own,) = join_call([following_two, swap(following_two, CHAIN[2])])
    first_far = to_core(first_near)

    first_far, second_own, x, late_two = sync(first_far, second_own, x, late_two)
    second_near = [second_own, *square(second_own)]
    late_got = swap(late_two, CHAIN[2])
    joint, probs, mixed, weight = attend_call(place, x, [*first_near, *first_far])

    mixed, second_near, late_two, late_got = sync(mixed, second_near, late_two, late_got)
    third_own, late_own = join_call(
        [late_two, late_got], (0, FIRST_ROWS), (FIRST_ROWS, SECOND_ROWS)
    )
    second_far = to_core(second_near)
    second_far, third_own, mixed = sync(second_far, third_own, mixed)
    third_near = [third_own, *square(third_own)]
    third_far = [swap(third_own, CORE)]
    middle, *dense_kept = dense_call(place, x, mixed, [*second_near, *second_far])

    middle, third_near, third_far, late_own = sync(middle, third_near, third_far, late_own)
    third_far += to_core(third_near[1:])
    third_far, late_own, middle = sync(third_far, late_own, middle)
    late_near = [late_own, *square(late_own)]
    late_far = [swap(late_own, CORE)]
    late_joint, late_probs, late_mixed, late_weight = attend_call(
        place, middle, [*third_near, *third_far]
    )

    late_mixed, late_near, late_far = sync(late_mixed, late_near, late_far)
    late_far += to_core(late_near[1:])
    result, grad_mixed, grad_one, kept, sent = dense_turn_call(
        place, live, dataset_ids, middle, late_mixed, [*late_near, *late_far], cotangent
    )

    sent, grad_mixed = sync(sent, grad_mixed)
    got = swap(sent, CORE)
    next_kept, next_sent, grad_joint = attend_back_call(
        place, middle, late_joint, late_probs, grad_mixed
    )

    got, next_sent, grad_joint = sync(got, next_sent, grad_joint)
    late_stacks = core_sum(kept, got)
    late_stacks, next_sent, grad_joint = sync(late_stacks, next_sent, grad_joint)
    late_got = square_back(late_stacks)
    got = swap(next_sent, CORE)
    grad_mixed, grad_one, kept, sent = dense_back_call(
        place, grad_one, grad_joint, late_weight, mixed, dense_kept
    )

    got, late_got, sent, grad_mixed = sync(got, late_got, sent, grad_mixed)
    first_stacks = core_sum(next_kept, got)
    late_kept, late_sent = square_sum_call([late_stacks[0], *late_got])
    first_stacks, late_kept, late_sent, sent, grad_mixed = sync(
        first_stacks, late_kept, late_sent, sent, grad_mixed
    )
    first_got = square_back(first_stacks)
    got = swap(sent, CORE)
    late_got = swap(late_sent, CHAIN[2])
    before = attend_back_call(place, x, joint, probs, grad_mixed, 0, pair)

    got, first_got, late_got, before = sync(got, first_got, late_got, before)
    second_stacks = core_sum(kept, got)
    late_own, late_sent = pair_sum(late_kept, late_got)
    second_stacks, before, late_sent = sync(second_stacks, before, late_sent)
    second_got = square_back(second_stacks)
    late_got = swap(late_sent, CHAIN[1])
    kept, sent, grad_joint = attend_back_call(
        place, x, joint, probs, grad_mixed, pair, HEADS - pair, before
    )

    second_got, sent, grad_joint, late_got = sync(second_got, sent, grad_joint, late_got)
    got = swap(sent, CORE)
    middle_kept, middle_sent = square_sum_call(
        [first_stacks[0], *first_got], [second_stacks[0], *second_got]
    )
    got, middle_sent = sync(got, middle_sent)
    stacks = core_sum(kept, got)
    stacks, middle_sent, grad_joint = sync(stacks, middle_sent, grad_joint)
    got = square_back(stacks)
    middle_got = swap(middle_sent, CHAIN[2])
    grad_rows = grad_x_call(grad_one, grad_joint, weight)

    middle_got, grad_rows = sync(middle_got, grad_rows)
    middle_own, middle_sent = pair_sum(middle_kept, middle_got)
    middle_got = swap(middle_sent, CHAIN[1])

    def state_of(*which):
        return [item for at in which for item in (masters[at], moments[at], averages[at])]

    last_blocks = square_sum_call([stacks[0], *got], halves=False)
    last_got = chain_back(last_blocks)
    *stepped, late_first, small = step_call(
        second_step_kernel,
        [rates],
        [middle_own, middle_got, late_own, late_got, *state_of(1, 2, 3)],
        [*step_shapes(masters[1:4]), LIKE((FIRST_ROWS, width), FLOAT),
         LIKE((2, 16, width), FLOAT)],
        "second_step",
    )
    rest = step_call(
        first_step_kernel,
        [place, rates],
        [small, late_first, last_blocks[0], *last_got, *state_of(0, 4, 5)],
        step_shapes((masters[0], masters[4], masters[5])),
        "first_step",
    )
    return (result, grad_rows, *rest[:4], *stepped, *rest[4:])


def shards(
    tokens,
    cotangent,
    dataset_ids,
    query_counts,
    learn_rate,
    momentum_coef,
    average_decay,
    step_count,
    *state,
):
    masters, moments, averages = state[0::3], state[1::3], state[2::3]
    position = lax.axis_index(AXES)
    direct = lax.axis_size(AXES) == OWNERS
    place = (position if direct else jnp.zeros_like(position)).astype(jnp.int32).reshape(1)
    step_value = step_count[0].astype(FLOAT)
    decay_now = average_decay[0] * (1.0 + step_value) / (4.0 + step_value)
    rates = jnp.stack([momentum_coef[0], learn_rate[0], decay_now])
    run = one_per_owner if direct else any_size
    result, grad_rows, *outputs = run(
        place, tokens[0], cotangent[0], dataset_ids, query_counts + CTX, masters, moments, averages,
        rates,
    )
    return (result[None], grad_rows[None], *outputs)


def solution(mesh):
    rows = P(AXES, None, None)
    weight = P(None, AXES, None)
    vector = P(None, None, AXES)
    scalar = P()
    return jax.shard_map(
        shards,
        mesh=mesh,
        in_specs=(rows, rows, P(AXES), P(AXES), *[scalar] * 4, *[weight] * 12, *[vector] * 6),
        out_specs=(rows, rows, *[weight] * 16, *[vector] * 8),
        check_vma=False,
    )
```

profile of v0, /device:TPU:0, one launch (start us, length us, event | category | flops | bytes accessed | tf_op | source)
XLA Modules:
  0.0 248.8 jit_solution(9741132542958321574)
XLA Ops:
  1.3 2.0 pack.1
  3.3 4.1 %collective-permute-start = (bf16[64,512]{1,0:T(8,128)(2,1)}, bf16[64,512]{1,0:T(8,128)(2,1)S(1)}, u32[]{:S(2)}, u32[]{:S(2)}) collective-permute-start(bf16[64,512]{1,0:T(8,128)(2,1)} %get-tuple-element.201.refs_0_), channel_id=1, source_target_pairs={{0,4},{1,5},{2,6},{3,7},{4,0},{5,1},{6,2},{7,3},{8,12},{9,13},{10,... | collective-permute-start | bytes 196616 | tf_op jit(solution)/shard_map/ppermute | solution.py:170
  8.9 1.7 collective-permute-done.refs_1_
  11.8 3.4 %collective-permute-done.2.refs_3_ = bf16[64,512]{1,0:T(8,128)(2,1)S(1)} collective-permute-done((bf16[64,512]{1,0:T(8,128)(2,1)}, bf16[64,512]{1,0:T(8,128)(2,1)S(1)}, u32[]{:S(2)}, u32[]{:S(2)}) %collective-permute-start.2) | collective-permute-done | bytes 65568 | tf_op jit(solution)/shard_map/ppermute | solution.py:170
  22.6 6.5 %collective-permute-done.10.refs_1_ = bf16[96,512]{1,0:T(8,128)(2,1)S(1)} collective-permute-done((bf16[96,512]{1,0:T(8,128)(2,1)}, bf16[96,512]{1,0:T(8,128)(2,1)S(1)}, u32[]{:S(2)}, u32[]{:S(2)}) %collective-permute-start.10) | collective-permute-done | bytes 98336 | tf_op jit(solution)/shard_map/ppermute | solution.py:170
  33.0 5.5 %collective-permute-done.11.refs_1_ = bf16[2,96,512]{2,1,0:T(8,128)(2,1)S(1)} collective-permute-done((bf16[2,96,512]{2,1,0:T(8,128)(2,1)S(1)}, bf16[2,96,512]{2,1,0:T(8,128)(2,1)S(1)}, u32[]{:S(2)}, u32[]{:S(2)}) %collective-permute-start.11) | collective-permute-done | bytes 196640 | tf_op jit(solution)/shard_map/ppermute | solution.py:170
  43.3 19.0 %attend.2 = (bf16[4,1024,384]{2,1,0:T(8,128)(2,1)}, bf16[4,896,1024]{2,1,0:T(8,128)(2,1)}, bf16[1024,512]{1,0:T(8,128)(2,1)}, bf16[4,512,384]{2,1,0:T(8,128)(2,1)}) custom-call(s32[1]{0:T(128)} %bitcast.place_ref, bf16[1024,512]{1,0:T(8,128)(2,1)} %bitcast.13, bf16[4,64,512]{2,1,0:T(8,128)(2,1)} %copy-done.4, bf16[4,64,512]{2,1,0:T(8,128)(2,1)} %copy-done.45, ...), custom_call_target="tpu_custom_call" | custom-call | flops 3489660928 | bytes 16777216 | tf_op jit(solution)/shard_map/attend/pallas_call | solution.py:226
  69.4 10.4 %dense.1 = (bf16[1024,512]{1,0:T(8,128)(2,1)}, f32[1024,512]{1,0:T(8,128)}, f32[1024,1]{1,0:T(8,128)}, bf16[1024,1024]{1,0:T(8,128)(2,1)}, f32[1024,1024]{1,0:T(...) custom-call(s32[1]{0:T(128)} %bitcast.place_ref, ...), custom_call_target="tpu_custom_call" | custom-call | flops 2684354560 | bytes 16777216 | tf_op jit(solution)/shard_map/dense/pallas_call | solution.py:446
  86.9 19.0 %attend.3 = (bf16[4,1024,384]{2,1,0:T(8,128)(2,1)}, bf16[4,896,1024]{2,1,0:T(8,128)(2,1)}, bf16[1024,512]{1,0:T(8,128)(2,1)}, bf16[4,512,384]{2,1,0:T(8,128)(2,1)}) custom-call(s32[1]{0:T(128)} %bitcast.place_ref, bf16[1024,512]{1,0:T(8,128)(2,1)} %get-tuple-element.237.x_ref, bf16[4,64,512]{2,1,0:T(8,128)(2,1)} %copy-done.24, ...), custom_call_target="tpu_custom_call" | custom-call | flops 3489660928 | bytes 16777216 | tf_op jit(solution)/shard_map/attend/pallas_call | solution.py:226
  109.8 19.5 %dense_turn.1 = (bf16[1024,512]{1,0:T(8,128)(2,1)}, bf16[1024,512]{1,0:T(8,128)(2,1)}, f32[1024,512]{1,0:T(8,128)}, bf16[16,96,512]{2,1,0:T(8,128)(2,1)}, bf16[16,96,512]{2,1,0:T(8,128)(2,1)}) custom-call(s32[1]{0:T(128)} %bitcast.place_ref, s32[1]{0:T(128)S(6)} %add.71.live_ref, s32[1]{0:T(128)S(6)} %copy.58.ids_ref, ...), custom_call_target="tpu_custom_call" | custom-call | flops 8053063680 | bytes 16777216 | tf_op jit(solution)/shard_map/dense_turn/pallas_call | solution.py:502
  129.6 21.8 %attend_back.3 = (bf16[16,64,512]{2,1,0:T(8,128)(2,1)}, bf16[16,64,512]{2,1,0:T(8,128)(2,1)}, bf16[4,1024,384]{2,1,0:T(8,128)(2,1)}) custom-call(s32[1]{0:T(128)} %bitcast.place_ref, bf16[1024,512]{1,0:T(8,128)(2,1)} %get-tuple-element.237.x_ref, bf16[4,1024,384]{2,1,0:T(8,128)(2,1)} %get-tuple-element.254.joint_ref, ...), custom_call_target="tpu_custom_call" | custom-call | flops 5368709120 | bytes 16777216 | tf_op jit(solution)/shard_map/attend_back/pallas_call | solution.py:579
  156.6 17.5 %dense_back.1 = (bf16[1024,512]{1,0:T(8,128)(2,1)}, f32[1024,512]{1,0:T(8,128)}, bf16[16,96,512]{2,1,0:T(8,128)(2,1)}, bf16[16,96,512]{2,1,0:T(8,128)(2,1)}) custom-call(s32[1]{0:T(128)} %bitcast.place_ref, f32[1024,512]{1,0:T(8,128)} %get-tuple-element.271.grad_one_next, bf16[4,1024,384]{2,1,0:T(8,128)(2,1)} %get-tuple-element.272.grad_joint_next, ...), custom_call_target="tpu_custom_call" | custom-call | flops 6979321856 | bytes 20971520 | tf_op jit(solution)/shard_map/dense_back/pallas_call | solution.py:475
  174.2 2.2 add_convert_fusion.12
  180.2 1.7 collective-permute-start.44
  182.0 12.9 %attend_back.4 = (bf16[16,64,512]{2,1,0:T(8,128)(2,1)}, bf16[16,64,512]{2,1,0:T(8,128)(2,1)}, bf16[4,1024,384]{2,1,0:T(8,128)(2,1)}) custom-call(s32[1]{0:T(128)} %bitcast.place_ref, bf16[1024,512]{1,0:T(8,128)(2,1)} %bitcast.15, bf16[4,1024,384]{2,1,0:T(8,128)(2,1)} %get-tuple-element.252.joint_ref, bf16[4,896,1024]{2,1,0:T(8,128)(2,1)} %get-tuple-element.253.probs_ref, ...), custom_call_target="tpu_custom_call" | custom-call | flops 2684354560 | bytes 8388608 | tf_op jit(solution)/shard_map/attend_back/pallas_call | solution.py:579
  195.6 2.8 %add_convert_fusion = (bf16[4,96,512]{2,1,0:T(8,128)(2,1)S(1)}, bf16[4,96,512]{2,1,0:T(8,128)(2,1)}, bf16[4,96,512]{2,1,0:T(8,128)(2,1)}, bf16[4,96,512]{2,1,0:T(8,128)(2,1)S(1)}) fusion(bf16[16,96,512]{2,1,0:T(8,128)(2,1)} %collective-permute-done.40, bf16[16,96,512]{2,1,0:T(8,128)(2,1)S(1)} %copy-done.26), kind=kLoop, calls=%fused_computation | loop fusion | flops 3145728 | bytes 4718592 | tf_op jit(solution)/shard_map/convert_element_type | solution.py:134
  202.0 1.7 collective-permute-start.48
  203.7 12.8 %attend_back.5 = (bf16[16,64,512]{2,1,0:T(8,128)(2,1)}, bf16[16,64,512]{2,1,0:T(8,128)(2,1)}, bf16[4,1024,384]{2,1,0:T(8,128)(2,1)}) custom-call(s32[1]{0:T(128)} %bitcast.place_ref, bf16[1024,512]{1,0:T(8,128)(2,1)} %bitcast.16, bf16[4,1024,384]{2,1,0:T(8,128)(2,1)} %get-tuple-element.252.joint_ref, ...), custom_call_target="tpu_custom_call", output_to_operand_aliasing={{0}: (5, {}), {1}: (6, {}), {2}: (7, {})} | custom-call | flops 2684354560 | bytes 8388608 | tf_op jit(solution)/shard_map/attend_back/pallas_call | solution.py:579
  218.7 2.5 %collective-permute-done.49 = bf16[16,64,512]{2,1,0:T(8,128)(2,1)S(1)} collective-permute-done((bf16[16,64,512]{2,1,0:T(8,128)(2,1)}, bf16[16,64,512]{2,1,0:T(8,128)(2,1)S(1)}, u32[]{:S(2)}, u32[]{:S(2)}) %collective-permute-start.49) | collective-permute-done | bytes 1048608 | tf_op jit(solution)/shard_map/ppermute | solution.py:170
  225.5 6.4 %grad_x.1 = f32[1024,512]{1,0:T(8,128)} custom-call(f32[1024,512]{1,0:T(8,128)} %get-tuple-element.335.grad_one_ref, bf16[4,1024,384]{2,1,0:T(8,128)(2,1)} %get-tuple-element.336.grad_joint_ref, bf16[4,512,384]{2,1,0:T(8,128)(2,1)} %get-tuple-element.337.weight_ref), custom_call_target="tpu_custom_call" | custom-call | flops 1610612736 | bytes 10485760 | tf_op jit(solution)/shard_map/grad_x/pallas_call | solution.py:614
  232.2 2.9 %collective-permute-start.51 = (bf16[160,512]{1,0:T(8,128)(2,1)S(1)}, bf16[160,512]{1,0:T(8,128)(2,1)S(1)}, u32[]{:S(2)}, u32[]{:S(2)}) collective-permute-start(bf16[160,512]{1,0:T(8,128)(2,1)S(1)} %get-tuple-element.392), channel_id=1, source_target_pairs={{0,4},{1,5},{2,6},{3,7},{4,0},{5,1},{6,2},{7,3},{8,12},{9,13},{10,... | collective-permute-start | bytes 491528 | tf_op jit(solution)/shard_map/ppermute | solution.py:170
  240.0 2.4 collective-permute-start.57
  242.5 2.8 %collective-permute-done.51.refs_1_ = bf16[160,512]{1,0:T(8,128)(2,1)S(1)} collective-permute-done((bf16[160,512]{1,0:T(8,128)(2,1)S(1)}, bf16[160,512]{1,0:T(8,128)(2,1)S(1)}, u32[]{:S(2)}, u32[]{:S(2)}) %collective-permute-start.51) | collective-permute-done | bytes 163872 | tf_op jit(solution)/shard_map/ppermute | solution.py:170
  245.4 1.6 second_step.1
  (235 shorter events, 59.8 us)
Async XLA Ops:
  39.5 22.9 %collective-permute-start.13 = (bf16[4,96,512]{2,1,0:T(8,128)(2,1)S(1)}, bf16[4,96,512]{2,1,0:T(8,128)(2,1)S(1)}, u32[]{:S(2)}, u32[]{:S(2)}) collective-permute-start(bf16[4,96,512]{2,1,0:T(8,128)(2,1)S(1)} %join.7.refs_0_), channel_id=1, source_target_pairs={{0,1},{1,0},{2,3},{3,2},{4,5},{5,4},{6,7},{7,6},{8,9},{9,8},{10,11... | collective-permute-start | bytes 1179656 | tf_op jit(solution)/shard_map/ppermute | solution.py:170
  40.9 21.4 %collective-permute-start.14 = (bf16[4,96,512]{2,1,0:T(8,128)(2,1)S(1)}, bf16[4,96,512]{2,1,0:T(8,128)(2,1)S(1)}, u32[]{:S(2)}, u32[]{:S(2)}) collective-permute-start(bf16[4,96,512]{2,1,0:T(8,128)(2,1)S(1)} %join.7.refs_0_), channel_id=1, source_target_pairs={{0,16},{1,17},{2,18},{3,19},{4,20},{5,21},{6,22},{7,23},{8,24},{9,... | collective-permute-start | bytes 1179656 | tf_op jit(solution)/shard_map/ppermute | solution.py:170
  42.5 19.9 %collective-permute-start.15 = (bf16[4,96,512]{2,1,0:T(8,128)(2,1)S(1)}, bf16[4,96,512]{2,1,0:T(8,128)(2,1)S(1)}, u32[]{:S(2)}, u32[]{:S(2)}) collective-permute-start(bf16[4,96,512]{2,1,0:T(8,128)(2,1)S(1)} %join.7.refs_0_), channel_id=1, source_target_pairs={{0,17},{1,16},{2,19},{3,18},{4,21},{5,20},{6,23},{7,22},{8,25},{9,... | collective-permute-start | bytes 1179656 | tf_op jit(solution)/shard_map/ppermute | solution.py:170
  42.9 19.4 %collective-permute-start.16 = (bf16[2,160,512]{2,1,0:T(8,128)(2,1)S(1)}, bf16[2,160,512]{2,1,0:T(8,128)(2,1)S(1)}, u32[]{:S(2)}, u32[]{:S(2)}) collective-permute-start(bf16[2,160,512]{2,1,0:T(8,128)(2,1)S(1)} %join.8.refs_0_), channel_id=1, source_target_pairs={{0,2},{1,3},{2,0},{3,1},{4,6},{5,7},{6,4},{7,5},{8,10},{9,11},{10,... | collective-permute-start | bytes 983048 | tf_op jit(solution)/shard_map/ppermute | solution.py:170
  83.4 22.5 %collective-permute-start.28 = (bf16[4,96,512]{2,1,0:T(8,128)(2,1)S(1)}, bf16[4,96,512]{2,1,0:T(8,128)(2,1)S(1)}, u32[]{:S(2)}, u32[]{:S(2)}) collective-permute-start(bf16[4,96,512]{2,1,0:T(8,128)(2,1)S(1)} %get-tuple-element.246.refs_0_), channel_id=1, source_target_pairs={{0,1},{1,0},{2,3},{3,2},{4,5},{5,4},{6,7},{7,6},{8,9},{9,8},{10,11... | collective-permute-start | bytes 1179656 | tf_op jit(solution)/shard_map/ppermute | solution.py:170
  84.6 21.4 %collective-permute-start.29 = (bf16[4,96,512]{2,1,0:T(8,128)(2,1)S(1)}, bf16[4,96,512]{2,1,0:T(8,128)(2,1)S(1)}, u32[]{:S(2)}, u32[]{:S(2)}) collective-permute-start(bf16[4,96,512]{2,1,0:T(8,128)(2,1)S(1)} %get-tuple-element.246.refs_0_), channel_id=1, source_target_pairs={{0,16},{1,17},{2,18},{3,19},{4,20},{5,21},{6,22},{7,23},{8,24},{9,... | collective-permute-start | bytes 1179656 | tf_op jit(solution)/shard_map/ppermute | solution.py:170
  85.5 20.5 %collective-permute-start.30 = (bf16[4,96,512]{2,1,0:T(8,128)(2,1)S(1)}, bf16[4,96,512]{2,1,0:T(8,128)(2,1)S(1)}, u32[]{:S(2)}, u32[]{:S(2)}) collective-permute-start(bf16[4,96,512]{2,1,0:T(8,128)(2,1)S(1)} %get-tuple-element.246.refs_0_), channel_id=1, source_target_pairs={{0,17},{1,16},{2,19},{3,18},{4,21},{5,20},{6,23},{7,22},{8,25},{9,... | collective-permute-start | bytes 1179656 | tf_op jit(solution)/shard_map/ppermute | solution.py:170
  86.9 19.1 %collective-permute-start.31 = (bf16[4,96,512]{2,1,0:T(8,128)(2,1)S(1)}, bf16[4,96,512]{2,1,0:T(8,128)(2,1)S(1)}, u32[]{:S(2)}, u32[]{:S(2)}) collective-permute-start(bf16[4,96,512]{2,1,0:T(8,128)(2,1)S(1)} %get-tuple-element.246.refs_0_), channel_id=1, source_target_pairs={{0,8},{1,9},{2,10},{3,11},{4,12},{5,13},{6,14},{7,15},{8,0},{9,1},... | collective-permute-start | bytes 1179656 | tf_op jit(solution)/shard_map/ppermute | solution.py:170
  129.3 22.2 %collective-permute-start.35 = (bf16[16,96,512]{2,1,0:T(8,128)(2,1)}, bf16[16,96,512]{2,1,0:T(8,128)(2,1)S(1)}, u32[]{:S(2)}, u32[]{:S(2)}) collective-permute-start(bf16[16,96,512]{2,1,0:T(8,128)(2,1)} %get-tuple-element.261), channel_id=1, source_target_pairs={{0,8},{1,9},{2,10},{3,11},{4,12},{5,13},{6,14},{7,15},{8,0},{9,1},... | collective-permute-start | bytes 4718600 | tf_op jit(solution)/shard_map/ppermute | solution.py:170
  152.9 21.3 %collective-permute-start.36 = (bf16[16,64,512]{2,1,0:T(8,128)(2,1)}, bf16[16,64,512]{2,1,0:T(8,128)(2,1)}, u32[]{:S(2)}, u32[]{:S(2)}) collective-permute-start(bf16[16,64,512]{2,1,0:T(8,128)(2,1)} %get-tuple-element.267), channel_id=1, source_target_pairs={{0,8},{1,9},{2,10},{3,11},{4,12},{5,13},{6,14},{7,15},{8,0},{9,1},... | collective-permute-start | bytes 3145736 | tf_op jit(solution)/shard_map/ppermute | solution.py:170
  153.1 21.0 %collective-permute-start.37 = (bf16[4,96,512]{2,1,0:T(8,128)(2,1)}, bf16[4,96,512]{2,1,0:T(8,128)(2,1)S(1)}, u32[]{:S(2)}, u32[]{:S(2)}) collective-permute-start(bf16[4,96,512]{2,1,0:T(8,128)(2,1)} %get-tuple-element.268), channel_id=1, source_target_pairs={{0,1},{1,0},{2,3},{3,2},{4,5},{5,4},{6,7},{7,6},{8,9},{9,8},{10,11... | collective-permute-start | bytes 1179656 | tf_op jit(solution)/shard_map/ppermute | solution.py:170
  154.3 19.9 %collective-permute-start.38 = (bf16[4,96,512]{2,1,0:T(8,128)(2,1)}, bf16[4,96,512]{2,1,0:T(8,128)(2,1)S(1)}, u32[]{:S(2)}, u32[]{:S(2)}) collective-permute-start(bf16[4,96,512]{2,1,0:T(8,128)(2,1)} %get-tuple-element.269), channel_id=1, source_target_pairs={{0,16},{1,17},{2,18},{3,19},{4,20},{5,21},{6,22},{7,23},{8,24},{9,... | collective-permute-start | bytes 1179656 | tf_op jit(solution)/shard_map/ppermute | solution.py:170
  155.2 19.0 %collective-permute-start.39 = (bf16[4,96,512]{2,1,0:T(8,128)(2,1)S(1)}, bf16[4,96,512]{2,1,0:T(8,128)(2,1)S(1)}, u32[]{:S(2)}, u32[]{:S(2)}) collective-permute-start(bf16[4,96,512]{2,1,0:T(8,128)(2,1)S(1)} %get-tuple-element.270), channel_id=1, source_target_pairs={{0,17},{1,16},{2,19},{3,18},{4,21},{5,20},{6,23},{7,22},{8,25},{9,... | collective-permute-start | bytes 1179656 | tf_op jit(solution)/shard_map/ppermute | solution.py:170
  176.6 18.4 %collective-permute-start.40 = (bf16[16,96,512]{2,1,0:T(8,128)(2,1)}, bf16[16,96,512]{2,1,0:T(8,128)(2,1)}, u32[]{:S(2)}, u32[]{:S(2)}) collective-permute-start(bf16[16,96,512]{2,1,0:T(8,128)(2,1)} %get-tuple-element.297), channel_id=1, source_target_pairs={{0,8},{1,9},{2,10},{3,11},{4,12},{5,13},{6,14},{7,15},{8,0},{9,1},... | collective-permute-start | bytes 4718600 | tf_op jit(solution)/shard_map/ppermute | solution.py:170
  176.7 18.3 %collective-permute-start.41 = (bf16[4,64,512]{2,1,0:T(8,128)(2,1)}, bf16[4,64,512]{2,1,0:T(8,128)(2,1)S(1)}, u32[]{:S(2)}, u32[]{:S(2)}) collective-permute-start(bf16[4,64,512]{2,1,0:T(8,128)(2,1)} %get-tuple-element.298), channel_id=1, source_target_pairs={{0,1},{1,0},{2,3},{3,2},{4,5},{5,4},{6,7},{7,6},{8,9},{9,8},{10,11... | collective-permute-start | bytes 786440 | tf_op jit(solution)/shard_map/ppermute | solution.py:170
  177.9 17.0 %collective-permute-start.42 = (bf16[4,64,512]{2,1,0:T(8,128)(2,1)S(1)}, bf16[4,64,512]{2,1,0:T(8,128)(2,1)S(1)}, u32[]{:S(2)}, u32[]{:S(2)}) collective-permute-start(bf16[4,64,512]{2,1,0:T(8,128)(2,1)S(1)} %get-tuple-element.299), channel_id=1, source_target_pairs={{0,16},{1,17},{2,18},{3,19},{4,20},{5,21},{6,22},{7,23},{8,24},{9,... | collective-permute-start | bytes 786440 | tf_op jit(solution)/shard_map/ppermute | solution.py:170
  178.9 16.1 %collective-permute-start.43 = (bf16[4,64,512]{2,1,0:T(8,128)(2,1)S(1)}, bf16[4,64,512]{2,1,0:T(8,128)(2,1)S(1)}, u32[]{:S(2)}, u32[]{:S(2)}) collective-permute-start(bf16[4,64,512]{2,1,0:T(8,128)(2,1)S(1)} %get-tuple-element.300), channel_id=1, source_target_pairs={{0,17},{1,16},{2,19},{3,18},{4,21},{5,20},{6,23},{7,22},{8,25},{9,... | collective-permute-start | bytes 786440 | tf_op jit(solution)/shard_map/ppermute | solution.py:170
  180.2 14.7 %collective-permute-start.44 = (bf16[2,96,512]{2,1,0:T(8,128)(2,1)S(1)}, bf16[2,96,512]{2,1,0:T(8,128)(2,1)S(1)}, u32[]{:S(2)}, u32[]{:S(2)}) collective-permute-start(bf16[2,96,512]{2,1,0:T(8,128)(2,1)S(1)} %get-tuple-element.301), channel_id=1, source_target_pairs={{0,2},{1,3},{2,0},{3,1},{4,6},{5,7},{6,4},{7,5},{8,10},{9,11},{10,... | collective-permute-start | bytes 589832 | tf_op jit(solution)/shard_map/ppermute | solution.py:170
  198.4 18.1 %collective-permute-start.45 = (bf16[4,96,512]{2,1,0:T(8,128)(2,1)}, bf16[4,96,512]{2,1,0:T(8,128)(2,1)S(1)}, u32[]{:S(2)}, u32[]{:S(2)}) collective-permute-start(bf16[4,96,512]{2,1,0:T(8,128)(2,1)} %get-tuple-element.315), channel_id=1, source_target_pairs={{0,1},{1,0},{2,3},{3,2},{4,5},{5,4},{6,7},{7,6},{8,9},{9,8},{10,11... | collective-permute-start | bytes 1179656 | tf_op jit(solution)/shard_map/ppermute | solution.py:170
  199.7 17.3 %collective-permute-start.46 = (bf16[4,96,512]{2,1,0:T(8,128)(2,1)}, bf16[4,96,512]{2,1,0:T(8,128)(2,1)S(1)}, u32[]{:S(2)}, u32[]{:S(2)}) collective-permute-start(bf16[4,96,512]{2,1,0:T(8,128)(2,1)} %get-tuple-element.316), channel_id=1, source_target_pairs={{0,16},{1,17},{2,18},{3,19},{4,20},{5,21},{6,22},{7,23},{8,24},{9,... | collective-permute-start | bytes 1179656 | tf_op jit(solution)/shard_map/ppermute | solution.py:170
  200.6 17.8 %collective-permute-start.47 = (bf16[4,96,512]{2,1,0:T(8,128)(2,1)S(1)}, bf16[4,96,512]{2,1,0:T(8,128)(2,1)S(1)}, u32[]{:S(2)}, u32[]{:S(2)}) collective-permute-start(bf16[4,96,512]{2,1,0:T(8,128)(2,1)S(1)} %get-tuple-element.317), channel_id=1, source_target_pairs={{0,17},{1,16},{2,19},{3,18},{4,21},{5,20},{6,23},{7,22},{8,25},{9,... | collective-permute-start | bytes 1179656 | tf_op jit(solution)/shard_map/ppermute | solution.py:170
  202.0 14.6 %collective-permute-start.48 = (bf16[96,512]{1,0:T(8,128)(2,1)S(1)}, bf16[96,512]{1,0:T(8,128)(2,1)S(1)}, u32[]{:S(2)}, u32[]{:S(2)}) collective-permute-start(bf16[96,512]{1,0:T(8,128)(2,1)S(1)} %get-tuple-element.320), channel_id=1, source_target_pairs={{0,4},{1,5},{2,6},{3,7},{4,0},{5,1},{6,2},{7,3},{8,12},{9,13},{10,... | collective-permute-start | bytes 294920 | tf_op jit(solution)/shard_map/ppermute | solution.py:170
  222.0 15.8 %collective-permute-start.52 = (bf16[4,64,512]{2,1,0:T(8,128)(2,1)S(1)}, bf16[4,64,512]{2,1,0:T(8,128)(2,1)S(1)}, u32[]{:S(2)}, u32[]{:S(2)}) collective-permute-start(bf16[4,64,512]{2,1,0:T(8,128)(2,1)S(1)} %get-tuple-element.345), channel_id=1, source_target_pairs={{0,1},{1,0},{2,3},{3,2},{4,5},{5,4},{6,7},{7,6},{8,9},{9,8},{10,11... | collective-permute-start | bytes 786440 | tf_op jit(solution)/shard_map/ppermute | solution.py:170
  222.8 15.0 %collective-permute-start.53 = (bf16[4,64,512]{2,1,0:T(8,128)(2,1)S(1)}, bf16[4,64,512]{2,1,0:T(8,128)(2,1)S(1)}, u32[]{:S(2)}, u32[]{:S(2)}) collective-permute-start(bf16[4,64,512]{2,1,0:T(8,128)(2,1)S(1)} %get-tuple-element.346), channel_id=1, source_target_pairs={{0,16},{1,17},{2,18},{3,19},{4,20},{5,21},{6,22},{7,23},{8,24},{9,... | collective-permute-start | bytes 786440 | tf_op jit(solution)/shard_map/ppermute | solution.py:170
  (92 other events, 792.8 us)
where the time goes:
time: 249 us
  Pallas kernels  145 us (58%)
  starting transfers between devices  52.6 us (21%)
  waiting for transfers between devices  33.1 us (13%)
  other arithmetic  6.91 us (3%)
  between operations  5.67 us (2%)
  local copies, waits for them, and re-layouts  5.06 us (2%)
    ppermute x58, starting transfers between devices, swap(): lax.ppermute(block, AXES, [(one, one ^ offset) for one in range(OWNERS)])  52.6 us
    pallas_call x3, Pallas kernels, attend_back_call(): pl.pallas_call(attend_back_kernel, grid_spec=pltpu.PrefetchScalarGridSpec...  47.6 us
    pallas_call x2, Pallas kernels, attend_call(): pl.pallas_call(attend_kernel, grid_spec=pltpu.PrefetchScalarGridSpec(num_...  38 us
    ppermute x58, waiting for transfers between devices, swap(): lax.ppermute(block, AXES, [(one, one ^ offset) for one in range(OWNERS)])  33.1 us
    pallas_call x1, Pallas kernels, dense_turn_call(): pl.pallas_call(dense_turn_kernel, grid_spec=pltpu.PrefetchScalarGridSpec(...  19.5 us
    pallas_call x1, Pallas kernels, dense_back_call(): pl.pallas_call(dense_back_kernel, grid_spec=pltpu.PrefetchScalarGridSpec(...  17.5 us
    pallas_call x1, Pallas kernels, dense_call(): pl.pallas_call(dense_kernel, grid_spec=pltpu.PrefetchScalarGridSpec(num_s...  10.4 us
    convert_element_type x4, other arithmetic, core_sum(): (kept[at:at + 4].astype(FLOAT) + got[at:at + 4].astype(FLOAT)).astype(HALF)  6.7 us
  transfers between devices with their start and end apart: 58, of which 22 were waited for; matrix products, arithmetic and copies ran while one was open for 0% of the time, Pallas kernels for 49%

commit v1 on v0

--- a/solution.py
+++ b/solution.py
@@ -20,11 +20,11 @@
 CORE = 8
 ORDER = tuple(core ^ side ^ link for core in (0, CORE) for side in SQUARE for link in CHAIN)
 
-FIRST_ROWS = 64
-SECOND_ROWS = 96
-
-SCORE_BLOCK = 256
-ROW_BLOCK = 256
+FIRST_ROWS = 56
+SECOND_ROWS = 88
+
+ROW_BLOCK = 512
+BACK_BLOCK = 256
 ROOT_HALF = 0.7071067811865476
 PDF_PEAK = 0.3989422804014327
 VMEM_LIMIT = 60 * 1024 * 1024
@@ -69,7 +69,8 @@
             ].astype(HALF)
         small[...] = jnp.zeros_like(small)
         small[0:2, :] = biases[0:2, :]
-        first[48:64, :] = small[...].astype(HALF)
+        small[2:3, :] = (lanes == ids_ref[0]).astype(FLOAT)
+        first[48:56, :] = small[...].astype(HALF)
         second[top : top + 16, :] = output_ref[layer].astype(HALF)
         for piece in range(2):
             second[top + (piece + 1) * 16 : top + (piece + 2) * 16, :] = expand_ref[
@@ -78,8 +79,7 @@
         second[top + 48 : top + 80, :] = shrink_ref[layer].astype(HALF)
         small[0:2, :] = gains
         small[2:8, :] = biases[2:8, :]
-        small[8:9, :] = (lanes == ids_ref[0]).astype(FLOAT)
-        second[top + 80 : top + 96, :] = small[...].astype(HALF)
+        second[top + 80 : top + 88, :] = small[...].astype(HALF)
 
 
 def pack_call(place, ids, masters):
@@ -91,7 +91,7 @@
         + [pl.BlockSpec(memory_space=pltpu.VMEM)] * 6,
         out_specs=[pl.BlockSpec(memory_space=pltpu.VMEM)] * 3,
         out_shape=[LIKE((count, width), HALF) for count in rows],
-        scratch_shapes=[pltpu.VMEM((16, width), FLOAT)],
+        scratch_shapes=[pltpu.VMEM((8, width), FLOAT)],
         compiler_params=params(),
         cost_estimate=pl.CostEstimate(flops=0, bytes_accessed=1 << 20, transcendentals=0),
         name="pack",
@@ -183,14 +183,14 @@
     total = None
     for slots in slot_refs:
         for at in range(slots.shape[0]):
-            block = slots[at, start : start + 16, :].astype(FLOAT)
+            block = slots[at, start : start + 8, :].astype(FLOAT)
             total = block if total is None else total + block
     return total
 
 
 def attend_kernel(place_ref, x_ref, *refs):
     slot_refs = refs[:8]
-    joint_ref, probs_ref, mixed_ref, weight_ref = refs[8:]
+    joint_ref, probs_ref, mixed_ref, weight_ref, small_ref = refs[8:]
     head_size = mixed_ref.shape[1]
     place = place_ref[0]
 
@@ -202,22 +202,20 @@
             ]
     zeros = jnp.zeros((1, head_size), FLOAT)
     small = small_rows(slot_refs, 48)
+    small_ref[...] = small
     shift = jnp.concatenate([small[0:1, :], zeros, small[1:2, :]], axis=1)
     joint_ref[0] = (product(x_ref[...], weight_ref[0], 1, 0) + shift).astype(HALF)
     keys = joint_ref[0, :CTX, head_size : 2 * head_size]
     values = joint_ref[0, :CTX, 2 * head_size :]
     values_turned = jnp.transpose(values)
     factor = head_size ** (-0.5) * 1.4426950408889634
-    for start in range(0, x_ref.shape[0], SCORE_BLOCK):
-        span = slice(start, start + SCORE_BLOCK)
-        queries = joint_ref[0, span, :head_size]
-        scores = product(keys, queries, 1, 1)
-        top = jnp.max(scores, axis=0, keepdims=True)
-        grown = jnp.exp2((scores - top) * factor)
-        total = jnp.sum(grown, axis=0, keepdims=True)
-        probs = (grown * (1.0 / total)).astype(HALF)
-        probs_ref[0, :, span] = probs
-        mixed_ref[span, :] = jnp.transpose(product(values_turned, probs, 1, 0)).astype(HALF)
+    scores = product(keys, joint_ref[0, :, :head_size], 1, 1)
+    top = jnp.max(scores, axis=0, keepdims=True)
+    grown = jnp.exp2((scores - top) * factor)
+    total = jnp.sum(grown, axis=0, keepdims=True)
+    probs = (grown * (1.0 / total)).astype(HALF)
+    probs_ref[0] = probs
+    mixed_ref[...] = jnp.transpose(product(values_turned, probs, 1, 0)).astype(HALF)
 
 
 def attend_call(place, x, slots):
@@ -236,6 +234,7 @@
                 pl.BlockSpec((1, CTX, rows), lambda h, p: (h, 0, 0)),
                 pl.BlockSpec((rows, head_size), lambda h, p: (0, h)),
                 pl.BlockSpec((1, width, 3 * head_size), lambda h, p: (h, 0, 0)),
+                pl.BlockSpec((8, head_size), lambda h, p: (0, h)),
             ],
         ),
         out_shape=[
@@ -243,6 +242,7 @@
             LIKE((HEADS, CTX, rows), HALF),
             LIKE((rows, HEADS * head_size), HALF),
             LIKE((HEADS, width, 3 * head_size), HALF),
+            LIKE((8, width), FLOAT),
         ],
         compiler_params=params(),
         cost_estimate=pl.CostEstimate(
@@ -337,7 +337,7 @@
         slots_ref[at, 16:32, :] = grad_expand[rows, :width].astype(HALF)
         slots_ref[at, 32:48, :] = grad_expand[rows, width:].astype(HALF)
         slots_ref[at, 48:80, :] = grad_shrink[owner_rows(offset, place, 32), :].astype(HALF)
-        slots_ref[at, 80:96, :] = small
+        slots_ref[at, 80:88, :] = small
 
 
 def dense_kernel(place_ref, x_ref, mixed_ref, *refs):
@@ -397,7 +397,7 @@
 
 def dense_turn_kernel(place_ref, live_ref, ids_ref, x_ref, mixed_ref, *refs):
     slot_refs = refs[:8]
-    (cot_ref, result_ref, grad_mixed_ref, grad_one_ref, kept_ref, sent_ref, output_w, expand_w,
+    (counts_ref, cot_ref, result_ref, grad_mixed_ref, grad_one_ref, kept_ref, sent_ref, output_w, expand_w,
      shrink_w, vec_ref, grad_output, grad_expand, grad_shrink, sums) = refs[8:]
     step = pl.program_id(0)
 
@@ -408,7 +408,7 @@
 
     *kept, result = forward_rows(x_ref, mixed_ref, vec_ref, output_w, expand_w, shrink_w)
     result_ref[...] = result.astype(HALF)
-    counts = vec_ref[8:9, :]
+    counts = counts_ref[2:3, :]
     lanes = lax.broadcasted_iota(jnp.int32, counts.shape, 1)
     own_count = jnp.sum(jnp.where(lanes == ids_ref[0], counts, 0.0), axis=1, keepdims=True)
     row_weight = jnp.sum(counts, axis=1, keepdims=True) / (NDS * own_count)
@@ -423,17 +423,17 @@
         pack_second(place_ref[0], kept_ref, sent_ref, grad_output, grad_expand, grad_shrink, sums)
 
 
-def by_rows(width):
-    return pl.BlockSpec((ROW_BLOCK, width), lambda i, *p: (i, 0))
+def by_rows(width, block=ROW_BLOCK):
+    return pl.BlockSpec((block, width), lambda i, *p: (i, 0))
 
 
 def fixed(*shape):
     return pl.BlockSpec(shape, lambda i, *p: (0,) * len(shape))
 
 
-def joint_rows(grad_joint):
+def joint_rows(grad_joint, block=ROW_BLOCK):
     heads, _, width = grad_joint.shape
-    return pl.BlockSpec((heads, ROW_BLOCK, width), lambda i, *p: (0, i, 0))
+    return pl.BlockSpec((heads, block, width), lambda i, *p: (0, i, 0))
 
 
 def weight_shapes(width):
@@ -453,13 +453,13 @@
             out_specs=[by_rows(width), by_rows(width), by_rows(1), by_rows(2 * width),
                        by_rows(2 * width), by_rows(width), by_rows(1)]
             + [fixed(*shape) for shape in weights]
-            + [fixed(16, width)],
+            + [fixed(8, width)],
         ),
         out_shape=[LIKE((rows, width), HALF), LIKE((rows, width), FLOAT), LIKE((rows, 1), FLOAT),
                    LIKE((rows, 2 * width), HALF), LIKE((rows, 2 * width), FLOAT),
                    LIKE((rows, width), FLOAT), LIKE((rows, 1), FLOAT)]
         + [LIKE(shape, HALF) for shape in weights]
-        + [LIKE((16, width), FLOAT)],
+        + [LIKE((8, width), FLOAT)],
         compiler_params=params(),
         cost_estimate=pl.CostEstimate(
             flops=10 * rows * width * width, bytes_accessed=16 * 1024 * 1024,
@@ -472,18 +472,19 @@
 def dense_back_call(place, grad_one, grad_joint, weight, mixed, kept):
     rows, width = grad_one.shape
     weights = weight_shapes(width)
+    some_rows = functools.partial(by_rows, block=BACK_BLOCK)
     return pl.pallas_call(
         dense_back_kernel,
         grid_spec=pltpu.PrefetchScalarGridSpec(
             num_scalar_prefetch=1,
-            grid=(rows // ROW_BLOCK,),
-            in_specs=[by_rows(width), joint_rows(grad_joint), fixed(*weight.shape), by_rows(width)]
-            + [by_rows(width), by_rows(1), by_rows(2 * width), by_rows(2 * width), by_rows(width),
-               by_rows(1)]
+            grid=(rows // BACK_BLOCK,),
+            in_specs=[some_rows(width), joint_rows(grad_joint, BACK_BLOCK), fixed(*weight.shape), some_rows(width)]
+            + [some_rows(width), some_rows(1), some_rows(2 * width), some_rows(2 * width), some_rows(width),
+               some_rows(1)]
             + [fixed(*shape) for shape in weights]
-            + [fixed(16, width)],
-            out_specs=[by_rows(width), by_rows(width)] + [fixed(16, SECOND_ROWS, width)] * 2,
-            scratch_shapes=[pltpu.VMEM((16, width), FLOAT)]
+            + [fixed(8, width)],
+            out_specs=[some_rows(width), some_rows(width)] + [fixed(16, SECOND_ROWS, width)] * 2,
+            scratch_shapes=[pltpu.VMEM((8, width), FLOAT)]
             + [pltpu.VMEM(shape, FLOAT) for shape in weights],
         ),
         out_shape=[LIKE((rows, width), HALF), LIKE((rows, width), FLOAT)]
@@ -496,7 +497,7 @@
     )(place, grad_one, grad_joint, weight, mixed, *kept)
 
 
-def dense_turn_call(place, live, ids, x, mixed, slots, cotangent):
+def dense_turn_call(place, live, ids, x, mixed, slots, small, cotangent):
     rows, width = x.shape
     weights = weight_shapes(width)
     return pl.pallas_call(
@@ -506,12 +507,12 @@
             grid=(rows // ROW_BLOCK,),
             in_specs=[by_rows(width)] * 2
             + [fixed(*part.shape) for part in slots]
-            + [by_rows(width)],
+            + [fixed(8, width), by_rows(width)],
             out_specs=[by_rows(width)] * 3 + [fixed(16, SECOND_ROWS, width)] * 2,
             scratch_shapes=[pltpu.VMEM(shape, HALF) for shape in weights]
-            + [pltpu.VMEM((16, width), FLOAT)]
+            + [pltpu.VMEM((8, width), FLOAT)]
             + [pltpu.VMEM(shape, FLOAT) for shape in weights]
-            + [pltpu.VMEM((16, width), FLOAT)],
+            + [pltpu.VMEM((8, width), FLOAT)],
         ),
         out_shape=[LIKE((rows, width), HALF), LIKE((rows, width), HALF), LIKE((rows, width), FLOAT)]
         + [LIKE((16, SECOND_ROWS, width), HALF)] * 2,
@@ -521,7 +522,7 @@
             transcendentals=4 * rows * width,
         ),
         name="dense_turn",
-    )(place, live, ids, x, mixed, *slots, cotangent)
+    )(place, live, ids, x, mixed, *slots, small, cotangent)
 
 
 def attend_back_kernel(place_ref, x_ref, joint_ref, probs_ref, grad_mixed_ref, *refs):
@@ -541,18 +542,16 @@
     values = joint_ref[0, :CTX, 2 * head_size :]
     keys_turned = jnp.transpose(keys)
     factor = head_size ** (-0.5)
-    for start in range(0, rows, SCORE_BLOCK):
-        span = slice(start, start + SCORE_BLOCK)
-        grad_probs = product(values, grad_mixed_ref[span, :], 1, 1)
-        probs = probs_ref[0, :, span].astype(FLOAT)
-        weighted = probs * grad_probs
-        grad_low = (factor * (weighted - probs * column_sum(weighted))).astype(HALF)
-        grad_scores[:, span] = grad_low
-        grad_joint[span, :head_size] = jnp.transpose(product(keys_turned, grad_low, 1, 0)).astype(
-            HALF
-        )
-    grad_joint[:CTX, head_size : 2 * head_size] = product(
-        grad_scores[...], joint_ref[0, :, :head_size], 1, 0
+    grad_probs = product(values, grad_mixed_ref[...], 1, 1)
+    probs = probs_ref[0].astype(FLOAT)
+    level = column_sum(probs * grad_probs)
+    grad_low = (probs * (grad_probs - level)).astype(HALF)
+    grad_scores[...] = grad_low
+    grad_joint[:, :head_size] = jnp.transpose(factor * product(keys_turned, grad_low, 1, 0)).astype(
+        HALF
+    )
+    grad_joint[:CTX, head_size : 2 * head_size] = (
+        factor * product(grad_scores[...], joint_ref[0, :, :head_size], 1, 0)
     ).astype(HALF)
     grad_joint[:CTX, 2 * head_size :] = product(probs_ref[0], grad_mixed_ref[...], 1, 0).astype(HALF)
     sums = column_sum(grad_joint[...].astype(FLOAT))
@@ -570,7 +569,7 @@
             slots_ref[at, piece * 16 : (piece + 1) * 16, :] = holder[
                 span, piece * head_size : (piece + 1) * head_size
             ]
-        slots_ref[at, 48:64, :] = small_low
+        slots_ref[at, 48:56, :] = small_low
 
 
 def attend_back_call(place, x, joint, probs, grad_mixed, base=0, heads=HEADS, before=()):
@@ -591,7 +590,7 @@
             out_specs=[pl.BlockSpec((16, FIRST_ROWS, head_size), lambda h, p: (0, 0, h + base))] * 2
             + [pl.BlockSpec((1, rows, 3 * head_size), lambda h, p: (h + base, 0, 0))],
             scratch_shapes=[pltpu.VMEM((width, rows), HALF), pltpu.VMEM((CTX, rows), HALF),
-                            pltpu.VMEM((16, head_size), FLOAT)],
+                            pltpu.VMEM((8, head_size), FLOAT)],
         ),
         out_shape=[LIKE((16, FIRST_ROWS, width), HALF)] * 2
         + [LIKE((HEADS, rows, 3 * head_size), HALF)],
@@ -657,7 +656,7 @@
         step(1, (layer, slice(None), slice(0, width)), piece[16:32])
         step(1, (layer, slice(None), slice(width, 2 * width)), piece[32:48])
         step(2, (layer,), piece[48:80])
-        small_ref[layer] = piece[80:96]
+        small_ref[layer] = piece[80:88]
     first_ref[...] = middle[:FIRST_ROWS]
 
 
@@ -690,7 +689,7 @@
         for piece in range(3):
             columns = slice(piece * width, (piece + 1) * width)
             step(0, (layer, slice(None), columns), total[piece * 16 : (piece + 1) * 16])
-        own_first = pltpu.roll(total[48:64], turn, 1)[:, :each]
+        own_first = pltpu.roll(total[48:56], turn, 1)[:, :each]
         own_second = pltpu.roll(small_ref[layer], turn, 1)[:, :each]
         step(1, (layer,), own_second[0:2])
         step(2, (layer, slice(0, 2)), own_first[0:2])
@@ -746,33 +745,34 @@
     counts = low(lax.psum(onehot, AXES))[None]
     first, second = [], []
     for at in range(layers):
-        pad = lambda rows: jnp.pad(rows, ((0, 16 - rows.shape[0]), (0, 0)))
+        pad = lambda rows: jnp.pad(rows, ((0, 8 - rows.shape[0]), (0, 0)))
         attend_w = masters[0][at]
         first.append(gather_rows(
             [low(attend_w[:, piece * width : (piece + 1) * width]) for piece in range(3)],
-            pad(wide[at, 2:4]),
+            pad(jnp.concatenate([wide[at, 2:4], counts])),
         ))
         expand_w = masters[2][at]
         second.append(gather_rows(
             [low(masters[1][at]), low(expand_w[:, :width]), low(expand_w[:, width:]),
              low(masters[3][at])],
-            pad(jnp.concatenate([wide[at, 0:2], wide[at, 4:10], counts])),
+            jnp.concatenate([wide[at, 0:2], wide[at, 4:10]]),
         ))
     current = x
     saved = []
     for at in range(layers):
-        joint, probs, mixed, weight = attend_call(place, current, first[at])
+        joint, probs, mixed, weight, small = attend_call(place, current, first[at])
         keep = (current, joint, probs, mixed, weight)
         if at + 1 < layers:
             current, *rest = dense_call(place, current, mixed, second[at])
             keep = (*keep, rest)
         saved.append(keep)
+    counted = small
     first_grads, second_grads = [None] * layers, [None] * layers
     for at in reversed(range(layers)):
         start, joint, probs, mixed, weight = saved[at][:5]
         if at + 1 == layers:
             result, grad_mixed, grad_one, *slots = dense_turn_call(
-                place, live, dataset_ids, start, mixed, second[at], cotangent
+                place, live, dataset_ids, start, mixed, second[at], counted, cotangent
             )
         else:
             grad_mixed, grad_one, *slots = dense_back_call(
@@ -833,7 +833,7 @@
     first_far, second_own, x, late_two = sync(first_far, second_own, x, late_two)
     second_near = [second_own, *square(second_own)]
     late_got = swap(late_two, CHAIN[2])
-    joint, probs, mixed, weight = attend_call(place, x, [*first_near, *first_far])
+    joint, probs, mixed, weight, _ = attend_call(place, x, [*first_near, *first_far])
 
     mixed, second_near, late_two, late_got = sync(mixed, second_near, late_two, late_got)
     third_own, late_own = join_call(
@@ -850,14 +850,14 @@
     third_far, late_own, middle = sync(third_far, late_own, middle)
     late_near = [late_own, *square(late_own)]
     late_far = [swap(late_own, CORE)]
-    late_joint, late_probs, late_mixed, late_weight = attend_call(
+    late_joint, late_probs, late_mixed, late_weight, small = attend_call(
         place, middle, [*third_near, *third_far]
     )
 
     late_mixed, late_near, late_far = sync(late_mixed, late_near, late_far)
     late_far += to_core(late_near[1:])
     result, grad_mixed, grad_one, kept, sent = dense_turn_call(
-        place, live, dataset_ids, middle, late_mixed, [*late_near, *late_far], cotangent
+        place, live, dataset_ids, middle, late_mixed, [*late_near, *late_far], small, cotangent
     )
 
     sent, grad_mixed = sync(sent, grad_mixed)
@@ -922,7 +922,7 @@
         [rates],
         [middle_own, middle_got, late_own, late_got, *state_of(1, 2, 3)],
         [*step_shapes(masters[1:4]), LIKE((FIRST_ROWS, width), FLOAT),
-         LIKE((2, 16, width), FLOAT)],
+         LIKE((2, 8, width), FLOAT)],
         "second_step",
     )
     rest = step_call(

time: 249 us -> 223 us (0.90)
  Pallas kernels: 145 us -> 121 us
    pallas_call x2, Pallas kernels: 38 us -> 26.6 us  [attend_call(): pl.pallas_call(attend_kernel, grid_spec=pltpu.PrefetchScalarGridSpec(num_...]
    pallas_call x3, Pallas kernels: 47.6 us -> 37.8 us  [attend_back_call(): pl.pallas_call(attend_back_kernel, grid_spec=pltpu.PrefetchScalarGridSpec...]
    unnamed x116 -> x112, local copies, waits for them, and re-layouts: 5.06 us -> 3.55 us
  transfers between devices with their start and end apart: 58 -> 58, of which waited for: 22 -> 24; matrix products, arithmetic and copies ran while one was open for 0% -> 0% of each run, Pallas kernels for 49% -> 45%
where the time goes in v1:
time: 223 us; the launch traced here: 222 us
  Pallas kernels  121 us (54%)
  starting transfers between devices  52 us (23%)
  waiting for transfers between devices  34.7 us (16%)
  other arithmetic  5.67 us (3%)
  between operations  5.63 us (3%)
  local copies, waits for them, and re-layouts  3.55 us (2%)
    ppermute x58, starting transfers between devices, swap(): lax.ppermute(block, AXES, [(one, one ^ offset) for one in range(OWNERS)])  52 us
    pallas_call x3, Pallas kernels, attend_back_call(): pl.pallas_call(attend_back_kernel, grid_spec=pltpu.PrefetchScalarGridSpec...  37.8 us
    ppermute x58, waiting for transfers between devices, swap(): lax.ppermute(block, AXES, [(one, one ^ offset) for one in range(OWNERS)])  34.7 us
    pallas_call x2, Pallas kernels, attend_call(): pl.pallas_call(attend_kernel, grid_spec=pltpu.PrefetchScalarGridSpec(num_...  26.6 us
    pallas_call x1, Pallas kernels, dense_back_call(): pl.pallas_call(dense_back_kernel, grid_spec=pltpu.PrefetchScalarGridSpec(...  17.6 us
    pallas_call x1, Pallas kernels, dense_turn_call(): pl.pallas_call(dense_turn_kernel, grid_spec=pltpu.PrefetchScalarGridSpec(...  17.5 us
    pallas_call x1, Pallas kernels, dense_call(): pl.pallas_call(dense_kernel, grid_spec=pltpu.PrefetchScalarGridSpec(num_s...  9.36 us
    pallas_call x1, Pallas kernels, grad_x_call(): pl.pallas_call(grad_x_kernel, grid=(rows // ROW_BLOCK,), in_specs=[by_row...  5.88 us
  transfers between devices with their start and end apart: 58, of which 24 were waited for; matrix products, arithmetic and copies ran while one was open for 0% of the time, Pallas kernels for 45%

profile of v1, /device:TPU:0, one launch (start us, length us, event | category | flops | bytes accessed | tf_op | source)
XLA Modules:
  0.0 222.1 jit_solution(6580677592661070126)
XLA Ops:
  1.3 2.0 pack.1
  3.3 4.1 %collective-permute-start = (bf16[56,512]{1,0:T(8,128)(2,1)}, bf16[56,512]{1,0:T(8,128)(2,1)S(1)}, u32[]{:S(2)}, u32[]{:S(2)}) collective-permute-start(bf16[56,512]{1,0:T(8,128)(2,1)} %get-tuple-element.202.refs_0_), channel_id=1, source_target_pairs={{0,4},{1,5},{2,6},{3,7},{4,0},{5,1},{6,2},{7,3},{8,12},{9,13},{10,... | collective-permute-start | bytes 172040 | tf_op jit(solution)/shard_map/ppermute | solution.py:170
  7.3 1.6 collective-permute-start.1
  11.7 3.4 %collective-permute-done.2.refs_3_ = bf16[56,512]{1,0:T(8,128)(2,1)S(1)} collective-permute-done((bf16[56,512]{1,0:T(8,128)(2,1)}, bf16[56,512]{1,0:T(8,128)(2,1)S(1)}, u32[]{:S(2)}, u32[]{:S(2)}) %collective-permute-start.2) | collective-permute-done | bytes 57376 | tf_op jit(solution)/shard_map/ppermute | solution.py:170
  20.2 2.2 %collective-permute-start.10 = (bf16[88,512]{1,0:T(8,128)(2,1)}, bf16[88,512]{1,0:T(8,128)(2,1)S(1)}, u32[]{:S(2)}, u32[]{:S(2)}) collective-permute-start(bf16[88,512]{1,0:T(8,128)(2,1)} %get-tuple-element.206.refs_0_), channel_id=1, source_target_pairs={{0,4},{1,5},{2,6},{3,7},{4,0},{5,1},{6,2},{7,3},{8,12},{9,13},{10,... | collective-permute-start | bytes 270344 | tf_op jit(solution)/shard_map/ppermute | solution.py:170
  22.4 7.2 %collective-permute-done.10.refs_1_ = bf16[88,512]{1,0:T(8,128)(2,1)S(1)} collective-permute-done((bf16[88,512]{1,0:T(8,128)(2,1)}, bf16[88,512]{1,0:T(8,128)(2,1)S(1)}, u32[]{:S(2)}, u32[]{:S(2)}) %collective-permute-start.10) | collective-permute-done | bytes 90144 | tf_op jit(solution)/shard_map/ppermute | solution.py:170
  32.6 5.6 %collective-permute-done.11.refs_1_ = bf16[2,88,512]{2,1,0:T(8,128)(2,1)S(1)} collective-permute-done((bf16[2,88,512]{2,1,0:T(8,128)(2,1)S(1)}, bf16[2,88,512]{2,1,0:T(8,128)(2,1)S(1)}, u32[]{:S(2)}, u32[]{:S(2)}) %collective-permute-start.11) | collective-permute-done | bytes 180256 | tf_op jit(solution)/shard_map/ppermute | solution.py:170
  38.3 1.6 collective-permute-start.13
  42.2 13.3 %attend.2 = (bf16[4,1024,384]{2,1,0:T(8,128)(2,1)}, bf16[4,896,1024]{2,1,0:T(8,128)(2,1)}, bf16[1024,512]{1,0:T(8,128)(2,1)}, bf16[4,512,384]{2,1,0:T(8,128)(2,1)}, f32[8,512]{1,0:T(8,128)}) custom-call(s32[1]{0:T(128)} %bitcast.place_ref, bf16[1024,512]{1,0:T(8,128)(2,1)} %bitcast.13, bf16[4,56,512]{2,1,0:T(8,128)(2,1)} %copy-done.5, ...), custom_call_target="tpu_custom_call" | custom-call | flops 3489660928 | bytes 16777216 | tf_op jit(solution)/shard_map/attend/pallas_call | solution.py:224
  63.8 9.4 %dense.1 = (bf16[1024,512]{1,0:T(8,128)(2,1)}, f32[1024,512]{1,0:T(8,128)}, f32[1024,1]{1,0:T(8,128)}, bf16[1024,1024]{1,0:T(8,128)(2,1)}, f32[1024,1024]{1,0:T(...) custom-call(s32[1]{0:T(128)} %bitcast.place_ref, ...), custom_call_target="tpu_custom_call" | custom-call | flops 2684354560 | bytes 16777216 | tf_op jit(solution)/shard_map/dense/pallas_call | solution.py:446
  79.4 13.3 %attend.3 = (bf16[4,1024,384]{2,1,0:T(8,128)(2,1)}, bf16[4,896,1024]{2,1,0:T(8,128)(2,1)}, bf16[1024,512]{1,0:T(8,128)(2,1)}, bf16[4,512,384]{2,1,0:T(8,128)(2,1)}, f32[8,512]{1,0:T(8,128)}) custom-call(s32[1]{0:T(128)} %bitcast.place_ref, bf16[1024,512]{1,0:T(8,128)(2,1)} %get-tuple-element.238.x_ref, bf16[4,56,512]{2,1,0:T(8,128)(2,1)} %copy-done.24, ...), custom_call_target="tpu_custom_call" | custom-call | flops 3489660928 | bytes 16777216 | tf_op jit(solution)/shard_map/attend/pallas_call | solution.py:224
  98.4 17.5 %dense_turn.1 = (bf16[1024,512]{1,0:T(8,128)(2,1)}, bf16[1024,512]{1,0:T(8,128)(2,1)}, f32[1024,512]{1,0:T(8,128)}, bf16[16,88,512]{2,1,0:T(8,128)(2,1)}, bf16[16,88,512]{2,1,0:T(8,128)(2,1)}) custom-call(s32[1]{0:T(128)} %bitcast.place_ref, s32[1]{0:T(128)S(6)} %add.71.live_ref, s32[1]{0:T(128)S(6)} %copy.58.ids_ref, ...), custom_call_target="tpu_custom_call" | custom-call | flops 8053063680 | bytes 16777216 | tf_op jit(solution)/shard_map/dense_turn/pallas_call | solution.py:503
  116.1 16.9 %attend_back.3 = (bf16[16,56,512]{2,1,0:T(8,128)(2,1)}, bf16[16,56,512]{2,1,0:T(8,128)(2,1)}, bf16[4,1024,384]{2,1,0:T(8,128)(2,1)}) custom-call(s32[1]{0:T(128)} %bitcast.place_ref, bf16[1024,512]{1,0:T(8,128)(2,1)} %get-tuple-element.238.x_ref, bf16[4,1024,384]{2,1,0:T(8,128)(2,1)} %get-tuple-element.256.joint_ref, ...), custom_call_target="tpu_custom_call" | custom-call | flops 5368709120 | bytes 16777216 | tf_op jit(solution)/shard_map/attend_back/pallas_call | solution.py:578
  138.1 17.6 %dense_back.1 = (bf16[1024,512]{1,0:T(8,128)(2,1)}, f32[1024,512]{1,0:T(8,128)}, bf16[16,88,512]{2,1,0:T(8,128)(2,1)}, bf16[16,88,512]{2,1,0:T(8,128)(2,1)}) custom-call(s32[1]{0:T(128)} %bitcast.place_ref, f32[1024,512]{1,0:T(8,128)} %get-tuple-element.273.grad_one_next, bf16[4,1024,384]{2,1,0:T(8,128)(2,1)} %get-tuple-element.274.grad_joint_next, ...), custom_call_target="tpu_custom_call" | custom-call | flops 6979321856 | bytes 20971520 | tf_op jit(solution)/shard_map/dense_back/pallas_call | solution.py:476
  162.1 10.5 %attend_back.4 = (bf16[16,56,512]{2,1,0:T(8,128)(2,1)}, bf16[16,56,512]{2,1,0:T(8,128)(2,1)}, bf16[4,1024,384]{2,1,0:T(8,128)(2,1)}) custom-call(s32[1]{0:T(128)} %bitcast.place_ref, bf16[1024,512]{1,0:T(8,128)(2,1)} %bitcast.15, bf16[4,1024,384]{2,1,0:T(8,128)(2,1)} %get-tuple-element.254.joint_ref, bf16[4,896,1024]{2,1,0:T(8,128)(2,1)} %get-tuple-element.255.probs_ref, ...), custom_call_target="tpu_custom_call" | custom-call | flops 2684354560 | bytes 8388608 | tf_op jit(solution)/shard_map/attend_back/pallas_call | solution.py:578
  172.6 2.5 %add_convert_fusion = (bf16[4,88,512]{2,1,0:T(8,128)(2,1)S(1)}, bf16[4,88,512]{2,1,0:T(8,128)(2,1)S(1)}, bf16[4,88,512]{2,1,0:T(8,128)(2,1)}, bf16[4,88,512]{2,1,0:T(8,128)(2,1)S(1)}) fusion(bf16[16,88,512]{2,1,0:T(8,128)(2,1)} %collective-permute-done.40, bf16[16,88,512]{2,1,0:T(8,128)(2,1)S(1)} %copy-done.26), kind=kLoop, calls=%fused_computation | loop fusion | flops 2883584 | bytes 4325376 | tf_op jit(solution)/shard_map/convert_element_type | solution.py:134
  178.7 2.3 %collective-permute-start.48 = (bf16[88,512]{1,0:T(8,128)(2,1)S(1)}, bf16[88,512]{1,0:T(8,128)(2,1)S(1)}, u32[]{:S(2)}, u32[]{:S(2)}) collective-permute-start(bf16[88,512]{1,0:T(8,128)(2,1)S(1)} %get-tuple-element.322), channel_id=1, source_target_pairs={{0,4},{1,5},{2,6},{3,7},{4,0},{5,1},{6,2},{7,3},{8,12},{9,13},{10,... | collective-permute-start | bytes 270344 | tf_op jit(solution)/shard_map/ppermute | solution.py:170
  181.0 10.3 %attend_back.5 = (bf16[16,56,512]{2,1,0:T(8,128)(2,1)}, bf16[16,56,512]{2,1,0:T(8,128)(2,1)}, bf16[4,1024,384]{2,1,0:T(8,128)(2,1)}) custom-call(s32[1]{0:T(128)} %bitcast.place_ref, bf16[1024,512]{1,0:T(8,128)(2,1)} %bitcast.16, bf16[4,1024,384]{2,1,0:T(8,128)(2,1)} %get-tuple-element.254.joint_ref, ...), custom_call_target="tpu_custom_call", output_to_operand_aliasing={{0}: (5, {}), {1}: (6, {}), {2}: (7, {})} | custom-call | flops 2684354560 | bytes 8388608 | tf_op jit(solution)/shard_map/attend_back/pallas_call | solution.py:578
  193.9 2.4 %collective-permute-done.49 = bf16[16,56,512]{2,1,0:T(8,128)(2,1)S(1)} collective-permute-done((bf16[16,56,512]{2,1,0:T(8,128)(2,1)}, bf16[16,56,512]{2,1,0:T(8,128)(2,1)S(1)}, u32[]{:S(2)}, u32[]{:S(2)}) %collective-permute-start.49) | collective-permute-done | bytes 917536 | tf_op jit(solution)/shard_map/ppermute | solution.py:170
  201.2 5.9 %grad_x.1 = f32[1024,512]{1,0:T(8,128)} custom-call(f32[1024,512]{1,0:T(8,128)} %get-tuple-element.337.grad_one_ref, bf16[4,1024,384]{2,1,0:T(8,128)(2,1)} %get-tuple-element.338.grad_joint_ref, bf16[4,512,384]{2,1,0:T(8,128)(2,1)} %get-tuple-element.339.weight_ref), custom_call_target="tpu_custom_call" | custom-call | flops 1610612736 | bytes 10485760 | tf_op jit(solution)/shard_map/grad_x/pallas_call | solution.py:613
  207.3 2.2 collective-permute-start.51
  214.1 2.6 %collective-permute-start.57 = (bf16[56,512]{1,0:T(8,128)(2,1)S(1)}, bf16[56,512]{1,0:T(8,128)(2,1)S(1)}, u32[]{:S(2)}, u32[]{:S(2)}) collective-permute-start(bf16[56,512]{1,0:T(8,128)(2,1)S(1)} %get-tuple-element.353), channel_id=1, source_target_pairs={{0,6},{1,7},{2,4},{3,5},{4,2},{5,3},{6,0},{7,1},{8,14},{9,15},{10,... | collective-permute-start | bytes 172040 | tf_op jit(solution)/shard_map/ppermute | solution.py:170
  216.8 1.7 collective-permute-done.51.refs_1_
  218.6 1.6 second_step.1
  (231 shorter events, 58.9 us)
Async XLA Ops:
  16.0 13.7 %collective-permute-start.4 = (bf16[4,56,512]{2,1,0:T(8,128)(2,1)S(1)}, bf16[4,56,512]{2,1,0:T(8,128)(2,1)S(1)}, u32[]{:S(2)}, u32[]{:S(2)}) collective-permute-start(bf16[4,56,512]{2,1,0:T(8,128)(2,1)S(1)} %join.5.refs_0_), channel_id=1, source_target_pairs={{0,1},{1,0},{2,3},{3,2},{4,5},{5,4},{6,7},{7,6},{8,9},{9,8},{10,11... | collective-permute-start | bytes 688136 | tf_op jit(solution)/shard_map/ppermute | solution.py:170
  17.5 12.7 %collective-permute-start.6 = (bf16[4,56,512]{2,1,0:T(8,128)(2,1)S(1)}, bf16[4,56,512]{2,1,0:T(8,128)(2,1)S(1)}, u32[]{:S(2)}, u32[]{:S(2)}) collective-permute-start(bf16[4,56,512]{2,1,0:T(8,128)(2,1)S(1)} %join.5.refs_0_), channel_id=1, source_target_pairs={{0,16},{1,17},{2,18},{3,19},{4,20},{5,21},{6,22},{7,23},{8,24},{9,... | collective-permute-start | bytes 688136 | tf_op jit(solution)/shard_map/ppermute | solution.py:170
  38.3 17.2 %collective-permute-start.13 = (bf16[4,88,512]{2,1,0:T(8,128)(2,1)S(1)}, bf16[4,88,512]{2,1,0:T(8,128)(2,1)S(1)}, u32[]{:S(2)}, u32[]{:S(2)}) collective-permute-start(bf16[4,88,512]{2,1,0:T(8,128)(2,1)S(1)} %join.7.refs_0_), channel_id=1, source_target_pairs={{0,1},{1,0},{2,3},{3,2},{4,5},{5,4},{6,7},{7,6},{8,9},{9,8},{10,11... | collective-permute-start | bytes 1081352 | tf_op jit(solution)/shard_map/ppermute | solution.py:170
  39.9 17.0 %collective-permute-start.14 = (bf16[4,88,512]{2,1,0:T(8,128)(2,1)S(1)}, bf16[4,88,512]{2,1,0:T(8,128)(2,1)S(1)}, u32[]{:S(2)}, u32[]{:S(2)}) collective-permute-start(bf16[4,88,512]{2,1,0:T(8,128)(2,1)S(1)} %join.7.refs_0_), channel_id=1, source_target_pairs={{0,16},{1,17},{2,18},{3,19},{4,20},{5,21},{6,22},{7,23},{8,24},{9,... | collective-permute-start | bytes 1081352 | tf_op jit(solution)/shard_map/ppermute | solution.py:170
  41.4 15.5 %collective-permute-start.15 = (bf16[4,88,512]{2,1,0:T(8,128)(2,1)S(1)}, bf16[4,88,512]{2,1,0:T(8,128)(2,1)S(1)}, u32[]{:S(2)}, u32[]{:S(2)}) collective-permute-start(bf16[4,88,512]{2,1,0:T(8,128)(2,1)S(1)} %join.7.refs_0_), channel_id=1, source_target_pairs={{0,17},{1,16},{2,19},{3,18},{4,21},{5,20},{6,23},{7,22},{8,25},{9,... | collective-permute-start | bytes 1081352 | tf_op jit(solution)/shard_map/ppermute | solution.py:170
  41.9 13.7 %collective-permute-start.16 = (bf16[2,144,512]{2,1,0:T(8,128)(2,1)S(1)}, bf16[2,144,512]{2,1,0:T(8,128)(2,1)S(1)}, u32[]{:S(2)}, u32[]{:S(2)}) collective-permute-start(bf16[2,144,512]{2,1,0:T(8,128)(2,1)S(1)} %join.8.refs_0_), channel_id=1, source_target_pairs={{0,2},{1,3},{2,0},{3,1},{4,6},{5,7},{6,4},{7,5},{8,10},{9,11},{10,... | collective-permute-start | bytes 884744 | tf_op jit(solution)/shard_map/ppermute | solution.py:170
  60.2 12.9 %collective-permute-start.21 = (bf16[4,56,512]{2,1,0:T(8,128)(2,1)S(1)}, bf16[4,56,512]{2,1,0:T(8,128)(2,1)S(1)}, u32[]{:S(2)}, u32[]{:S(2)}) collective-permute-start(bf16[4,56,512]{2,1,0:T(8,128)(2,1)S(1)} %get-tuple-element.239.refs_0_), channel_id=1, source_target_pairs={{0,1},{1,0},{2,3},{3,2},{4,5},{5,4},{6,7},{7,6},{8,9},{9,8},{10,11... | collective-permute-start | bytes 688136 | tf_op jit(solution)/shard_map/ppermute | solution.py:170
  75.9 16.9 %collective-permute-start.28 = (bf16[4,88,512]{2,1,0:T(8,128)(2,1)S(1)}, bf16[4,88,512]{2,1,0:T(8,128)(2,1)S(1)}, u32[]{:S(2)}, u32[]{:S(2)}) collective-permute-start(bf16[4,88,512]{2,1,0:T(8,128)(2,1)S(1)} %get-tuple-element.247.refs_0_), channel_id=1, source_target_pairs={{0,1},{1,0},{2,3},{3,2},{4,5},{5,4},{6,7},{7,6},{8,9},{9,8},{10,11... | collective-permute-start | bytes 1081352 | tf_op jit(solution)/shard_map/ppermute | solution.py:170
  76.7 17.0 %collective-permute-start.29 = (bf16[4,88,512]{2,1,0:T(8,128)(2,1)S(1)}, bf16[4,88,512]{2,1,0:T(8,128)(2,1)S(1)}, u32[]{:S(2)}, u32[]{:S(2)}) collective-permute-start(bf16[4,88,512]{2,1,0:T(8,128)(2,1)S(1)} %get-tuple-element.247.refs_0_), channel_id=1, source_target_pairs={{0,16},{1,17},{2,18},{3,19},{4,20},{5,21},{6,22},{7,23},{8,24},{9,... | collective-permute-start | bytes 1081352 | tf_op jit(solution)/shard_map/ppermute | solution.py:170
  78.3 16.7 %collective-permute-start.30 = (bf16[4,88,512]{2,1,0:T(8,128)(2,1)S(1)}, bf16[4,88,512]{2,1,0:T(8,128)(2,1)S(1)}, u32[]{:S(2)}, u32[]{:S(2)}) collective-permute-start(bf16[4,88,512]{2,1,0:T(8,128)(2,1)S(1)} %get-tuple-element.247.refs_0_), channel_id=1, source_target_pairs={{0,17},{1,16},{2,19},{3,18},{4,21},{5,20},{6,23},{7,22},{8,25},{9,... | collective-permute-start | bytes 1081352 | tf_op jit(solution)/shard_map/ppermute | solution.py:170
  79.4 15.6 %collective-permute-start.31 = (bf16[4,88,512]{2,1,0:T(8,128)(2,1)S(1)}, bf16[4,88,512]{2,1,0:T(8,128)(2,1)S(1)}, u32[]{:S(2)}, u32[]{:S(2)}) collective-permute-start(bf16[4,88,512]{2,1,0:T(8,128)(2,1)S(1)} %get-tuple-element.247.refs_0_), channel_id=1, source_target_pairs={{0,8},{1,9},{2,10},{3,11},{4,12},{5,13},{6,14},{7,15},{8,0},{9,1},... | collective-permute-start | bytes 1081352 | tf_op jit(solution)/shard_map/ppermute | solution.py:170
  115.9 17.1 %collective-permute-start.35 = (bf16[16,88,512]{2,1,0:T(8,128)(2,1)}, bf16[16,88,512]{2,1,0:T(8,128)(2,1)S(1)}, u32[]{:S(2)}, u32[]{:S(2)}) collective-permute-start(bf16[16,88,512]{2,1,0:T(8,128)(2,1)} %get-tuple-element.263), channel_id=1, source_target_pairs={{0,8},{1,9},{2,10},{3,11},{4,12},{5,13},{6,14},{7,15},{8,0},{9,1},... | collective-permute-start | bytes 4325384 | tf_op jit(solution)/shard_map/ppermute | solution.py:170
  134.3 21.5 %collective-permute-start.36 = (bf16[16,56,512]{2,1,0:T(8,128)(2,1)}, bf16[16,56,512]{2,1,0:T(8,128)(2,1)}, u32[]{:S(2)}, u32[]{:S(2)}) collective-permute-start(bf16[16,56,512]{2,1,0:T(8,128)(2,1)} %get-tuple-element.269), channel_id=1, source_target_pairs={{0,8},{1,9},{2,10},{3,11},{4,12},{5,13},{6,14},{7,15},{8,0},{9,1},... | collective-permute-start | bytes 2752520 | tf_op jit(solution)/shard_map/ppermute | solution.py:170
  134.6 21.1 %collective-permute-start.37 = (bf16[4,88,512]{2,1,0:T(8,128)(2,1)}, bf16[4,88,512]{2,1,0:T(8,128)(2,1)S(1)}, u32[]{:S(2)}, u32[]{:S(2)}) collective-permute-start(bf16[4,88,512]{2,1,0:T(8,128)(2,1)} %get-tuple-element.270), channel_id=1, source_target_pairs={{0,1},{1,0},{2,3},{3,2},{4,5},{5,4},{6,7},{7,6},{8,9},{9,8},{10,11... | collective-permute-start | bytes 1081352 | tf_op jit(solution)/shard_map/ppermute | solution.py:170
  135.7 20.1 %collective-permute-start.38 = (bf16[4,88,512]{2,1,0:T(8,128)(2,1)S(1)}, bf16[4,88,512]{2,1,0:T(8,128)(2,1)S(1)}, u32[]{:S(2)}, u32[]{:S(2)}) collective-permute-start(bf16[4,88,512]{2,1,0:T(8,128)(2,1)S(1)} %get-tuple-element.271), channel_id=1, source_target_pairs={{0,16},{1,17},{2,18},{3,19},{4,20},{5,21},{6,22},{7,23},{8,24},{9,... | collective-permute-start | bytes 1081352 | tf_op jit(solution)/shard_map/ppermute | solution.py:170
  137.0 18.8 %collective-permute-start.39 = (bf16[4,88,512]{2,1,0:T(8,128)(2,1)S(1)}, bf16[4,88,512]{2,1,0:T(8,128)(2,1)S(1)}, u32[]{:S(2)}, u32[]{:S(2)}) collective-permute-start(bf16[4,88,512]{2,1,0:T(8,128)(2,1)S(1)} %get-tuple-element.272), channel_id=1, source_target_pairs={{0,17},{1,16},{2,19},{3,18},{4,21},{5,20},{6,23},{7,22},{8,25},{9,... | collective-permute-start | bytes 1081352 | tf_op jit(solution)/shard_map/ppermute | solution.py:170
  157.5 15.1 %collective-permute-start.40 = (bf16[16,88,512]{2,1,0:T(8,128)(2,1)}, bf16[16,88,512]{2,1,0:T(8,128)(2,1)}, u32[]{:S(2)}, u32[]{:S(2)}) collective-permute-start(bf16[16,88,512]{2,1,0:T(8,128)(2,1)} %get-tuple-element.299), channel_id=1, source_target_pairs={{0,8},{1,9},{2,10},{3,11},{4,12},{5,13},{6,14},{7,15},{8,0},{9,1},... | collective-permute-start | bytes 4325384 | tf_op jit(solution)/shard_map/ppermute | solution.py:170
  157.6 15.0 %collective-permute-start.41 = (bf16[4,56,512]{2,1,0:T(8,128)(2,1)S(1)}, bf16[4,56,512]{2,1,0:T(8,128)(2,1)S(1)}, u32[]{:S(2)}, u32[]{:S(2)}) collective-permute-start(bf16[4,56,512]{2,1,0:T(8,128)(2,1)S(1)} %get-tuple-element.300), channel_id=1, source_target_pairs={{0,1},{1,0},{2,3},{3,2},{4,5},{5,4},{6,7},{7,6},{8,9},{9,8},{10,11... | collective-permute-start | bytes 688136 | tf_op jit(solution)/shard_map/ppermute | solution.py:170
  158.7 13.9 %collective-permute-start.42 = (bf16[4,56,512]{2,1,0:T(8,128)(2,1)S(1)}, bf16[4,56,512]{2,1,0:T(8,128)(2,1)S(1)}, u32[]{:S(2)}, u32[]{:S(2)}) collective-permute-start(bf16[4,56,512]{2,1,0:T(8,128)(2,1)S(1)} %get-tuple-element.301), channel_id=1, source_target_pairs={{0,16},{1,17},{2,18},{3,19},{4,20},{5,21},{6,22},{7,23},{8,24},{9,... | collective-permute-start | bytes 688136 | tf_op jit(solution)/shard_map/ppermute | solution.py:170
  175.2 16.2 %collective-permute-start.45 = (bf16[4,88,512]{2,1,0:T(8,128)(2,1)}, bf16[4,88,512]{2,1,0:T(8,128)(2,1)S(1)}, u32[]{:S(2)}, u32[]{:S(2)}) collective-permute-start(bf16[4,88,512]{2,1,0:T(8,128)(2,1)} %get-tuple-element.317), channel_id=1, source_target_pairs={{0,1},{1,0},{2,3},{3,2},{4,5},{5,4},{6,7},{7,6},{8,9},{9,8},{10,11... | collective-permute-start | bytes 1081352 | tf_op jit(solution)/shard_map/ppermute | solution.py:170
  176.2 15.9 %collective-permute-start.46 = (bf16[4,88,512]{2,1,0:T(8,128)(2,1)S(1)}, bf16[4,88,512]{2,1,0:T(8,128)(2,1)S(1)}, u32[]{:S(2)}, u32[]{:S(2)}) collective-permute-start(bf16[4,88,512]{2,1,0:T(8,128)(2,1)S(1)} %get-tuple-element.318), channel_id=1, source_target_pairs={{0,16},{1,17},{2,18},{3,19},{4,20},{5,21},{6,22},{7,23},{8,24},{9,... | collective-permute-start | bytes 1081352 | tf_op jit(solution)/shard_map/ppermute | solution.py:170
  177.6 16.0 %collective-permute-start.47 = (bf16[4,88,512]{2,1,0:T(8,128)(2,1)S(1)}, bf16[4,88,512]{2,1,0:T(8,128)(2,1)S(1)}, u32[]{:S(2)}, u32[]{:S(2)}) collective-permute-start(bf16[4,88,512]{2,1,0:T(8,128)(2,1)S(1)} %get-tuple-element.319), channel_id=1, source_target_pairs={{0,17},{1,16},{2,19},{3,18},{4,21},{5,20},{6,23},{7,22},{8,25},{9,... | collective-permute-start | bytes 1081352 | tf_op jit(solution)/shard_map/ppermute | solution.py:170
  197.7 14.4 %collective-permute-start.52 = (bf16[4,56,512]{2,1,0:T(8,128)(2,1)S(1)}, bf16[4,56,512]{2,1,0:T(8,128)(2,1)S(1)}, u32[]{:S(2)}, u32[]{:S(2)}) collective-permute-start(bf16[4,56,512]{2,1,0:T(8,128)(2,1)S(1)} %get-tuple-element.347), channel_id=1, source_target_pairs={{0,1},{1,0},{2,3},{3,2},{4,5},{5,4},{6,7},{7,6},{8,9},{9,8},{10,11... | collective-permute-start | bytes 688136 | tf_op jit(solution)/shard_map/ppermute | solution.py:170
  198.7 13.4 %collective-permute-start.53 = (bf16[4,56,512]{2,1,0:T(8,128)(2,1)S(1)}, bf16[4,56,512]{2,1,0:T(8,128)(2,1)S(1)}, u32[]{:S(2)}, u32[]{:S(2)}) collective-permute-start(bf16[4,56,512]{2,1,0:T(8,128)(2,1)S(1)} %get-tuple-element.348), channel_id=1, source_target_pairs={{0,16},{1,17},{2,18},{3,19},{4,20},{5,21},{6,22},{7,23},{8,24},{9,... | collective-permute-start | bytes 688136 | tf_op jit(solution)/shard_map/ppermute | solution.py:170
  (90 other events, 775.3 us)

commit v2 on v1

--- a/solution.py
+++ b/solution.py
@@ -49,8 +49,9 @@
 
 
 def pack_kernel(place_ref, ids_ref, attend_ref, output_ref, expand_ref, shrink_ref, gains_ref,
-                bias_ref, near_ref, next_ref, late_ref, small):
-    width = near_ref.shape[1]
+                bias_ref, *outs):
+    *outs, small = outs
+    width = small.shape[1]
     each = gains_ref.shape[2]
     lane = lax.broadcasted_iota(jnp.int32, (each, width), 1)
     own = lax.broadcasted_iota(jnp.int32, (each, width), 0) + place_ref[0] * each
@@ -58,38 +59,36 @@
     lanes = lax.broadcasted_iota(jnp.int32, (1, width), 1)
 
     for layer in range(attend_ref.shape[0]):
-        first, second, top = (
-            (near_ref, next_ref, 0) if layer == 0 else (late_ref, late_ref, FIRST_ROWS)
-        )
+        first, top, second = (outs[0], 0, outs[1]) if layer == 0 else (outs[1], SECOND_ROWS, outs[2])
         gains = product(gains_ref[layer].astype(HALF), pick, 1, 0)
         biases = product(bias_ref[layer].astype(HALF), pick, 1, 0)
         for piece in range(3):
-            first[piece * 16 : (piece + 1) * 16, :] = attend_ref[
+            first[top + piece * 16 : top + (piece + 1) * 16, :] = attend_ref[
                 layer, :, piece * width : (piece + 1) * width
             ].astype(HALF)
         small[...] = jnp.zeros_like(small)
         small[0:2, :] = biases[0:2, :]
         small[2:3, :] = (lanes == ids_ref[0]).astype(FLOAT)
-        first[48:56, :] = small[...].astype(HALF)
-        second[top : top + 16, :] = output_ref[layer].astype(HALF)
+        first[top + 48 : top + 56, :] = small[...].astype(HALF)
+        second[0:16, :] = output_ref[layer].astype(HALF)
         for piece in range(2):
-            second[top + (piece + 1) * 16 : top + (piece + 2) * 16, :] = expand_ref[
+            second[(piece + 1) * 16 : (piece + 2) * 16, :] = expand_ref[
                 layer, :, piece * width : (piece + 1) * width
             ].astype(HALF)
-        second[top + 48 : top + 80, :] = shrink_ref[layer].astype(HALF)
+        second[48:80, :] = shrink_ref[layer].astype(HALF)
         small[0:2, :] = gains
         small[2:8, :] = biases[2:8, :]
-        second[top + 80 : top + 88, :] = small[...].astype(HALF)
+        second[80:88, :] = small[...].astype(HALF)
 
 
 def pack_call(place, ids, masters):
     width = masters[1].shape[2]
-    rows = (FIRST_ROWS, SECOND_ROWS, FIRST_ROWS + SECOND_ROWS)
+    rows = (FIRST_ROWS, SECOND_ROWS + FIRST_ROWS, SECOND_ROWS)
     return pl.pallas_call(
         pack_kernel,
         in_specs=[pl.BlockSpec(memory_space=pltpu.SMEM)] * 2
         + [pl.BlockSpec(memory_space=pltpu.VMEM)] * 6,
-        out_specs=[pl.BlockSpec(memory_space=pltpu.VMEM)] * 3,
+        out_specs=[pl.BlockSpec(memory_space=pltpu.VMEM)] * len(rows),
         out_shape=[LIKE((count, width), HALF) for count in rows],
         scratch_shapes=[pltpu.VMEM((8, width), FLOAT)],
         compiler_params=params(),
@@ -191,31 +190,42 @@
 def attend_kernel(place_ref, x_ref, *refs):
     slot_refs = refs[:8]
     joint_ref, probs_ref, mixed_ref, weight_ref, small_ref = refs[8:]
-    head_size = mixed_ref.shape[1]
+    count = joint_ref.shape[0]
+    head_size = joint_ref.shape[2] // 3
     place = place_ref[0]
 
     for slots, at, offset in slot_places(slot_refs):
         rows = owner_rows(offset, place, 16)
         for piece in range(3):
-            weight_ref[0, rows, piece * head_size : (piece + 1) * head_size] = slots[
-                at, piece * 16 : (piece + 1) * 16, :
-            ]
+            for head in range(count):
+                weight_ref[head, rows, piece * head_size : (piece + 1) * head_size] = slots[
+                    at, piece * 16 : (piece + 1) * 16, head * head_size : (head + 1) * head_size
+                ]
     zeros = jnp.zeros((1, head_size), FLOAT)
     small = small_rows(slot_refs, 48)
     small_ref[...] = small
-    shift = jnp.concatenate([small[0:1, :], zeros, small[1:2, :]], axis=1)
-    joint_ref[0] = (product(x_ref[...], weight_ref[0], 1, 0) + shift).astype(HALF)
-    keys = joint_ref[0, :CTX, head_size : 2 * head_size]
-    values = joint_ref[0, :CTX, 2 * head_size :]
-    values_turned = jnp.transpose(values)
     factor = head_size ** (-0.5) * 1.4426950408889634
-    scores = product(keys, joint_ref[0, :, :head_size], 1, 1)
-    top = jnp.max(scores, axis=0, keepdims=True)
-    grown = jnp.exp2((scores - top) * factor)
-    total = jnp.sum(grown, axis=0, keepdims=True)
-    probs = (grown * (1.0 / total)).astype(HALF)
-    probs_ref[0] = probs
-    mixed_ref[...] = jnp.transpose(product(values_turned, probs, 1, 0)).astype(HALF)
+    weights = jnp.concatenate([weight_ref[head] for head in range(count)], axis=1)
+    wide = product(x_ref[...], weights, 1, 0)
+    for head in range(count):
+        own = slice(head * head_size, (head + 1) * head_size)
+        shift = jnp.concatenate([small[0:1, own], zeros, small[1:2, own]], axis=1)
+        part = wide[:, 3 * head * head_size : 3 * (head + 1) * head_size]
+        joint_ref[head] = (part + shift).astype(HALF)
+    scores = []
+    for head in range(count):
+        keys = joint_ref[head, :CTX, head_size : 2 * head_size]
+        scores.append(product(keys, joint_ref[head, :, :head_size], 1, 1))
+    for head in range(count):
+        values_turned = jnp.transpose(joint_ref[head, :CTX, 2 * head_size :])
+        top = jnp.max(scores[head], axis=0, keepdims=True)
+        grown = jnp.exp2((scores[head] - top) * factor)
+        total = jnp.sum(grown, axis=0, keepdims=True)
+        probs = (grown * (1.0 / total)).astype(HALF)
+        probs_ref[head] = probs
+        mixed_ref[:, head * head_size : (head + 1) * head_size] = jnp.transpose(
+            product(values_turned, probs, 1, 0)
+        ).astype(HALF)
 
 
 def attend_call(place, x, slots):
@@ -225,16 +235,16 @@
         attend_kernel,
         grid_spec=pltpu.PrefetchScalarGridSpec(
             num_scalar_prefetch=1,
-            grid=(HEADS,),
+            grid=(HEADS // 2,),
             in_specs=[pl.BlockSpec((rows, width), lambda h, p: (0, 0))]
-            + [pl.BlockSpec((part.shape[0], FIRST_ROWS, head_size), lambda h, p: (0, 0, h))
+            + [pl.BlockSpec((part.shape[0], FIRST_ROWS, 2 * head_size), lambda h, p: (0, 0, h))
                for part in slots],
             out_specs=[
-                pl.BlockSpec((1, rows, 3 * head_size), lambda h, p: (h, 0, 0)),
-                pl.BlockSpec((1, CTX, rows), lambda h, p: (h, 0, 0)),
-                pl.BlockSpec((rows, head_size), lambda h, p: (0, h)),
-                pl.BlockSpec((1, width, 3 * head_size), lambda h, p: (h, 0, 0)),
-                pl.BlockSpec((8, head_size), lambda h, p: (0, h)),
+                pl.BlockSpec((2, rows, 3 * head_size), lambda h, p: (h, 0, 0)),
+                pl.BlockSpec((2, CTX, rows), lambda h, p: (h, 0, 0)),
+                pl.BlockSpec((rows, 2 * head_size), lambda h, p: (0, h)),
+                pl.BlockSpec((2, width, 3 * head_size), lambda h, p: (h, 0, 0)),
+                pl.BlockSpec((8, 2 * head_size), lambda h, p: (0, h)),
             ],
         ),
         out_shape=[
@@ -526,7 +536,7 @@
 
 
 def attend_back_kernel(place_ref, x_ref, joint_ref, probs_ref, grad_mixed_ref, *refs):
-    kept_ref, sent_ref, grad_joint_ref, x_turned, grad_scores, small = refs[-6:]
+    kept_ref, sent_ref, grad_joint_ref, grad_scores, small = refs[-5:]
     grad_joint = grad_joint_ref.at[0]
     rows = x_ref.shape[0]
     head_size = grad_mixed_ref.shape[1]
@@ -534,7 +544,6 @@
 
     @pl.when(pl.program_id(0) == 0)
     def _():
-        x_turned[...] = jnp.transpose(x_ref[...])
         clear(small)
 
     grad_joint[CTX:, head_size:] = jnp.zeros((rows - CTX, 2 * head_size), HALF)
@@ -558,7 +567,7 @@
     small[0:1, :] = sums[:, :head_size]
     small[1:2, :] = sums[:, 2 * head_size :]
     small_low = small[...].astype(HALF)
-    grad_low = product(x_turned[...], grad_joint[...], 1, 0).astype(HALF)
+    grad_low = product(x_ref[...], grad_joint[...], 0, 0).astype(HALF)
     holder = grad_scores
     holder[: grad_low.shape[0], : 3 * head_size] = grad_low
     for at, offset in enumerate(ORDER):
@@ -589,8 +598,7 @@
             + [pl.BlockSpec(memory_space=pl.ANY)] * len(before),
             out_specs=[pl.BlockSpec((16, FIRST_ROWS, head_size), lambda h, p: (0, 0, h + base))] * 2
             + [pl.BlockSpec((1, rows, 3 * head_size), lambda h, p: (h + base, 0, 0))],
-            scratch_shapes=[pltpu.VMEM((width, rows), HALF), pltpu.VMEM((CTX, rows), HALF),
-                            pltpu.VMEM((8, head_size), FLOAT)],
+            scratch_shapes=[pltpu.VMEM((CTX, rows), HALF), pltpu.VMEM((8, head_size), FLOAT)],
         ),
         out_shape=[LIKE((16, FIRST_ROWS, width), HALF)] * 2
         + [LIKE((HEADS, rows, 3 * head_size), HALF)],
@@ -820,33 +828,41 @@
     def chain_back(blocks):
         return [swap(one, offset) for one, offset in zip(blocks[1:], CHAIN[1:])]
 
-    near, following, late = pack_call(place, dataset_ids, masters)
-    (first_own,) = join_call([near, *swaps(near, CHAIN[1:])])
-
-    first_own, following, late = sync(first_own, following, late)
+    first, following, late = pack_call(place, dataset_ids, masters)
+    (first_own,) = join_call([first, *swaps(first, CHAIN[1:])])
+
+    first_own, following = sync(first_own, following)
     first_near = [first_own, *square(first_own)]
     (following_two,) = join_call([following, swap(following, CHAIN[1])])
-    (late_two,) = join_call([late, swap(late, CHAIN[1])])
-    (second_own,) = join_call([following_two, swap(following_two, CHAIN[2])])
+    second_own, third_own = join_call(
+        [following_two, swap(following_two, CHAIN[2])],
+        (0, SECOND_ROWS),
+        (SECOND_ROWS, FIRST_ROWS),
+    )
     first_far = to_core(first_near)
 
-    first_far, second_own, x, late_two = sync(first_far, second_own, x, late_two)
+    first_far, second_own, third_own, x, late = sync(first_far, second_own, third_own, x, late)
     second_near = [second_own, *square(second_own)]
-    late_got = swap(late_two, CHAIN[2])
+    second_far = [swap(second_own, CORE)]
+    late_got = swap(late, CHAIN[1])
     joint, probs, mixed, weight, _ = attend_call(place, x, [*first_near, *first_far])
 
-    mixed, second_near, late_two, late_got = sync(mixed, second_near, late_two, late_got)
-    third_own, late_own = join_call(
-        [late_two, late_got], (0, FIRST_ROWS), (FIRST_ROWS, SECOND_ROWS)
-    )
-    second_far = to_core(second_near)
-    second_far, third_own, mixed = sync(second_far, third_own, mixed)
+    mixed, second_near, second_far, third_own, late, late_got = sync(
+        mixed, second_near, second_far, third_own, late, late_got
+    )
+    (late_two,) = join_call([late, late_got])
+    second_far += to_core(second_near[1:])
+    second_far, third_own, late_two, mixed = sync(second_far, third_own, late_two, mixed)
     third_near = [third_own, *square(third_own)]
     third_far = [swap(third_own, CORE)]
+    late_got = swap(late_two, CHAIN[2])
     middle, *dense_kept = dense_call(place, x, mixed, [*second_near, *second_far])
 
-    middle, third_near, third_far, late_own = sync(middle, third_near, third_far, late_own)
+    middle, third_near, third_far, late_two, late_got = sync(
+        middle, third_near, third_far, late_two, late_got
+    )
     third_far += to_core(third_near[1:])
+    (late_own,) = join_call([late_two, late_got])
     third_far, late_own, middle = sync(third_far, late_own, middle)
     late_near = [late_own, *square(late_own)]
     late_far = [swap(late_own, CORE)]

time: 223 us -> 217 us (0.973)
  Pallas kernels: 121 us -> 118 us
  transfers between devices with their start and end apart: 58 -> 58, of which waited for: 24 -> 21; matrix products, arithmetic and copies ran while one was open for 0% -> 0% of each run, Pallas kernels for 45% -> 45%
where the time goes in v2:
time: 217 us
  Pallas kernels  118 us (54%)
  starting transfers between devices  50.1 us (23%)
  waiting for transfers between devices  35 us (16%)
  between operations  5.75 us (3%)
  other arithmetic  5.67 us (3%)
  local copies, waits for them, and re-layouts  2.69 us (1%)
    ppermute x58, starting transfers between devices, swap(): lax.ppermute(block, AXES, [(one, one ^ offset) for one in range(OWNERS)])  50.1 us
    pallas_call x3, Pallas kernels, attend_back_call(): pl.pallas_call(attend_back_kernel, grid_spec=pltpu.PrefetchScalarGridSpec...  36.8 us
    ppermute x58, waiting for transfers between devices, swap(): lax.ppermute(block, AXES, [(one, one ^ offset) for one in range(OWNERS)])  35 us
    pallas_call x2, Pallas kernels, attend_call(): pl.pallas_call(attend_kernel, grid_spec=pltpu.PrefetchScalarGridSpec(num_...  24.8 us
    pallas_call x1, Pallas kernels, dense_back_call(): pl.pallas_call(dense_back_kernel, grid_spec=pltpu.PrefetchScalarGridSpec(...  17.6 us
    pallas_call x1, Pallas kernels, dense_turn_call(): pl.pallas_call(dense_turn_kernel, grid_spec=pltpu.PrefetchScalarGridSpec(...  17.5 us
    pallas_call x1, Pallas kernels, dense_call(): pl.pallas_call(dense_kernel, grid_spec=pltpu.PrefetchScalarGridSpec(num_s...  9.35 us
    pallas_call x1, Pallas kernels, grad_x_call(): pl.pallas_call(grad_x_kernel, grid=(rows // ROW_BLOCK,), in_specs=[by_row...  5.88 us
  transfers between devices with their start and end apart: 58, of which 21 were waited for; matrix products, arithmetic and copies ran while one was open for 0% of the time, Pallas kernels for 45%

profile of v2, /device:TPU:0, one launch (start us, length us, event | category | flops | bytes accessed | tf_op | source)
XLA Modules:
  0.0 216.9 jit_solution(17747089753272051995)
XLA Ops:
  1.3 2.0 pack.1
  3.3 4.1 %collective-permute-start = (bf16[56,512]{1,0:T(8,128)(2,1)}, bf16[56,512]{1,0:T(8,128)(2,1)S(1)}, u32[]{:S(2)}, u32[]{:S(2)}) collective-permute-start(bf16[56,512]{1,0:T(8,128)(2,1)} %get-tuple-element.206.refs_0_), channel_id=1, source_target_pairs={{0,4},{1,5},{2,6},{3,7},{4,0},{5,1},{6,2},{7,3},{8,12},{9,13},{10,... | collective-permute-start | bytes 172040 | tf_op jit(solution)/shard_map/ppermute | solution.py:169
  7.3 1.6 collective-permute-start.1
  11.7 3.4 %collective-permute-done.2.refs_3_ = bf16[56,512]{1,0:T(8,128)(2,1)S(1)} collective-permute-done((bf16[56,512]{1,0:T(8,128)(2,1)}, bf16[56,512]{1,0:T(8,128)(2,1)S(1)}, u32[]{:S(2)}, u32[]{:S(2)}) %collective-permute-start.2) | collective-permute-done | bytes 57376 | tf_op jit(solution)/shard_map/ppermute | solution.py:169
  20.2 5.8 %collective-permute-done.10.refs_1_ = bf16[144,512]{1,0:T(8,128)(2,1)S(1)} collective-permute-done((bf16[144,512]{1,0:T(8,128)(2,1)}, bf16[144,512]{1,0:T(8,128)(2,1)S(1)}, u32[]{:S(2)}, u32[]{:S(2)}) %collective-permute-start.10) | collective-permute-done | bytes 147488 | tf_op jit(solution)/shard_map/ppermute | solution.py:169
  28.4 5.4 %collective-permute-done.11.refs_1_ = bf16[2,144,512]{2,1,0:T(8,128)(2,1)S(1)} collective-permute-done((bf16[2,144,512]{2,1,0:T(8,128)(2,1)S(1)}, bf16[2,144,512]{2,1,0:T(8,128)(2,1)S(1)}, u32[]{:S(2)}, u32[]{:S(2)}) %collective-permute-start.11) | collective-permute-done | bytes 294944 | tf_op jit(solution)/shard_map/ppermute | solution.py:169
  38.5 12.4 %attend.2 = (bf16[4,1024,384]{2,1,0:T(8,128)(2,1)}, bf16[4,896,1024]{2,1,0:T(8,128)(2,1)}, bf16[1024,512]{1,0:T(8,128)(2,1)}, bf16[4,512,384]{2,1,0:T(8,128)(2,1)}, f32[8,512]{1,0:T(8,128)}) custom-call(s32[1]{0:T(128)} %bitcast.place_ref, bf16[1024,512]{1,0:T(8,128)(2,1)} %bitcast.13, bf16[4,56,512]{2,1,0:T(8,128)(2,1)} %copy-done.5, ...), custom_call_target="tpu_custom_call" | custom-call | flops 3489660928 | bytes 16777216 | tf_op jit(solution)/shard_map/attend/pallas_call | solution.py:234
  57.2 2.0 collective-permute-start.24
  59.3 9.4 %dense.1 = (bf16[1024,512]{1,0:T(8,128)(2,1)}, f32[1024,512]{1,0:T(8,128)}, f32[1024,1]{1,0:T(8,128)}, bf16[1024,1024]{1,0:T(8,128)(2,1)}, f32[1024,1024]{1,0:T(...) custom-call(s32[1]{0:T(128)} %bitcast.place_ref, ...), custom_call_target="tpu_custom_call" | custom-call | flops 2684354560 | bytes 16777216 | tf_op jit(solution)/shard_map/dense/pallas_call | solution.py:456
  74.5 12.4 %attend.3 = (bf16[4,1024,384]{2,1,0:T(8,128)(2,1)}, bf16[4,896,1024]{2,1,0:T(8,128)(2,1)}, bf16[1024,512]{1,0:T(8,128)(2,1)}, bf16[4,512,384]{2,1,0:T(8,128)(2,1)}, f32[8,512]{1,0:T(8,128)}) custom-call(s32[1]{0:T(128)} %bitcast.place_ref, bf16[1024,512]{1,0:T(8,128)(2,1)} %get-tuple-element.246.x_ref, bf16[4,56,512]{2,1,0:T(8,128)(2,1)} %copy-done.24, ...), custom_call_target="tpu_custom_call" | custom-call | flops 3489660928 | bytes 16777216 | tf_op jit(solution)/shard_map/attend/pallas_call | solution.py:234
  87.0 3.5 %collective-permute-done.29.refs_2_ = bf16[4,88,512]{2,1,0:T(8,128)(2,1)S(1)} collective-permute-done((bf16[4,88,512]{2,1,0:T(8,128)(2,1)S(1)}, bf16[4,88,512]{2,1,0:T(8,128)(2,1)S(1)}, u32[]{:S(2)}, u32[]{:S(2)}) %collective-permute-start.29) | collective-permute-done | bytes 360480 | tf_op jit(solution)/shard_map/ppermute | solution.py:169
  94.0 17.5 %dense_turn.1 = (bf16[1024,512]{1,0:T(8,128)(2,1)}, bf16[1024,512]{1,0:T(8,128)(2,1)}, f32[1024,512]{1,0:T(8,128)}, bf16[16,88,512]{2,1,0:T(8,128)(2,1)}, bf16[16,88,512]{2,1,0:T(8,128)(2,1)}) custom-call(s32[1]{0:T(128)} %bitcast.place_ref, s32[1]{0:T(128)S(6)} %add.71.live_ref, s32[1]{0:T(128)S(6)} %copy.58.ids_ref, ...), custom_call_target="tpu_custom_call" | custom-call | flops 8053063680 | bytes 16777216 | tf_op jit(solution)/shard_map/dense_turn/pallas_call | solution.py:513
  111.7 16.7 %attend_back.3 = (bf16[16,56,512]{2,1,0:T(8,128)(2,1)}, bf16[16,56,512]{2,1,0:T(8,128)(2,1)}, bf16[4,1024,384]{2,1,0:T(8,128)(2,1)}) custom-call(s32[1]{0:T(128)} %bitcast.place_ref, bf16[1024,512]{1,0:T(8,128)(2,1)} %get-tuple-element.246.x_ref, bf16[4,1024,384]{2,1,0:T(8,128)(2,1)} %get-tuple-element.264.joint_ref, ...), custom_call_target="tpu_custom_call" | custom-call | flops 5368709120 | bytes 16777216 | tf_op jit(solution)/shard_map/attend_back/pallas_call | solution.py:587
  133.4 17.6 %dense_back.1 = (bf16[1024,512]{1,0:T(8,128)(2,1)}, f32[1024,512]{1,0:T(8,128)}, bf16[16,88,512]{2,1,0:T(8,128)(2,1)}, bf16[16,88,512]{2,1,0:T(8,128)(2,1)}) custom-call(s32[1]{0:T(128)} %bitcast.place_ref, f32[1024,512]{1,0:T(8,128)} %get-tuple-element.281.grad_one_next, bf16[4,1024,384]{2,1,0:T(8,128)(2,1)} %get-tuple-element.282.grad_joint_next, ...), custom_call_target="tpu_custom_call" | custom-call | flops 6979321856 | bytes 20971520 | tf_op jit(solution)/shard_map/dense_back/pallas_call | solution.py:486
  157.0 10.1 %attend_back.4 = (bf16[16,56,512]{2,1,0:T(8,128)(2,1)}, bf16[16,56,512]{2,1,0:T(8,128)(2,1)}, bf16[4,1024,384]{2,1,0:T(8,128)(2,1)}) custom-call(s32[1]{0:T(128)} %bitcast.place_ref, bf16[1024,512]{1,0:T(8,128)(2,1)} %bitcast.15, bf16[4,1024,384]{2,1,0:T(8,128)(2,1)} %get-tuple-element.262.joint_ref, bf16[4,896,1024]{2,1,0:T(8,128)(2,1)} %get-tuple-element.263.probs_ref, ...), custom_call_target="tpu_custom_call" | custom-call | flops 2684354560 | bytes 8388608 | tf_op jit(solution)/shard_map/attend_back/pallas_call | solution.py:587
  167.2 2.5 %add_convert_fusion = (bf16[4,88,512]{2,1,0:T(8,128)(2,1)S(1)}, bf16[4,88,512]{2,1,0:T(8,128)(2,1)S(1)}, bf16[4,88,512]{2,1,0:T(8,128)(2,1)}, bf16[4,88,512]{2,1,0:T(8,128)(2,1)S(1)}) fusion(bf16[16,88,512]{2,1,0:T(8,128)(2,1)} %collective-permute-done.40, bf16[16,88,512]{2,1,0:T(8,128)(2,1)S(1)} %copy-done.26), kind=kLoop, calls=%fused_computation | loop fusion | flops 2883584 | bytes 4325376 | tf_op jit(solution)/shard_map/convert_element_type | solution.py:133
  174.7 10.1 %attend_back.5 = (bf16[16,56,512]{2,1,0:T(8,128)(2,1)}, bf16[16,56,512]{2,1,0:T(8,128)(2,1)}, bf16[4,1024,384]{2,1,0:T(8,128)(2,1)}) custom-call(s32[1]{0:T(128)} %bitcast.place_ref, bf16[1024,512]{1,0:T(8,128)(2,1)} %bitcast.16, bf16[4,1024,384]{2,1,0:T(8,128)(2,1)} %get-tuple-element.262.joint_ref, ...), custom_call_target="tpu_custom_call", output_to_operand_aliasing={{0}: (5, {}), {1}: (6, {}), {2}: (7, {})} | custom-call | flops 2684354560 | bytes 8388608 | tf_op jit(solution)/shard_map/attend_back/pallas_call | solution.py:587
  184.8 2.0 collective-permute-done.46.refs_6_
  188.4 2.4 %collective-permute-done.49 = bf16[16,56,512]{2,1,0:T(8,128)(2,1)S(1)} collective-permute-done((bf16[16,56,512]{2,1,0:T(8,128)(2,1)}, bf16[16,56,512]{2,1,0:T(8,128)(2,1)S(1)}, u32[]{:S(2)}, u32[]{:S(2)}) %collective-permute-start.49) | collective-permute-done | bytes 917536 | tf_op jit(solution)/shard_map/ppermute | solution.py:169
  191.0 1.8 collective-permute-start.50
  196.4 5.9 %grad_x.1 = f32[1024,512]{1,0:T(8,128)} custom-call(f32[1024,512]{1,0:T(8,128)} %get-tuple-element.345.grad_one_ref, bf16[4,1024,384]{2,1,0:T(8,128)(2,1)} %get-tuple-element.346.grad_joint_ref, bf16[4,512,384]{2,1,0:T(8,128)(2,1)} %get-tuple-element.347.weight_ref), custom_call_target="tpu_custom_call" | custom-call | flops 1610612736 | bytes 10485760 | tf_op jit(solution)/shard_map/grad_x/pallas_call | solution.py:621
  205.6 2.7 %collective-permute-start.55 = (bf16[56,512]{1,0:T(8,128)(2,1)S(1)}, bf16[56,512]{1,0:T(8,128)(2,1)S(1)}, u32[]{:S(2)}, u32[]{:S(2)}) collective-permute-start(bf16[56,512]{1,0:T(8,128)(2,1)S(1)} %get-tuple-element.359), channel_id=1, source_target_pairs={{0,4},{1,5},{2,6},{3,7},{4,0},{5,1},{6,2},{7,3},{8,12},{9,13},{10,... | collective-permute-start | bytes 172040 | tf_op jit(solution)/shard_map/ppermute | solution.py:169
  210.1 3.2 %collective-permute-done.51.refs_1_ = bf16[144,512]{1,0:T(8,128)(2,1)S(1)} collective-permute-done((bf16[144,512]{1,0:T(8,128)(2,1)S(1)}, bf16[144,512]{1,0:T(8,128)(2,1)S(1)}, u32[]{:S(2)}, u32[]{:S(2)}) %collective-permute-start.51) | collective-permute-done | bytes 147488 | tf_op jit(solution)/shard_map/ppermute | solution.py:169
  213.4 1.6 second_step.1
  (233 shorter events, 55.3 us)
Async XLA Ops:
  33.9 17.0 %collective-permute-start.12 = (bf16[4,88,512]{2,1,0:T(8,128)(2,1)S(1)}, bf16[4,88,512]{2,1,0:T(8,128)(2,1)S(1)}, u32[]{:S(2)}, u32[]{:S(2)}) collective-permute-start(bf16[4,88,512]{2,1,0:T(8,128)(2,1)S(1)} %get-tuple-element.231.refs_0_), channel_id=1, source_target_pairs={{0,1},{1,0},{2,3},{3,2},{4,5},{5,4},{6,7},{7,6},{8,9},{9,8},{10,11... | collective-permute-start | bytes 1081352 | tf_op jit(solution)/shard_map/ppermute | solution.py:169
  35.5 15.4 %collective-permute-start.13 = (bf16[4,88,512]{2,1,0:T(8,128)(2,1)S(1)}, bf16[4,88,512]{2,1,0:T(8,128)(2,1)S(1)}, u32[]{:S(2)}, u32[]{:S(2)}) collective-permute-start(bf16[4,88,512]{2,1,0:T(8,128)(2,1)S(1)} %get-tuple-element.231.refs_0_), channel_id=1, source_target_pairs={{0,16},{1,17},{2,18},{3,19},{4,20},{5,21},{6,22},{7,23},{8,24},{9,... | collective-permute-start | bytes 1081352 | tf_op jit(solution)/shard_map/ppermute | solution.py:169
  37.0 13.9 %collective-permute-start.14 = (bf16[4,88,512]{2,1,0:T(8,128)(2,1)S(1)}, bf16[4,88,512]{2,1,0:T(8,128)(2,1)S(1)}, u32[]{:S(2)}, u32[]{:S(2)}) collective-permute-start(bf16[4,88,512]{2,1,0:T(8,128)(2,1)S(1)} %get-tuple-element.231.refs_0_), channel_id=1, source_target_pairs={{0,17},{1,16},{2,19},{3,18},{4,21},{5,20},{6,23},{7,22},{8,25},{9,... | collective-permute-start | bytes 1081352 | tf_op jit(solution)/shard_map/ppermute | solution.py:169
  37.5 13.5 %collective-permute-start.15 = (bf16[4,88,512]{2,1,0:T(8,128)(2,1)S(1)}, bf16[4,88,512]{2,1,0:T(8,128)(2,1)S(1)}, u32[]{:S(2)}, u32[]{:S(2)}) collective-permute-start(bf16[4,88,512]{2,1,0:T(8,128)(2,1)S(1)} %get-tuple-element.231.refs_0_), channel_id=1, source_target_pairs={{0,8},{1,9},{2,10},{3,11},{4,12},{5,13},{6,14},{7,15},{8,0},{9,1},... | collective-permute-start | bytes 1081352 | tf_op jit(solution)/shard_map/ppermute | solution.py:169
  37.5 13.4 %collective-permute-start.16 = (bf16[88,512]{1,0:T(8,128)(2,1)}, bf16[88,512]{1,0:T(8,128)(2,1)S(1)}, u32[]{:S(2)}, u32[]{:S(2)}) collective-permute-start(bf16[88,512]{1,0:T(8,128)(2,1)} %get-tuple-element.227.refs_0_), channel_id=1, source_target_pairs={{0,4},{1,5},{2,6},{3,7},{4,0},{5,1},{6,2},{7,3},{8,12},{9,13},{10,... | collective-permute-start | bytes 270344 | tf_op jit(solution)/shard_map/ppermute | solution.py:169
  53.7 14.9 %collective-permute-start.20 = (bf16[4,56,512]{2,1,0:T(8,128)(2,1)S(1)}, bf16[4,56,512]{2,1,0:T(8,128)(2,1)S(1)}, u32[]{:S(2)}, u32[]{:S(2)}) collective-permute-start(bf16[4,56,512]{2,1,0:T(8,128)(2,1)S(1)} %get-tuple-element.247.refs_0_), channel_id=1, source_target_pairs={{0,1},{1,0},{2,3},{3,2},{4,5},{5,4},{6,7},{7,6},{8,9},{9,8},{10,11... | collective-permute-start | bytes 688136 | tf_op jit(solution)/shard_map/ppermute | solution.py:169
  55.2 13.5 %collective-permute-start.21 = (bf16[4,56,512]{2,1,0:T(8,128)(2,1)S(1)}, bf16[4,56,512]{2,1,0:T(8,128)(2,1)S(1)}, u32[]{:S(2)}, u32[]{:S(2)}) collective-permute-start(bf16[4,56,512]{2,1,0:T(8,128)(2,1)S(1)} %get-tuple-element.247.refs_0_), channel_id=1, source_target_pairs={{0,16},{1,17},{2,18},{3,19},{4,20},{5,21},{6,22},{7,23},{8,24},{9,... | collective-permute-start | bytes 688136 | tf_op jit(solution)/shard_map/ppermute | solution.py:169
  71.0 16.0 %collective-permute-start.28 = (bf16[4,88,512]{2,1,0:T(8,128)(2,1)S(1)}, bf16[4,88,512]{2,1,0:T(8,128)(2,1)S(1)}, u32[]{:S(2)}, u32[]{:S(2)}) collective-permute-start(bf16[4,88,512]{2,1,0:T(8,128)(2,1)S(1)} %join.9.refs_0_), channel_id=1, source_target_pairs={{0,1},{1,0},{2,3},{3,2},{4,5},{5,4},{6,7},{7,6},{8,9},{9,8},{10,11... | collective-permute-start | bytes 1081352 | tf_op jit(solution)/shard_map/ppermute | solution.py:169
  72.5 18.0 %collective-permute-start.29 = (bf16[4,88,512]{2,1,0:T(8,128)(2,1)S(1)}, bf16[4,88,512]{2,1,0:T(8,128)(2,1)S(1)}, u32[]{:S(2)}, u32[]{:S(2)}) collective-permute-start(bf16[4,88,512]{2,1,0:T(8,128)(2,1)S(1)} %join.9.refs_0_), channel_id=1, source_target_pairs={{0,16},{1,17},{2,18},{3,19},{4,20},{5,21},{6,22},{7,23},{8,24},{9,... | collective-permute-start | bytes 1081352 | tf_op jit(solution)/shard_map/ppermute | solution.py:169
  74.0 16.5 %collective-permute-start.30 = (bf16[4,88,512]{2,1,0:T(8,128)(2,1)S(1)}, bf16[4,88,512]{2,1,0:T(8,128)(2,1)S(1)}, u32[]{:S(2)}, u32[]{:S(2)}) collective-permute-start(bf16[4,88,512]{2,1,0:T(8,128)(2,1)S(1)} %join.9.refs_0_), channel_id=1, source_target_pairs={{0,17},{1,16},{2,19},{3,18},{4,21},{5,20},{6,23},{7,22},{8,25},{9,... | collective-permute-start | bytes 1081352 | tf_op jit(solution)/shard_map/ppermute | solution.py:169
  74.5 16.0 %collective-permute-start.31 = (bf16[4,88,512]{2,1,0:T(8,128)(2,1)S(1)}, bf16[4,88,512]{2,1,0:T(8,128)(2,1)S(1)}, u32[]{:S(2)}, u32[]{:S(2)}) collective-permute-start(bf16[4,88,512]{2,1,0:T(8,128)(2,1)S(1)} %join.9.refs_0_), channel_id=1, source_target_pairs={{0,8},{1,9},{2,10},{3,11},{4,12},{5,13},{6,14},{7,15},{8,0},{9,1},... | collective-permute-start | bytes 1081352 | tf_op jit(solution)/shard_map/ppermute | solution.py:169
  111.5 16.9 %collective-permute-start.35 = (bf16[16,88,512]{2,1,0:T(8,128)(2,1)}, bf16[16,88,512]{2,1,0:T(8,128)(2,1)S(1)}, u32[]{:S(2)}, u32[]{:S(2)}) collective-permute-start(bf16[16,88,512]{2,1,0:T(8,128)(2,1)} %get-tuple-element.271), channel_id=1, source_target_pairs={{0,8},{1,9},{2,10},{3,11},{4,12},{5,13},{6,14},{7,15},{8,0},{9,1},... | collective-permute-start | bytes 4325384 | tf_op jit(solution)/shard_map/ppermute | solution.py:169
  129.6 21.5 %collective-permute-start.36 = (bf16[16,56,512]{2,1,0:T(8,128)(2,1)}, bf16[16,56,512]{2,1,0:T(8,128)(2,1)}, u32[]{:S(2)}, u32[]{:S(2)}) collective-permute-start(bf16[16,56,512]{2,1,0:T(8,128)(2,1)} %get-tuple-element.277), channel_id=1, source_target_pairs={{0,8},{1,9},{2,10},{3,11},{4,12},{5,13},{6,14},{7,15},{8,0},{9,1},... | collective-permute-start | bytes 2752520 | tf_op jit(solution)/shard_map/ppermute | solution.py:169
  129.9 21.1 %collective-permute-start.37 = (bf16[4,88,512]{2,1,0:T(8,128)(2,1)}, bf16[4,88,512]{2,1,0:T(8,128)(2,1)S(1)}, u32[]{:S(2)}, u32[]{:S(2)}) collective-permute-start(bf16[4,88,512]{2,1,0:T(8,128)(2,1)} %get-tuple-element.278), channel_id=1, source_target_pairs={{0,1},{1,0},{2,3},{3,2},{4,5},{5,4},{6,7},{7,6},{8,9},{9,8},{10,11... | collective-permute-start | bytes 1081352 | tf_op jit(solution)/shard_map/ppermute | solution.py:169
  131.1 19.9 %collective-permute-start.38 = (bf16[4,88,512]{2,1,0:T(8,128)(2,1)S(1)}, bf16[4,88,512]{2,1,0:T(8,128)(2,1)S(1)}, u32[]{:S(2)}, u32[]{:S(2)}) collective-permute-start(bf16[4,88,512]{2,1,0:T(8,128)(2,1)S(1)} %get-tuple-element.279), channel_id=1, source_target_pairs={{0,16},{1,17},{2,18},{3,19},{4,20},{5,21},{6,22},{7,23},{8,24},{9,... | collective-permute-start | bytes 1081352 | tf_op jit(solution)/shard_map/ppermute | solution.py:169
  132.0 19.1 %collective-permute-start.39 = (bf16[4,88,512]{2,1,0:T(8,128)(2,1)S(1)}, bf16[4,88,512]{2,1,0:T(8,128)(2,1)S(1)}, u32[]{:S(2)}, u32[]{:S(2)}) collective-permute-start(bf16[4,88,512]{2,1,0:T(8,128)(2,1)S(1)} %get-tuple-element.280), channel_id=1, source_target_pairs={{0,17},{1,16},{2,19},{3,18},{4,21},{5,20},{6,23},{7,22},{8,25},{9,... | collective-permute-start | bytes 1081352 | tf_op jit(solution)/shard_map/ppermute | solution.py:169
  152.8 14.4 %collective-permute-start.40 = (bf16[16,88,512]{2,1,0:T(8,128)(2,1)}, bf16[16,88,512]{2,1,0:T(8,128)(2,1)}, u32[]{:S(2)}, u32[]{:S(2)}) collective-permute-start(bf16[16,88,512]{2,1,0:T(8,128)(2,1)} %get-tuple-element.307), channel_id=1, source_target_pairs={{0,8},{1,9},{2,10},{3,11},{4,12},{5,13},{6,14},{7,15},{8,0},{9,1},... | collective-permute-start | bytes 4325384 | tf_op jit(solution)/shard_map/ppermute | solution.py:169
  152.9 14.3 %collective-permute-start.41 = (bf16[4,56,512]{2,1,0:T(8,128)(2,1)S(1)}, bf16[4,56,512]{2,1,0:T(8,128)(2,1)S(1)}, u32[]{:S(2)}, u32[]{:S(2)}) collective-permute-start(bf16[4,56,512]{2,1,0:T(8,128)(2,1)S(1)} %get-tuple-element.308), channel_id=1, source_target_pairs={{0,1},{1,0},{2,3},{3,2},{4,5},{5,4},{6,7},{7,6},{8,9},{9,8},{10,11... | collective-permute-start | bytes 688136 | tf_op jit(solution)/shard_map/ppermute | solution.py:169
  154.2 13.0 %collective-permute-start.42 = (bf16[4,56,512]{2,1,0:T(8,128)(2,1)S(1)}, bf16[4,56,512]{2,1,0:T(8,128)(2,1)S(1)}, u32[]{:S(2)}, u32[]{:S(2)}) collective-permute-start(bf16[4,56,512]{2,1,0:T(8,128)(2,1)S(1)} %get-tuple-element.309), channel_id=1, source_target_pairs={{0,16},{1,17},{2,18},{3,19},{4,20},{5,21},{6,22},{7,23},{8,24},{9,... | collective-permute-start | bytes 688136 | tf_op jit(solution)/shard_map/ppermute | solution.py:169
  155.0 12.2 %collective-permute-start.43 = (bf16[4,56,512]{2,1,0:T(8,128)(2,1)S(1)}, bf16[4,56,512]{2,1,0:T(8,128)(2,1)S(1)}, u32[]{:S(2)}, u32[]{:S(2)}) collective-permute-start(bf16[4,56,512]{2,1,0:T(8,128)(2,1)S(1)} %get-tuple-element.310), channel_id=1, source_target_pairs={{0,17},{1,16},{2,19},{3,18},{4,21},{5,20},{6,23},{7,22},{8,25},{9,... | collective-permute-start | bytes 688136 | tf_op jit(solution)/shard_map/ppermute | solution.py:169
  169.7 15.1 %collective-permute-start.45 = (bf16[4,88,512]{2,1,0:T(8,128)(2,1)}, bf16[4,88,512]{2,1,0:T(8,128)(2,1)S(1)}, u32[]{:S(2)}, u32[]{:S(2)}) collective-permute-start(bf16[4,88,512]{2,1,0:T(8,128)(2,1)} %get-tuple-element.325), channel_id=1, source_target_pairs={{0,1},{1,0},{2,3},{3,2},{4,5},{5,4},{6,7},{7,6},{8,9},{9,8},{10,11... | collective-permute-start | bytes 1081352 | tf_op jit(solution)/shard_map/ppermute | solution.py:169
  170.8 16.0 %collective-permute-start.46 = (bf16[4,88,512]{2,1,0:T(8,128)(2,1)S(1)}, bf16[4,88,512]{2,1,0:T(8,128)(2,1)S(1)}, u32[]{:S(2)}, u32[]{:S(2)}) collective-permute-start(bf16[4,88,512]{2,1,0:T(8,128)(2,1)S(1)} %get-tuple-element.326), channel_id=1, source_target_pairs={{0,16},{1,17},{2,18},{3,19},{4,20},{5,21},{6,22},{7,23},{8,24},{9,... | collective-permute-start | bytes 1081352 | tf_op jit(solution)/shard_map/ppermute | solution.py:169
  172.1 15.9 %collective-permute-start.47 = (bf16[4,88,512]{2,1,0:T(8,128)(2,1)S(1)}, bf16[4,88,512]{2,1,0:T(8,128)(2,1)S(1)}, u32[]{:S(2)}, u32[]{:S(2)}) collective-permute-start(bf16[4,88,512]{2,1,0:T(8,128)(2,1)S(1)} %get-tuple-element.327), channel_id=1, source_target_pairs={{0,17},{1,16},{2,19},{3,18},{4,21},{5,20},{6,23},{7,22},{8,25},{9,... | collective-permute-start | bytes 1081352 | tf_op jit(solution)/shard_map/ppermute | solution.py:169
  192.8 12.6 %collective-permute-start.52 = (bf16[4,56,512]{2,1,0:T(8,128)(2,1)S(1)}, bf16[4,56,512]{2,1,0:T(8,128)(2,1)S(1)}, u32[]{:S(2)}, u32[]{:S(2)}) collective-permute-start(bf16[4,56,512]{2,1,0:T(8,128)(2,1)S(1)} %get-tuple-element.355), channel_id=1, source_target_pairs={{0,1},{1,0},{2,3},{3,2},{4,5},{5,4},{6,7},{7,6},{8,9},{9,8},{10,11... | collective-permute-start | bytes 688136 | tf_op jit(solution)/shard_map/ppermute | solution.py:169
  (91 other events, 805.2 us)

commit v3 on v2

--- a/solution.py
+++ b/solution.py
@@ -133,6 +133,27 @@
         (kept[at : at + 4].astype(FLOAT) + got[at : at + 4].astype(FLOAT)).astype(HALF)
         for at in range(0, 16, 4)
     ]
+
+
+def core_sums_kernel(*refs):
+    *sources, one, two, three, four = refs
+    for to, out in enumerate((one, two, three, four)):
+        start = 0
+        for at in range(0, len(sources), 2):
+            kept, got = (ref[4 * to : 4 * to + 4].astype(FLOAT) for ref in sources[at : at + 2])
+            out[:, start : start + kept.shape[1], :] = (kept + got).astype(HALF)
+            start += kept.shape[1]
+
+
+def core_sums_call(*pieces):
+    rows = sum(piece.shape[1] for piece in pieces[::2])
+    return pl.pallas_call(
+        core_sums_kernel,
+        out_shape=[LIKE((4, rows, pieces[0].shape[2]), HALF)] * 4,
+        compiler_params=params(SMALL_LIMIT),
+        cost_estimate=pl.CostEstimate(flops=0, bytes_accessed=1 << 22, transcendentals=0),
+        name="core_sums",
+    )(*pieces)
 
 
 def square_sum_kernel(rows, *refs):
@@ -535,8 +556,8 @@
     )(place, live, ids, x, mixed, *slots, small, cotangent)
 
 
-def attend_back_kernel(place_ref, x_ref, joint_ref, probs_ref, grad_mixed_ref, *refs):
-    kept_ref, sent_ref, grad_joint_ref, grad_scores, small = refs[-5:]
+def attend_back_kernel(place_ref, x_ref, joint_ref, probs_ref, grad_mixed_ref, kept_ref, sent_ref,
+                       grad_joint_ref, grad_scores, small):
     grad_joint = grad_joint_ref.at[0]
     rows = x_ref.shape[0]
     head_size = grad_mixed_ref.shape[1]
@@ -581,35 +602,33 @@
         slots_ref[at, 48:56, :] = small_low
 
 
-def attend_back_call(place, x, joint, probs, grad_mixed, base=0, heads=HEADS, before=()):
+def attend_back_call(place, x, joint, probs, grad_mixed):
     rows, width = x.shape
     head_size = width // HEADS
     return pl.pallas_call(
         attend_back_kernel,
         grid_spec=pltpu.PrefetchScalarGridSpec(
             num_scalar_prefetch=1,
-            grid=(heads,),
+            grid=(HEADS,),
             in_specs=[
                 pl.BlockSpec((rows, width), lambda h, p: (0, 0)),
-                pl.BlockSpec((1, rows, 3 * head_size), lambda h, p: (h + base, 0, 0)),
-                pl.BlockSpec((1, CTX, rows), lambda h, p: (h + base, 0, 0)),
-                pl.BlockSpec((rows, head_size), lambda h, p: (0, h + base)),
-            ]
-            + [pl.BlockSpec(memory_space=pl.ANY)] * len(before),
-            out_specs=[pl.BlockSpec((16, FIRST_ROWS, head_size), lambda h, p: (0, 0, h + base))] * 2
-            + [pl.BlockSpec((1, rows, 3 * head_size), lambda h, p: (h + base, 0, 0))],
+                pl.BlockSpec((1, rows, 3 * head_size), lambda h, p: (h, 0, 0)),
+                pl.BlockSpec((1, CTX, rows), lambda h, p: (h, 0, 0)),
+                pl.BlockSpec((rows, head_size), lambda h, p: (0, h)),
+            ],
+            out_specs=[pl.BlockSpec((16, FIRST_ROWS, head_size), lambda h, p: (0, 0, h))] * 2
+            + [pl.BlockSpec((1, rows, 3 * head_size), lambda h, p: (h, 0, 0))],
             scratch_shapes=[pltpu.VMEM((CTX, rows), HALF), pltpu.VMEM((8, head_size), FLOAT)],
         ),
         out_shape=[LIKE((16, FIRST_ROWS, width), HALF)] * 2
         + [LIKE((HEADS, rows, 3 * head_size), HALF)],
-        input_output_aliases={5 + at: at for at in range(len(before))},
         compiler_params=params(),
         cost_estimate=pl.CostEstimate(
-            flops=heads * (6 * rows * width * head_size + 8 * rows * CTX * head_size),
-            bytes_accessed=heads * 4 * 1024 * 1024, transcendentals=0,
+            flops=HEADS * (6 * rows * width * head_size + 8 * rows * CTX * head_size),
+            bytes_accessed=HEADS * 4 * 1024 * 1024, transcendentals=0,
         ),
         name="attend_back",
-    )(place, x, joint, probs, grad_mixed, *before)
+    )(place, x, joint, probs, grad_mixed)
 
 
 def grad_x_kernel(grad_one_ref, grad_joint_ref, weight_ref, grad_x_ref):
@@ -814,7 +833,6 @@
 
 def one_per_owner(place, x, cotangent, dataset_ids, live, masters, moments, averages, rates):
     width = x.shape[1]
-    pair = HEADS // 2
 
     def to_core(stacks):
         return [swap(one, CORE) for one in stacks]
@@ -892,39 +910,25 @@
     )
 
     got, late_got, sent, grad_mixed = sync(got, late_got, sent, grad_mixed)
-    first_stacks = core_sum(next_kept, got)
     late_kept, late_sent = square_sum_call([late_stacks[0], *late_got])
-    first_stacks, late_kept, late_sent, sent, grad_mixed = sync(
-        first_stacks, late_kept, late_sent, sent, grad_mixed
-    )
-    first_got = square_back(first_stacks)
+    stacks = core_sums_call(next_kept, got, kept, swap(sent, CORE))
+    stacks, late_kept, late_sent, grad_mixed = sync(stacks, late_kept, late_sent, grad_mixed)
+    middle_got = square_back(stacks)
+    late_got = swap(late_sent, CHAIN[2])
+    kept, sent, grad_joint = attend_back_call(place, x, joint, probs, grad_mixed)
+    grad_rows = grad_x_call(grad_one, grad_joint, weight)
+
+    middle_got, late_got, sent, grad_rows = sync(middle_got, late_got, sent, grad_rows)
     got = swap(sent, CORE)
-    late_got = swap(late_sent, CHAIN[2])
-    before = attend_back_call(place, x, joint, probs, grad_mixed, 0, pair)
-
-    got, first_got, late_got, before = sync(got, first_got, late_got, before)
-    second_stacks = core_sum(kept, got)
     late_own, late_sent = pair_sum(late_kept, late_got)
-    second_stacks, before, late_sent = sync(second_stacks, before, late_sent)
-    second_got = square_back(second_stacks)
-    late_got = swap(late_sent, CHAIN[1])
-    kept, sent, grad_joint = attend_back_call(
-        place, x, joint, probs, grad_mixed, pair, HEADS - pair, before
-    )
-
-    second_got, sent, grad_joint, late_got = sync(second_got, sent, grad_joint, late_got)
-    got = swap(sent, CORE)
-    middle_kept, middle_sent = square_sum_call(
-        [first_stacks[0], *first_got], [second_stacks[0], *second_got]
-    )
-    got, middle_sent = sync(got, middle_sent)
+    middle_kept, middle_sent = square_sum_call([stacks[0], *middle_got])
+    got, middle_sent, late_sent = sync(got, middle_sent, late_sent)
     stacks = core_sum(kept, got)
-    stacks, middle_sent, grad_joint = sync(stacks, middle_sent, grad_joint)
+    stacks, middle_sent, late_sent = sync(stacks, middle_sent, late_sent)
     got = square_back(stacks)
     middle_got = swap(middle_sent, CHAIN[2])
-    grad_rows = grad_x_call(grad_one, grad_joint, weight)
-
-    middle_got, grad_rows = sync(middle_got, grad_rows)
+    late_got = swap(late_sent, CHAIN[1])
+    middle_got, late_got = sync(middle_got, late_got)
     middle_own, middle_sent = pair_sum(middle_kept, middle_got)
     middle_got = swap(middle_sent, CHAIN[1])
 

time: 217 us -> 215 us (level)
  waiting for transfers between devices: 35 us -> 42 us
  other arithmetic: 5.67 us -> 1.63 us
  starting transfers between devices: 50.1 us -> 46.1 us
    ppermute x58 -> x55, waiting for transfers between devices: 35 us -> 42 us  [swap(): lax.ppermute(block, AXES, [(one, one ^ offset) for one in range(OWNERS)])]
    convert_element_type x4 -> x2, other arithmetic: 5.47 us -> 1.43 us  [core_sum(): (kept[at:at + 4].astype(FLOAT) + got[at:at + 4].astype(FLOAT)).astype(HALF)]
    ppermute x58 -> x55, starting transfers between devices: 50.1 us -> 46.1 us  [swap(): lax.ppermute(block, AXES, [(one, one ^ offset) for one in range(OWNERS)])]
    pallas_call x3 -> x2, Pallas kernels: 36.8 us -> 33.2 us  [attend_back_call(): pl.pallas_call(attend_back_kernel, grid_spec=pltpu.PrefetchScalarGridSpec...]
  transfers between devices with their start and end apart: 58 -> 55, of which waited for: 21 -> 25; matrix products, arithmetic and copies ran while one was open for 0% -> 0% of each run, Pallas kernels for 45% -> 44%
where the time goes in v3:
time: 215 us; the launch traced here: 214 us
  Pallas kernels  116 us (54%)
  starting transfers between devices  46.1 us (21%)
  waiting for transfers between devices  42 us (20%)
  between operations  5.67 us (3%)
  local copies, waits for them, and re-layouts  2.9 us (1%)
    ppermute x55, starting transfers between devices, swap(): lax.ppermute(block, AXES, [(one, one ^ offset) for one in range(OWNERS)])  46.1 us
    ppermute x55, waiting for transfers between devices, swap(): lax.ppermute(block, AXES, [(one, one ^ offset) for one in range(OWNERS)])  42 us
    pallas_call x2, Pallas kernels, attend_back_call(): pl.pallas_call(attend_back_kernel, grid_spec=pltpu.PrefetchScalarGridSpec...  33.2 us
    pallas_call x2, Pallas kernels, attend_call(): pl.pallas_call(attend_kernel, grid_spec=pltpu.PrefetchScalarGridSpec(num_...  24.8 us
    pallas_call x1, Pallas kernels, dense_back_call(): pl.pallas_call(dense_back_kernel, grid_spec=pltpu.PrefetchScalarGridSpec(...  17.6 us
    pallas_call x1, Pallas kernels, dense_turn_call(): pl.pallas_call(dense_turn_kernel, grid_spec=pltpu.PrefetchScalarGridSpec(...  17.5 us
    pallas_call x1, Pallas kernels, dense_call(): pl.pallas_call(dense_kernel, grid_spec=pltpu.PrefetchScalarGridSpec(num_s...  9.38 us
    pallas_call x1, Pallas kernels, grad_x_call(): pl.pallas_call(grad_x_kernel, grid=(rows // ROW_BLOCK,), in_specs=[by_row...  5.77 us
  transfers between devices with their start and end apart: 55, of which 25 were waited for; matrix products, arithmetic and copies ran while one was open for 0% of the time, Pallas kernels for 44%

profile of v3, /device:TPU:0, one launch (start us, length us, event | category | flops | bytes accessed | tf_op | source)
XLA Modules:
  0.0 214.5 jit_solution(8258507708554622068)
XLA Ops:
  1.3 2.0 pack.1
  3.3 4.1 %collective-permute-start = (bf16[56,512]{1,0:T(8,128)(2,1)}, bf16[56,512]{1,0:T(8,128)(2,1)S(1)}, u32[]{:S(2)}, u32[]{:S(2)}) collective-permute-start(bf16[56,512]{1,0:T(8,128)(2,1)} %get-tuple-element.191.refs_0_), channel_id=1, source_target_pairs={{0,4},{1,5},{2,6},{3,7},{4,0},{5,1},{6,2},{7,3},{8,12},{9,13},{10,... | collective-permute-start | bytes 172040 | tf_op jit(solution)/shard_map/ppermute | solution.py:190
  11.7 3.4 %collective-permute-done.2.refs_3_ = bf16[56,512]{1,0:T(8,128)(2,1)S(1)} collective-permute-done((bf16[56,512]{1,0:T(8,128)(2,1)}, bf16[56,512]{1,0:T(8,128)(2,1)S(1)}, u32[]{:S(2)}, u32[]{:S(2)}) %collective-permute-start.2) | collective-permute-done | bytes 57376 | tf_op jit(solution)/shard_map/ppermute | solution.py:190
  20.2 5.8 %collective-permute-done.10.refs_1_ = bf16[144,512]{1,0:T(8,128)(2,1)S(1)} collective-permute-done((bf16[144,512]{1,0:T(8,128)(2,1)}, bf16[144,512]{1,0:T(8,128)(2,1)S(1)}, u32[]{:S(2)}, u32[]{:S(2)}) %collective-permute-start.10) | collective-permute-done | bytes 147488 | tf_op jit(solution)/shard_map/ppermute | solution.py:190
  28.4 5.4 %collective-permute-done.11.refs_1_ = bf16[2,144,512]{2,1,0:T(8,128)(2,1)S(1)} collective-permute-done((bf16[2,144,512]{2,1,0:T(8,128)(2,1)S(1)}, bf16[2,144,512]{2,1,0:T(8,128)(2,1)S(1)}, u32[]{:S(2)}, u32[]{:S(2)}) %collective-permute-start.11) | collective-permute-done | bytes 294944 | tf_op jit(solution)/shard_map/ppermute | solution.py:190
  38.5 12.4 %attend.2 = (bf16[4,1024,384]{2,1,0:T(8,128)(2,1)}, bf16[4,896,1024]{2,1,0:T(8,128)(2,1)}, bf16[1024,512]{1,0:T(8,128)(2,1)}, bf16[4,512,384]{2,1,0:T(8,128)(2,1)}, f32[8,512]{1,0:T(8,128)}) custom-call(s32[1]{0:T(128)} %bitcast.place_ref, bf16[1024,512]{1,0:T(8,128)(2,1)} %bitcast.15, bf16[4,56,512]{2,1,0:T(8,128)(2,1)} %copy-done.7, ...), custom_call_target="tpu_custom_call" | custom-call | flops 3489660928 | bytes 16777216 | tf_op jit(solution)/shard_map/attend/pallas_call | solution.py:255
  57.2 2.0 collective-permute-start.24
  59.3 9.4 %dense.1 = (bf16[1024,512]{1,0:T(8,128)(2,1)}, f32[1024,512]{1,0:T(8,128)}, f32[1024,1]{1,0:T(8,128)}, bf16[1024,1024]{1,0:T(8,128)(2,1)}, f32[1024,1024]{1,0:T(...) custom-call(s32[1]{0:T(128)} %bitcast.place_ref, ...), custom_call_target="tpu_custom_call" | custom-call | flops 2684354560 | bytes 16777216 | tf_op jit(solution)/shard_map/dense/pallas_call | solution.py:477
  74.8 12.4 %attend.3 = (bf16[4,1024,384]{2,1,0:T(8,128)(2,1)}, bf16[4,896,1024]{2,1,0:T(8,128)(2,1)}, bf16[1024,512]{1,0:T(8,128)(2,1)}, bf16[4,512,384]{2,1,0:T(8,128)(2,1)}, f32[8,512]{1,0:T(8,128)}) custom-call(s32[1]{0:T(128)} %bitcast.place_ref, bf16[1024,512]{1,0:T(8,128)(2,1)} %get-tuple-element.231.x_ref, bf16[4,56,512]{2,1,0:T(8,128)(2,1)} %copy-done.26, ...), custom_call_target="tpu_custom_call" | custom-call | flops 3489660928 | bytes 16777216 | tf_op jit(solution)/shard_map/attend/pallas_call | solution.py:255
  87.2 3.5 %collective-permute-done.29.refs_2_ = bf16[4,88,512]{2,1,0:T(8,128)(2,1)S(1)} collective-permute-done((bf16[4,88,512]{2,1,0:T(8,128)(2,1)S(1)}, bf16[4,88,512]{2,1,0:T(8,128)(2,1)S(1)}, u32[]{:S(2)}, u32[]{:S(2)}) %collective-permute-start.29) | collective-permute-done | bytes 360480 | tf_op jit(solution)/shard_map/ppermute | solution.py:190
  94.3 17.5 %dense_turn.1 = (bf16[1024,512]{1,0:T(8,128)(2,1)}, bf16[1024,512]{1,0:T(8,128)(2,1)}, f32[1024,512]{1,0:T(8,128)}, bf16[16,88,512]{2,1,0:T(8,128)(2,1)}, bf16[16,88,512]{2,1,0:T(8,128)(2,1)}) custom-call(s32[1]{0:T(128)} %bitcast.place_ref, s32[1]{0:T(128)S(6)} %add.47.live_ref, s32[1]{0:T(128)S(6)} %copy.52.ids_ref, ...), custom_call_target="tpu_custom_call" | custom-call | flops 8053063680 | bytes 16777216 | tf_op jit(solution)/shard_map/dense_turn/pallas_call | solution.py:534
  112.0 16.7 %attend_back.2 = (bf16[16,56,512]{2,1,0:T(8,128)(2,1)}, bf16[16,56,512]{2,1,0:T(8,128)(2,1)}, bf16[4,1024,384]{2,1,0:T(8,128)(2,1)}) custom-call(s32[1]{0:T(128)} %bitcast.place_ref, bf16[1024,512]{1,0:T(8,128)(2,1)} %get-tuple-element.231.x_ref, bf16[4,1024,384]{2,1,0:T(8,128)(2,1)} %get-tuple-element.247.joint_ref, ...), custom_call_target="tpu_custom_call" | custom-call | flops 5368709120 | bytes 16777216 | tf_op jit(solution)/shard_map/attend_back/pallas_call | solution.py:608
  133.7 17.6 %dense_back.1 = (bf16[1024,512]{1,0:T(8,128)(2,1)}, f32[1024,512]{1,0:T(8,128)}, bf16[16,88,512]{2,1,0:T(8,128)(2,1)}, bf16[16,88,512]{2,1,0:T(8,128)(2,1)}) custom-call(s32[1]{0:T(128)} %bitcast.place_ref, f32[1024,512]{1,0:T(8,128)} %get-tuple-element.264.grad_one_next, bf16[4,1024,384]{2,1,0:T(8,128)(2,1)} %get-tuple-element.265.grad_joint_next, ...), custom_call_target="tpu_custom_call" | custom-call | flops 6979321856 | bytes 20971520 | tf_op jit(solution)/shard_map/dense_back/pallas_call | solution.py:507
  152.2 2.6 %collective-permute-done.40.refs_3_ = bf16[16,88,512]{2,1,0:T(8,128)(2,1)S(1)} collective-permute-done((bf16[16,88,512]{2,1,0:T(8,128)(2,1)}, bf16[16,88,512]{2,1,0:T(8,128)(2,1)S(1)}, u32[]{:S(2)}, u32[]{:S(2)}) %collective-permute-start.40) | collective-permute-done | bytes 1441824 | tf_op jit(solution)/shard_map/ppermute | solution.py:190
  160.3 16.5 %attend_back.3 = (bf16[16,56,512]{2,1,0:T(8,128)(2,1)}, bf16[16,56,512]{2,1,0:T(8,128)(2,1)}, bf16[4,1024,384]{2,1,0:T(8,128)(2,1)}) custom-call(s32[1]{0:T(128)} %bitcast.place_ref, bf16[1024,512]{1,0:T(8,128)(2,1)} %bitcast.17, bf16[4,1024,384]{2,1,0:T(8,128)(2,1)} %get-tuple-element.297.joint_ref, bf16[4,896,1024]{2,1,0:T(8,128)(2,1)} %get-tuple-element.298.probs_ref, ...), custom_call_target="tpu_custom_call" | custom-call | flops 5368709120 | bytes 16777216 | tf_op jit(solution)/shard_map/attend_back/pallas_call | solution.py:608
  176.8 5.8 %grad_x.1 = f32[1024,512]{1,0:T(8,128)} custom-call(f32[1024,512]{1,0:T(8,128)} %get-tuple-element.301.grad_one_ref, bf16[4,1024,384]{2,1,0:T(8,128)(2,1)} %get-tuple-element.302.grad_joint_ref, bf16[4,512,384]{2,1,0:T(8,128)(2,1)} %get-tuple-element.303.weight_ref), custom_call_target="tpu_custom_call" | custom-call | flops 1610612736 | bytes 10485760 | tf_op jit(solution)/shard_map/grad_x/pallas_call | solution.py:640
  185.9 2.3 %collective-permute-done.45 = bf16[16,56,512]{2,1,0:T(8,128)(2,1)S(1)} collective-permute-done((bf16[16,56,512]{2,1,0:T(8,128)(2,1)}, bf16[16,56,512]{2,1,0:T(8,128)(2,1)S(1)}, u32[]{:S(2)}, u32[]{:S(2)}) %collective-permute-start.45) | collective-permute-done | bytes 917536 | tf_op jit(solution)/shard_map/ppermute | solution.py:190
  189.0 1.7 collective-permute-start.47
  194.2 3.3 %collective-permute-done.47.refs_3_ = bf16[88,512]{1,0:T(8,128)(2,1)S(1)} collective-permute-done((bf16[88,512]{1,0:T(8,128)(2,1)S(1)}, bf16[88,512]{1,0:T(8,128)(2,1)S(1)}, u32[]{:S(2)}, u32[]{:S(2)}) %collective-permute-start.47) | collective-permute-done | bytes 90144 | tf_op jit(solution)/shard_map/ppermute | solution.py:190
  197.5 2.2 %collective-permute-done.46 = bf16[2,144,512]{2,1,0:T(8,128)(2,1)S(1)} collective-permute-done((bf16[2,144,512]{2,1,0:T(8,128)(2,1)S(1)}, bf16[2,144,512]{2,1,0:T(8,128)(2,1)S(1)}, u32[]{:S(2)}, u32[]{:S(2)}) %collective-permute-start.46) | collective-permute-done | bytes 294944 | tf_op jit(solution)/shard_map/ppermute | solution.py:190
  203.8 1.8 collective-permute-start.52
  206.4 1.9 collective-permute-start.54
  208.4 2.3 %collective-permute-done.48.refs_1_ = bf16[144,512]{1,0:T(8,128)(2,1)S(1)} collective-permute-done((bf16[144,512]{1,0:T(8,128)(2,1)S(1)}, bf16[144,512]{1,0:T(8,128)(2,1)S(1)}, u32[]{:S(2)}, u32[]{:S(2)}) %collective-permute-start.48) | collective-permute-done | bytes 147488 | tf_op jit(solution)/shard_map/ppermute | solution.py:190
  210.7 1.6 second_step.1
  (223 shorter events, 54.7 us)
Async XLA Ops:
  33.9 17.0 %collective-permute-start.12 = (bf16[4,88,512]{2,1,0:T(8,128)(2,1)S(1)}, bf16[4,88,512]{2,1,0:T(8,128)(2,1)S(1)}, u32[]{:S(2)}, u32[]{:S(2)}) collective-permute-start(bf16[4,88,512]{2,1,0:T(8,128)(2,1)S(1)} %get-tuple-element.216.refs_0_), channel_id=1, source_target_pairs={{0,1},{1,0},{2,3},{3,2},{4,5},{5,4},{6,7},{7,6},{8,9},{9,8},{10,11... | collective-permute-start | bytes 1081352 | tf_op jit(solution)/shard_map/ppermute | solution.py:190
  35.5 15.4 %collective-permute-start.13 = (bf16[4,88,512]{2,1,0:T(8,128)(2,1)S(1)}, bf16[4,88,512]{2,1,0:T(8,128)(2,1)S(1)}, u32[]{:S(2)}, u32[]{:S(2)}) collective-permute-start(bf16[4,88,512]{2,1,0:T(8,128)(2,1)S(1)} %get-tuple-element.216.refs_0_), channel_id=1, source_target_pairs={{0,16},{1,17},{2,18},{3,19},{4,20},{5,21},{6,22},{7,23},{8,24},{9,... | collective-permute-start | bytes 1081352 | tf_op jit(solution)/shard_map/ppermute | solution.py:190
  37.0 13.9 %collective-permute-start.14 = (bf16[4,88,512]{2,1,0:T(8,128)(2,1)S(1)}, bf16[4,88,512]{2,1,0:T(8,128)(2,1)S(1)}, u32[]{:S(2)}, u32[]{:S(2)}) collective-permute-start(bf16[4,88,512]{2,1,0:T(8,128)(2,1)S(1)} %get-tuple-element.216.refs_0_), channel_id=1, source_target_pairs={{0,17},{1,16},{2,19},{3,18},{4,21},{5,20},{6,23},{7,22},{8,25},{9,... | collective-permute-start | bytes 1081352 | tf_op jit(solution)/shard_map/ppermute | solution.py:190
  37.5 13.5 %collective-permute-start.15 = (bf16[4,88,512]{2,1,0:T(8,128)(2,1)S(1)}, bf16[4,88,512]{2,1,0:T(8,128)(2,1)S(1)}, u32[]{:S(2)}, u32[]{:S(2)}) collective-permute-start(bf16[4,88,512]{2,1,0:T(8,128)(2,1)S(1)} %get-tuple-element.216.refs_0_), channel_id=1, source_target_pairs={{0,8},{1,9},{2,10},{3,11},{4,12},{5,13},{6,14},{7,15},{8,0},{9,1},... | collective-permute-start | bytes 1081352 | tf_op jit(solution)/shard_map/ppermute | solution.py:190
  37.5 13.4 %collective-permute-start.16 = (bf16[88,512]{1,0:T(8,128)(2,1)}, bf16[88,512]{1,0:T(8,128)(2,1)S(1)}, u32[]{:S(2)}, u32[]{:S(2)}) collective-permute-start(bf16[88,512]{1,0:T(8,128)(2,1)} %get-tuple-element.212.refs_0_), channel_id=1, source_target_pairs={{0,4},{1,5},{2,6},{3,7},{4,0},{5,1},{6,2},{7,3},{8,12},{9,13},{10,... | collective-permute-start | bytes 270344 | tf_op jit(solution)/shard_map/ppermute | solution.py:190
  53.7 15.0 %collective-permute-start.20 = (bf16[4,56,512]{2,1,0:T(8,128)(2,1)S(1)}, bf16[4,56,512]{2,1,0:T(8,128)(2,1)S(1)}, u32[]{:S(2)}, u32[]{:S(2)}) collective-permute-start(bf16[4,56,512]{2,1,0:T(8,128)(2,1)S(1)} %get-tuple-element.232.refs_0_), channel_id=1, source_target_pairs={{0,1},{1,0},{2,3},{3,2},{4,5},{5,4},{6,7},{7,6},{8,9},{9,8},{10,11... | collective-permute-start | bytes 688136 | tf_op jit(solution)/shard_map/ppermute | solution.py:190
  55.2 13.5 %collective-permute-start.21 = (bf16[4,56,512]{2,1,0:T(8,128)(2,1)S(1)}, bf16[4,56,512]{2,1,0:T(8,128)(2,1)S(1)}, u32[]{:S(2)}, u32[]{:S(2)}) collective-permute-start(bf16[4,56,512]{2,1,0:T(8,128)(2,1)S(1)} %get-tuple-element.232.refs_0_), channel_id=1, source_target_pairs={{0,16},{1,17},{2,18},{3,19},{4,20},{5,21},{6,22},{7,23},{8,24},{9,... | collective-permute-start | bytes 688136 | tf_op jit(solution)/shard_map/ppermute | solution.py:190
  56.8 12.0 %collective-permute-start.22 = (bf16[4,56,512]{2,1,0:T(8,128)(2,1)S(1)}, bf16[4,56,512]{2,1,0:T(8,128)(2,1)}, u32[]{:S(2)}, u32[]{:S(2)}) collective-permute-start(bf16[4,56,512]{2,1,0:T(8,128)(2,1)S(1)} %get-tuple-element.232.refs_0_), channel_id=1, source_target_pairs={{0,17},{1,16},{2,19},{3,18},{4,21},{5,20},{6,23},{7,22},{8,25},{9,... | collective-permute-start | bytes 688136 | tf_op jit(solution)/shard_map/ppermute | solution.py:190
  57.2 11.5 %collective-permute-start.23 = (bf16[4,56,512]{2,1,0:T(8,128)(2,1)S(1)}, bf16[4,56,512]{2,1,0:T(8,128)(2,1)S(1)}, u32[]{:S(2)}, u32[]{:S(2)}) collective-permute-start(bf16[4,56,512]{2,1,0:T(8,128)(2,1)S(1)} %get-tuple-element.232.refs_0_), channel_id=1, source_target_pairs={{0,8},{1,9},{2,10},{3,11},{4,12},{5,13},{6,14},{7,15},{8,0},{9,1},... | collective-permute-start | bytes 688136 | tf_op jit(solution)/shard_map/ppermute | solution.py:190
  71.3 15.9 %collective-permute-start.28 = (bf16[4,88,512]{2,1,0:T(8,128)(2,1)S(1)}, bf16[4,88,512]{2,1,0:T(8,128)(2,1)S(1)}, u32[]{:S(2)}, u32[]{:S(2)}) collective-permute-start(bf16[4,88,512]{2,1,0:T(8,128)(2,1)S(1)} %join.9.refs_0_), channel_id=1, source_target_pairs={{0,1},{1,0},{2,3},{3,2},{4,5},{5,4},{6,7},{7,6},{8,9},{9,8},{10,11... | collective-permute-start | bytes 1081352 | tf_op jit(solution)/shard_map/ppermute | solution.py:190
  72.8 18.0 %collective-permute-start.29 = (bf16[4,88,512]{2,1,0:T(8,128)(2,1)S(1)}, bf16[4,88,512]{2,1,0:T(8,128)(2,1)S(1)}, u32[]{:S(2)}, u32[]{:S(2)}) collective-permute-start(bf16[4,88,512]{2,1,0:T(8,128)(2,1)S(1)} %join.9.refs_0_), channel_id=1, source_target_pairs={{0,16},{1,17},{2,18},{3,19},{4,20},{5,21},{6,22},{7,23},{8,24},{9,... | collective-permute-start | bytes 1081352 | tf_op jit(solution)/shard_map/ppermute | solution.py:190
  74.3 16.5 %collective-permute-start.30 = (bf16[4,88,512]{2,1,0:T(8,128)(2,1)S(1)}, bf16[4,88,512]{2,1,0:T(8,128)(2,1)S(1)}, u32[]{:S(2)}, u32[]{:S(2)}) collective-permute-start(bf16[4,88,512]{2,1,0:T(8,128)(2,1)S(1)} %join.9.refs_0_), channel_id=1, source_target_pairs={{0,17},{1,16},{2,19},{3,18},{4,21},{5,20},{6,23},{7,22},{8,25},{9,... | collective-permute-start | bytes 1081352 | tf_op jit(solution)/shard_map/ppermute | solution.py:190
  74.7 16.0 %collective-permute-start.31 = (bf16[4,88,512]{2,1,0:T(8,128)(2,1)S(1)}, bf16[4,88,512]{2,1,0:T(8,128)(2,1)S(1)}, u32[]{:S(2)}, u32[]{:S(2)}) collective-permute-start(bf16[4,88,512]{2,1,0:T(8,128)(2,1)S(1)} %join.9.refs_0_), channel_id=1, source_target_pairs={{0,8},{1,9},{2,10},{3,11},{4,12},{5,13},{6,14},{7,15},{8,0},{9,1},... | collective-permute-start | bytes 1081352 | tf_op jit(solution)/shard_map/ppermute | solution.py:190
  111.8 16.9 %collective-permute-start.35 = (bf16[16,88,512]{2,1,0:T(8,128)(2,1)}, bf16[16,88,512]{2,1,0:T(8,128)(2,1)S(1)}, u32[]{:S(2)}, u32[]{:S(2)}) collective-permute-start(bf16[16,88,512]{2,1,0:T(8,128)(2,1)} %get-tuple-element.254), channel_id=1, source_target_pairs={{0,8},{1,9},{2,10},{3,11},{4,12},{5,13},{6,14},{7,15},{8,0},{9,1},... | collective-permute-start | bytes 4325384 | tf_op jit(solution)/shard_map/ppermute | solution.py:190
  129.9 21.5 %collective-permute-start.36 = (bf16[16,56,512]{2,1,0:T(8,128)(2,1)}, bf16[16,56,512]{2,1,0:T(8,128)(2,1)S(1)}, u32[]{:S(2)}, u32[]{:S(2)}) collective-permute-start(bf16[16,56,512]{2,1,0:T(8,128)(2,1)} %get-tuple-element.260), channel_id=1, source_target_pairs={{0,8},{1,9},{2,10},{3,11},{4,12},{5,13},{6,14},{7,15},{8,0},{9,1},... | collective-permute-start | bytes 2752520 | tf_op jit(solution)/shard_map/ppermute | solution.py:190
  130.2 21.1 %collective-permute-start.37 = (bf16[4,88,512]{2,1,0:T(8,128)(2,1)}, bf16[4,88,512]{2,1,0:T(8,128)(2,1)S(1)}, u32[]{:S(2)}, u32[]{:S(2)}) collective-permute-start(bf16[4,88,512]{2,1,0:T(8,128)(2,1)} %get-tuple-element.261), channel_id=1, source_target_pairs={{0,1},{1,0},{2,3},{3,2},{4,5},{5,4},{6,7},{7,6},{8,9},{9,8},{10,11... | collective-permute-start | bytes 1081352 | tf_op jit(solution)/shard_map/ppermute | solution.py:190
  131.4 19.9 %collective-permute-start.38 = (bf16[4,88,512]{2,1,0:T(8,128)(2,1)S(1)}, bf16[4,88,512]{2,1,0:T(8,128)(2,1)S(1)}, u32[]{:S(2)}, u32[]{:S(2)}) collective-permute-start(bf16[4,88,512]{2,1,0:T(8,128)(2,1)S(1)} %get-tuple-element.262), channel_id=1, source_target_pairs={{0,16},{1,17},{2,18},{3,19},{4,20},{5,21},{6,22},{7,23},{8,24},{9,... | collective-permute-start | bytes 1081352 | tf_op jit(solution)/shard_map/ppermute | solution.py:190
  132.3 19.1 %collective-permute-start.39 = (bf16[4,88,512]{2,1,0:T(8,128)(2,1)S(1)}, bf16[4,88,512]{2,1,0:T(8,128)(2,1)S(1)}, u32[]{:S(2)}, u32[]{:S(2)}) collective-permute-start(bf16[4,88,512]{2,1,0:T(8,128)(2,1)S(1)} %get-tuple-element.263), channel_id=1, source_target_pairs={{0,17},{1,16},{2,19},{3,18},{4,21},{5,20},{6,23},{7,22},{8,25},{9,... | collective-permute-start | bytes 1081352 | tf_op jit(solution)/shard_map/ppermute | solution.py:190
  156.3 26.3 %collective-permute-start.41 = (bf16[4,144,512]{2,1,0:T(8,128)(2,1)}, bf16[4,144,512]{2,1,0:T(8,128)(2,1)S(1)}, u32[]{:S(2)}, u32[]{:S(2)}) collective-permute-start(bf16[4,144,512]{2,1,0:T(8,128)(2,1)} %get-tuple-element.293), channel_id=1, source_target_pairs={{0,1},{1,0},{2,3},{3,2},{4,5},{5,4},{6,7},{7,6},{8,9},{9,8},{10,11... | collective-permute-start | bytes 1769480 | tf_op jit(solution)/shard_map/ppermute | solution.py:190
  157.6 26.4 %collective-permute-start.42 = (bf16[4,144,512]{2,1,0:T(8,128)(2,1)}, bf16[4,144,512]{2,1,0:T(8,128)(2,1)S(1)}, u32[]{:S(2)}, u32[]{:S(2)}) collective-permute-start(bf16[4,144,512]{2,1,0:T(8,128)(2,1)} %get-tuple-element.294), channel_id=1, source_target_pairs={{0,16},{1,17},{2,18},{3,19},{4,20},{5,21},{6,22},{7,23},{8,24},{9,... | collective-permute-start | bytes 1769480 | tf_op jit(solution)/shard_map/ppermute | solution.py:190
  158.4 27.1 %collective-permute-start.43 = (bf16[4,144,512]{2,1,0:T(8,128)(2,1)S(1)}, bf16[4,144,512]{2,1,0:T(8,128)(2,1)S(1)}, u32[]{:S(2)}, u32[]{:S(2)}) collective-permute-start(bf16[4,144,512]{2,1,0:T(8,128)(2,1)S(1)} %get-tuple-element.295), channel_id=1, source_target_pairs={{0,17},{1,16},{2,19},{3,18},{4,21},{5,20},{6,23},{7,22},{8,25},{9,... | collective-permute-start | bytes 1769480 | tf_op jit(solution)/shard_map/ppermute | solution.py:190
  159.8 22.8 %collective-permute-start.44 = (bf16[2,88,512]{2,1,0:T(8,128)(2,1)}, bf16[2,88,512]{2,1,0:T(8,128)(2,1)S(1)}, u32[]{:S(2)}, u32[]{:S(2)}) collective-permute-start(bf16[2,88,512]{2,1,0:T(8,128)(2,1)} %get-tuple-element.296), channel_id=1, source_target_pairs={{0,2},{1,3},{2,0},{3,1},{4,6},{5,7},{6,4},{7,5},{8,10},{9,11},{10,... | collective-permute-start | bytes 540680 | tf_op jit(solution)/shard_map/ppermute | solution.py:190
  190.7 12.9 %collective-permute-start.49 = (bf16[4,56,512]{2,1,0:T(8,128)(2,1)S(1)}, bf16[4,56,512]{2,1,0:T(8,128)(2,1)S(1)}, u32[]{:S(2)}, u32[]{:S(2)}) collective-permute-start(bf16[4,56,512]{2,1,0:T(8,128)(2,1)S(1)} %get-tuple-element.325), channel_id=1, source_target_pairs={{0,1},{1,0},{2,3},{3,2},{4,5},{5,4},{6,7},{7,6},{8,9},{9,8},{10,11... | collective-permute-start | bytes 688136 | tf_op jit(solution)/shard_map/ppermute | solution.py:190
  191.5 12.2 %collective-permute-start.50 = (bf16[4,56,512]{2,1,0:T(8,128)(2,1)S(1)}, bf16[4,56,512]{2,1,0:T(8,128)(2,1)S(1)}, u32[]{:S(2)}, u32[]{:S(2)}) collective-permute-start(bf16[4,56,512]{2,1,0:T(8,128)(2,1)S(1)} %get-tuple-element.326), channel_id=1, source_target_pairs={{0,16},{1,17},{2,18},{3,19},{4,20},{5,21},{6,22},{7,23},{8,24},{9,... | collective-permute-start | bytes 688136 | tf_op jit(solution)/shard_map/ppermute | solution.py:190
  (87 other events, 895.0 us)

commit v4 on v3

--- a/solution.py
+++ b/solution.py
@@ -922,13 +922,11 @@
     got = swap(sent, CORE)
     late_own, late_sent = pair_sum(late_kept, late_got)
     middle_kept, middle_sent = square_sum_call([stacks[0], *middle_got])
-    got, middle_sent, late_sent = sync(got, middle_sent, late_sent)
-    stacks = core_sum(kept, got)
-    stacks, middle_sent, late_sent = sync(stacks, middle_sent, late_sent)
-    got = square_back(stacks)
     middle_got = swap(middle_sent, CHAIN[2])
     late_got = swap(late_sent, CHAIN[1])
-    middle_got, late_got = sync(middle_got, late_got)
+    stacks = core_sum(kept, got)
+    got = square_back(stacks)
+    middle_got, late_got, got[0] = sync(middle_got, late_got, got[0])
     middle_own, middle_sent = pair_sum(middle_kept, middle_got)
     middle_got = swap(middle_sent, CHAIN[1])
 

time: 215 us -> 213 us (level)
  transfers between devices with their start and end apart: 55 -> 55, of which waited for: 25 -> 27; matrix products, arithmetic and copies ran while one was open for 0% -> 0% of each run, Pallas kernels for 44% -> 44%
where the time goes in v4:
time: 213 us
  Pallas kernels  116 us (54%)
  starting transfers between devices  44.8 us (21%)
  waiting for transfers between devices  42 us (20%)
  between operations  5.64 us (3%)
  local copies, waits for them, and re-layouts  2.9 us (1%)
    ppermute x55, starting transfers between devices, swap(): lax.ppermute(block, AXES, [(one, one ^ offset) for one in range(OWNERS)])  44.8 us
    ppermute x55, waiting for transfers between devices, swap(): lax.ppermute(block, AXES, [(one, one ^ offset) for one in range(OWNERS)])  42 us
    pallas_call x2, Pallas kernels, attend_back_call(): pl.pallas_call(attend_back_kernel, grid_spec=pltpu.PrefetchScalarGridSpec...  33.2 us
    pallas_call x2, Pallas kernels, attend_call(): pl.pallas_call(attend_kernel, grid_spec=pltpu.PrefetchScalarGridSpec(num_...  24.8 us
    pallas_call x1, Pallas kernels, dense_back_call(): pl.pallas_call(dense_back_kernel, grid_spec=pltpu.PrefetchScalarGridSpec(...  17.6 us
    pallas_call x1, Pallas kernels, dense_turn_call(): pl.pallas_call(dense_turn_kernel, grid_spec=pltpu.PrefetchScalarGridSpec(...  17.5 us
    pallas_call x1, Pallas kernels, dense_call(): pl.pallas_call(dense_kernel, grid_spec=pltpu.PrefetchScalarGridSpec(num_s...  9.38 us
    pallas_call x1, Pallas kernels, grad_x_call(): pl.pallas_call(grad_x_kernel, grid=(rows // ROW_BLOCK,), in_specs=[by_row...  5.77 us
  transfers between devices with their start and end apart: 55, of which 27 were waited for; matrix products, arithmetic and copies ran while one was open for 0% of the time, Pallas kernels for 44%

profile of v4, /device:TPU:0, one launch (start us, length us, event | category | flops | bytes accessed | tf_op | source)
XLA Modules:
  0.0 213.1 jit_solution(16536810364615360164)
XLA Ops:
  1.3 2.0 pack.1
  3.3 4.1 %collective-permute-start = (bf16[56,512]{1,0:T(8,128)(2,1)}, bf16[56,512]{1,0:T(8,128)(2,1)S(1)}, u32[]{:S(2)}, u32[]{:S(2)}) collective-permute-start(bf16[56,512]{1,0:T(8,128)(2,1)} %get-tuple-element.183.refs_0_), channel_id=1, source_target_pairs={{0,4},{1,5},{2,6},{3,7},{4,0},{5,1},{6,2},{7,3},{8,12},{9,13},{10,... | collective-permute-start | bytes 172040 | tf_op jit(solution)/shard_map/ppermute | solution.py:190
  7.3 1.6 collective-permute-start.1
  11.7 3.4 %collective-permute-done.2.refs_3_ = bf16[56,512]{1,0:T(8,128)(2,1)S(1)} collective-permute-done((bf16[56,512]{1,0:T(8,128)(2,1)}, bf16[56,512]{1,0:T(8,128)(2,1)S(1)}, u32[]{:S(2)}, u32[]{:S(2)}) %collective-permute-start.2) | collective-permute-done | bytes 57376 | tf_op jit(solution)/shard_map/ppermute | solution.py:190
  16.0 1.6 collective-permute-start.4
  20.2 5.8 %collective-permute-done.10.refs_1_ = bf16[144,512]{1,0:T(8,128)(2,1)S(1)} collective-permute-done((bf16[144,512]{1,0:T(8,128)(2,1)}, bf16[144,512]{1,0:T(8,128)(2,1)S(1)}, u32[]{:S(2)}, u32[]{:S(2)}) %collective-permute-start.10) | collective-permute-done | bytes 147488 | tf_op jit(solution)/shard_map/ppermute | solution.py:190
  28.4 5.4 %collective-permute-done.11.refs_1_ = bf16[2,144,512]{2,1,0:T(8,128)(2,1)S(1)} collective-permute-done((bf16[2,144,512]{2,1,0:T(8,128)(2,1)S(1)}, bf16[2,144,512]{2,1,0:T(8,128)(2,1)S(1)}, u32[]{:S(2)}, u32[]{:S(2)}) %collective-permute-start.11) | collective-permute-done | bytes 294944 | tf_op jit(solution)/shard_map/ppermute | solution.py:190
  33.9 1.6 collective-permute-start.12
  38.5 12.4 %attend.2 = (bf16[4,1024,384]{2,1,0:T(8,128)(2,1)}, bf16[4,896,1024]{2,1,0:T(8,128)(2,1)}, bf16[1024,512]{1,0:T(8,128)(2,1)}, bf16[4,512,384]{2,1,0:T(8,128)(2,1)}, f32[8,512]{1,0:T(8,128)}) custom-call(s32[1]{0:T(128)} %bitcast.place_ref, bf16[1024,512]{1,0:T(8,128)(2,1)} %bitcast.15, bf16[4,56,512]{2,1,0:T(8,128)(2,1)} %copy-done.7, ...), custom_call_target="tpu_custom_call" | custom-call | flops 3489660928 | bytes 16777216 | tf_op jit(solution)/shard_map/attend/pallas_call | solution.py:255
  57.2 2.0 collective-permute-start.24
  59.3 9.4 %dense.1 = (bf16[1024,512]{1,0:T(8,128)(2,1)}, f32[1024,512]{1,0:T(8,128)}, f32[1024,1]{1,0:T(8,128)}, bf16[1024,1024]{1,0:T(8,128)(2,1)}, f32[1024,1024]{1,0:T(...) custom-call(s32[1]{0:T(128)} %bitcast.place_ref, ...), custom_call_target="tpu_custom_call" | custom-call | flops 2684354560 | bytes 16777216 | tf_op jit(solution)/shard_map/dense/pallas_call | solution.py:477
  74.8 12.4 %attend.3 = (bf16[4,1024,384]{2,1,0:T(8,128)(2,1)}, bf16[4,896,1024]{2,1,0:T(8,128)(2,1)}, bf16[1024,512]{1,0:T(8,128)(2,1)}, bf16[4,512,384]{2,1,0:T(8,128)(2,1)}, f32[8,512]{1,0:T(8,128)}) custom-call(s32[1]{0:T(128)} %bitcast.place_ref, bf16[1024,512]{1,0:T(8,128)(2,1)} %get-tuple-element.223.x_ref, bf16[4,56,512]{2,1,0:T(8,128)(2,1)} %copy-done.26, ...), custom_call_target="tpu_custom_call" | custom-call | flops 3489660928 | bytes 16777216 | tf_op jit(solution)/shard_map/attend/pallas_call | solution.py:255
  87.2 3.5 %collective-permute-done.29.refs_2_ = bf16[4,88,512]{2,1,0:T(8,128)(2,1)S(1)} collective-permute-done((bf16[4,88,512]{2,1,0:T(8,128)(2,1)S(1)}, bf16[4,88,512]{2,1,0:T(8,128)(2,1)S(1)}, u32[]{:S(2)}, u32[]{:S(2)}) %collective-permute-start.29) | collective-permute-done | bytes 360480 | tf_op jit(solution)/shard_map/ppermute | solution.py:190
  94.3 17.5 %dense_turn.1 = (bf16[1024,512]{1,0:T(8,128)(2,1)}, bf16[1024,512]{1,0:T(8,128)(2,1)}, f32[1024,512]{1,0:T(8,128)}, bf16[16,88,512]{2,1,0:T(8,128)(2,1)}, bf16[16,88,512]{2,1,0:T(8,128)(2,1)}) custom-call(s32[1]{0:T(128)} %bitcast.place_ref, s32[1]{0:T(128)S(6)} %add.47.live_ref, s32[1]{0:T(128)S(6)} %copy.52.ids_ref, ...), custom_call_target="tpu_custom_call" | custom-call | flops 8053063680 | bytes 16777216 | tf_op jit(solution)/shard_map/dense_turn/pallas_call | solution.py:534
  112.0 16.7 %attend_back.2 = (bf16[16,56,512]{2,1,0:T(8,128)(2,1)}, bf16[16,56,512]{2,1,0:T(8,128)(2,1)}, bf16[4,1024,384]{2,1,0:T(8,128)(2,1)}) custom-call(s32[1]{0:T(128)} %bitcast.place_ref, bf16[1024,512]{1,0:T(8,128)(2,1)} %get-tuple-element.223.x_ref, bf16[4,1024,384]{2,1,0:T(8,128)(2,1)} %get-tuple-element.239.joint_ref, ...), custom_call_target="tpu_custom_call" | custom-call | flops 5368709120 | bytes 16777216 | tf_op jit(solution)/shard_map/attend_back/pallas_call | solution.py:608
  133.7 17.6 %dense_back.1 = (bf16[1024,512]{1,0:T(8,128)(2,1)}, f32[1024,512]{1,0:T(8,128)}, bf16[16,88,512]{2,1,0:T(8,128)(2,1)}, bf16[16,88,512]{2,1,0:T(8,128)(2,1)}) custom-call(s32[1]{0:T(128)} %bitcast.place_ref, f32[1024,512]{1,0:T(8,128)} %get-tuple-element.256.grad_one_next, bf16[4,1024,384]{2,1,0:T(8,128)(2,1)} %get-tuple-element.257.grad_joint_next, ...), custom_call_target="tpu_custom_call" | custom-call | flops 6979321856 | bytes 20971520 | tf_op jit(solution)/shard_map/dense_back/pallas_call | solution.py:507
  152.2 2.6 %collective-permute-done.40.refs_3_ = bf16[16,88,512]{2,1,0:T(8,128)(2,1)S(1)} collective-permute-done((bf16[16,88,512]{2,1,0:T(8,128)(2,1)}, bf16[16,88,512]{2,1,0:T(8,128)(2,1)S(1)}, u32[]{:S(2)}, u32[]{:S(2)}) %collective-permute-start.40) | collective-permute-done | bytes 1441824 | tf_op jit(solution)/shard_map/ppermute | solution.py:190
  160.3 16.5 %attend_back.3 = (bf16[16,56,512]{2,1,0:T(8,128)(2,1)}, bf16[16,56,512]{2,1,0:T(8,128)(2,1)}, bf16[4,1024,384]{2,1,0:T(8,128)(2,1)}) custom-call(s32[1]{0:T(128)} %bitcast.place_ref, bf16[1024,512]{1,0:T(8,128)(2,1)} %bitcast.17, bf16[4,1024,384]{2,1,0:T(8,128)(2,1)} %get-tuple-element.289.joint_ref, bf16[4,896,1024]{2,1,0:T(8,128)(2,1)} %get-tuple-element.290.probs_ref, ...), custom_call_target="tpu_custom_call" | custom-call | flops 5368709120 | bytes 16777216 | tf_op jit(solution)/shard_map/attend_back/pallas_call | solution.py:608
  176.8 5.8 %grad_x.1 = f32[1024,512]{1,0:T(8,128)} custom-call(f32[1024,512]{1,0:T(8,128)} %get-tuple-element.293.grad_one_ref, bf16[4,1024,384]{2,1,0:T(8,128)(2,1)} %get-tuple-element.294.grad_joint_ref, bf16[4,512,384]{2,1,0:T(8,128)(2,1)} %get-tuple-element.295.weight_ref), custom_call_target="tpu_custom_call" | custom-call | flops 1610612736 | bytes 10485760 | tf_op jit(solution)/shard_map/grad_x/pallas_call | solution.py:640
  186.2 2.0 collective-permute-done.47
  192.6 2.9 %collective-permute-done.46.refs_3_ = bf16[88,512]{1,0:T(8,128)(2,1)S(1)} collective-permute-done((bf16[88,512]{1,0:T(8,128)(2,1)S(1)}, bf16[88,512]{1,0:T(8,128)(2,1)S(1)}, u32[]{:S(2)}, u32[]{:S(2)}) %collective-permute-start.46) | collective-permute-done | bytes 90144 | tf_op jit(solution)/shard_map/ppermute | solution.py:190
  195.6 1.7 collective-permute-done.45
  202.2 2.5 %collective-permute-start.52 = (bf16[56,512]{1,0:T(8,128)(2,1)S(1)}, bf16[56,512]{1,0:T(8,128)(2,1)S(1)}, u32[]{:S(2)}, u32[]{:S(2)}) collective-permute-start(bf16[56,512]{1,0:T(8,128)(2,1)S(1)} %get-tuple-element.313), channel_id=1, source_target_pairs={{0,4},{1,5},{2,6},{3,7},{4,0},{5,1},{6,2},{7,3},{8,12},{9,13},{10,... | collective-permute-start | bytes 172040 | tf_op jit(solution)/shard_map/ppermute | solution.py:190
  207.4 1.6 second_step.1
  (223 shorter events, 55.0 us)
Async XLA Ops:
  33.9 17.0 %collective-permute-start.12 = (bf16[4,88,512]{2,1,0:T(8,128)(2,1)S(1)}, bf16[4,88,512]{2,1,0:T(8,128)(2,1)S(1)}, u32[]{:S(2)}, u32[]{:S(2)}) collective-permute-start(bf16[4,88,512]{2,1,0:T(8,128)(2,1)S(1)} %get-tuple-element.208.refs_0_), channel_id=1, source_target_pairs={{0,1},{1,0},{2,3},{3,2},{4,5},{5,4},{6,7},{7,6},{8,9},{9,8},{10,11... | collective-permute-start | bytes 1081352 | tf_op jit(solution)/shard_map/ppermute | solution.py:190
  35.5 15.4 %collective-permute-start.13 = (bf16[4,88,512]{2,1,0:T(8,128)(2,1)S(1)}, bf16[4,88,512]{2,1,0:T(8,128)(2,1)S(1)}, u32[]{:S(2)}, u32[]{:S(2)}) collective-permute-start(bf16[4,88,512]{2,1,0:T(8,128)(2,1)S(1)} %get-tuple-element.208.refs_0_), channel_id=1, source_target_pairs={{0,16},{1,17},{2,18},{3,19},{4,20},{5,21},{6,22},{7,23},{8,24},{9,... | collective-permute-start | bytes 1081352 | tf_op jit(solution)/shard_map/ppermute | solution.py:190
  37.0 13.9 %collective-permute-start.14 = (bf16[4,88,512]{2,1,0:T(8,128)(2,1)S(1)}, bf16[4,88,512]{2,1,0:T(8,128)(2,1)S(1)}, u32[]{:S(2)}, u32[]{:S(2)}) collective-permute-start(bf16[4,88,512]{2,1,0:T(8,128)(2,1)S(1)} %get-tuple-element.208.refs_0_), channel_id=1, source_target_pairs={{0,17},{1,16},{2,19},{3,18},{4,21},{5,20},{6,23},{7,22},{8,25},{9,... | collective-permute-start | bytes 1081352 | tf_op jit(solution)/shard_map/ppermute | solution.py:190
  37.5 13.5 %collective-permute-start.15 = (bf16[4,88,512]{2,1,0:T(8,128)(2,1)S(1)}, bf16[4,88,512]{2,1,0:T(8,128)(2,1)S(1)}, u32[]{:S(2)}, u32[]{:S(2)}) collective-permute-start(bf16[4,88,512]{2,1,0:T(8,128)(2,1)S(1)} %get-tuple-element.208.refs_0_), channel_id=1, source_target_pairs={{0,8},{1,9},{2,10},{3,11},{4,12},{5,13},{6,14},{7,15},{8,0},{9,1},... | collective-permute-start | bytes 1081352 | tf_op jit(solution)/shard_map/ppermute | solution.py:190
  37.5 13.4 %collective-permute-start.16 = (bf16[88,512]{1,0:T(8,128)(2,1)}, bf16[88,512]{1,0:T(8,128)(2,1)S(1)}, u32[]{:S(2)}, u32[]{:S(2)}) collective-permute-start(bf16[88,512]{1,0:T(8,128)(2,1)} %get-tuple-element.204.refs_0_), channel_id=1, source_target_pairs={{0,4},{1,5},{2,6},{3,7},{4,0},{5,1},{6,2},{7,3},{8,12},{9,13},{10,... | collective-permute-start | bytes 270344 | tf_op jit(solution)/shard_map/ppermute | solution.py:190
  53.7 15.0 %collective-permute-start.20 = (bf16[4,56,512]{2,1,0:T(8,128)(2,1)S(1)}, bf16[4,56,512]{2,1,0:T(8,128)(2,1)S(1)}, u32[]{:S(2)}, u32[]{:S(2)}) collective-permute-start(bf16[4,56,512]{2,1,0:T(8,128)(2,1)S(1)} %get-tuple-element.224.refs_0_), channel_id=1, source_target_pairs={{0,1},{1,0},{2,3},{3,2},{4,5},{5,4},{6,7},{7,6},{8,9},{9,8},{10,11... | collective-permute-start | bytes 688136 | tf_op jit(solution)/shard_map/ppermute | solution.py:190
  55.2 13.5 %collective-permute-start.21 = (bf16[4,56,512]{2,1,0:T(8,128)(2,1)S(1)}, bf16[4,56,512]{2,1,0:T(8,128)(2,1)S(1)}, u32[]{:S(2)}, u32[]{:S(2)}) collective-permute-start(bf16[4,56,512]{2,1,0:T(8,128)(2,1)S(1)} %get-tuple-element.224.refs_0_), channel_id=1, source_target_pairs={{0,16},{1,17},{2,18},{3,19},{4,20},{5,21},{6,22},{7,23},{8,24},{9,... | collective-permute-start | bytes 688136 | tf_op jit(solution)/shard_map/ppermute | solution.py:190
  56.8 12.0 %collective-permute-start.22 = (bf16[4,56,512]{2,1,0:T(8,128)(2,1)S(1)}, bf16[4,56,512]{2,1,0:T(8,128)(2,1)}, u32[]{:S(2)}, u32[]{:S(2)}) collective-permute-start(bf16[4,56,512]{2,1,0:T(8,128)(2,1)S(1)} %get-tuple-element.224.refs_0_), channel_id=1, source_target_pairs={{0,17},{1,16},{2,19},{3,18},{4,21},{5,20},{6,23},{7,22},{8,25},{9,... | collective-permute-start | bytes 688136 | tf_op jit(solution)/shard_map/ppermute | solution.py:190
  57.2 11.5 %collective-permute-start.23 = (bf16[4,56,512]{2,1,0:T(8,128)(2,1)S(1)}, bf16[4,56,512]{2,1,0:T(8,128)(2,1)S(1)}, u32[]{:S(2)}, u32[]{:S(2)}) collective-permute-start(bf16[4,56,512]{2,1,0:T(8,128)(2,1)S(1)} %get-tuple-element.224.refs_0_), channel_id=1, source_target_pairs={{0,8},{1,9},{2,10},{3,11},{4,12},{5,13},{6,14},{7,15},{8,0},{9,1},... | collective-permute-start | bytes 688136 | tf_op jit(solution)/shard_map/ppermute | solution.py:190
  57.2 11.5 %collective-permute-start.24 = (bf16[2,88,512]{2,1,0:T(8,128)(2,1)S(1)}, bf16[2,88,512]{2,1,0:T(8,128)(2,1)S(1)}, u32[]{:S(2)}, u32[]{:S(2)}) collective-permute-start(bf16[2,88,512]{2,1,0:T(8,128)(2,1)S(1)} %join.8.refs_0_), channel_id=1, source_target_pairs={{0,2},{1,3},{2,0},{3,1},{4,6},{5,7},{6,4},{7,5},{8,10},{9,11},{10,... | collective-permute-start | bytes 540680 | tf_op jit(solution)/shard_map/ppermute | solution.py:190
  71.3 15.9 %collective-permute-start.28 = (bf16[4,88,512]{2,1,0:T(8,128)(2,1)S(1)}, bf16[4,88,512]{2,1,0:T(8,128)(2,1)S(1)}, u32[]{:S(2)}, u32[]{:S(2)}) collective-permute-start(bf16[4,88,512]{2,1,0:T(8,128)(2,1)S(1)} %join.9.refs_0_), channel_id=1, source_target_pairs={{0,1},{1,0},{2,3},{3,2},{4,5},{5,4},{6,7},{7,6},{8,9},{9,8},{10,11... | collective-permute-start | bytes 1081352 | tf_op jit(solution)/shard_map/ppermute | solution.py:190
  72.8 18.0 %collective-permute-start.29 = (bf16[4,88,512]{2,1,0:T(8,128)(2,1)S(1)}, bf16[4,88,512]{2,1,0:T(8,128)(2,1)S(1)}, u32[]{:S(2)}, u32[]{:S(2)}) collective-permute-start(bf16[4,88,512]{2,1,0:T(8,128)(2,1)S(1)} %join.9.refs_0_), channel_id=1, source_target_pairs={{0,16},{1,17},{2,18},{3,19},{4,20},{5,21},{6,22},{7,23},{8,24},{9,... | collective-permute-start | bytes 1081352 | tf_op jit(solution)/shard_map/ppermute | solution.py:190
  74.3 16.5 %collective-permute-start.30 = (bf16[4,88,512]{2,1,0:T(8,128)(2,1)S(1)}, bf16[4,88,512]{2,1,0:T(8,128)(2,1)S(1)}, u32[]{:S(2)}, u32[]{:S(2)}) collective-permute-start(bf16[4,88,512]{2,1,0:T(8,128)(2,1)S(1)} %join.9.refs_0_), channel_id=1, source_target_pairs={{0,17},{1,16},{2,19},{3,18},{4,21},{5,20},{6,23},{7,22},{8,25},{9,... | collective-permute-start | bytes 1081352 | tf_op jit(solution)/shard_map/ppermute | solution.py:190
  74.7 16.0 %collective-permute-start.31 = (bf16[4,88,512]{2,1,0:T(8,128)(2,1)S(1)}, bf16[4,88,512]{2,1,0:T(8,128)(2,1)S(1)}, u32[]{:S(2)}, u32[]{:S(2)}) collective-permute-start(bf16[4,88,512]{2,1,0:T(8,128)(2,1)S(1)} %join.9.refs_0_), channel_id=1, source_target_pairs={{0,8},{1,9},{2,10},{3,11},{4,12},{5,13},{6,14},{7,15},{8,0},{9,1},... | collective-permute-start | bytes 1081352 | tf_op jit(solution)/shard_map/ppermute | solution.py:190
  111.8 16.9 %collective-permute-start.35 = (bf16[16,88,512]{2,1,0:T(8,128)(2,1)}, bf16[16,88,512]{2,1,0:T(8,128)(2,1)S(1)}, u32[]{:S(2)}, u32[]{:S(2)}) collective-permute-start(bf16[16,88,512]{2,1,0:T(8,128)(2,1)} %get-tuple-element.246), channel_id=1, source_target_pairs={{0,8},{1,9},{2,10},{3,11},{4,12},{5,13},{6,14},{7,15},{8,0},{9,1},... | collective-permute-start | bytes 4325384 | tf_op jit(solution)/shard_map/ppermute | solution.py:190
  129.9 21.5 %collective-permute-start.36 = (bf16[16,56,512]{2,1,0:T(8,128)(2,1)}, bf16[16,56,512]{2,1,0:T(8,128)(2,1)S(1)}, u32[]{:S(2)}, u32[]{:S(2)}) collective-permute-start(bf16[16,56,512]{2,1,0:T(8,128)(2,1)} %get-tuple-element.252), channel_id=1, source_target_pairs={{0,8},{1,9},{2,10},{3,11},{4,12},{5,13},{6,14},{7,15},{8,0},{9,1},... | collective-permute-start | bytes 2752520 | tf_op jit(solution)/shard_map/ppermute | solution.py:190
  130.2 21.1 %collective-permute-start.37 = (bf16[4,88,512]{2,1,0:T(8,128)(2,1)}, bf16[4,88,512]{2,1,0:T(8,128)(2,1)S(1)}, u32[]{:S(2)}, u32[]{:S(2)}) collective-permute-start(bf16[4,88,512]{2,1,0:T(8,128)(2,1)} %get-tuple-element.253), channel_id=1, source_target_pairs={{0,1},{1,0},{2,3},{3,2},{4,5},{5,4},{6,7},{7,6},{8,9},{9,8},{10,11... | collective-permute-start | bytes 1081352 | tf_op jit(solution)/shard_map/ppermute | solution.py:190
  131.4 19.9 %collective-permute-start.38 = (bf16[4,88,512]{2,1,0:T(8,128)(2,1)S(1)}, bf16[4,88,512]{2,1,0:T(8,128)(2,1)S(1)}, u32[]{:S(2)}, u32[]{:S(2)}) collective-permute-start(bf16[4,88,512]{2,1,0:T(8,128)(2,1)S(1)} %get-tuple-element.254), channel_id=1, source_target_pairs={{0,16},{1,17},{2,18},{3,19},{4,20},{5,21},{6,22},{7,23},{8,24},{9,... | collective-permute-start | bytes 1081352 | tf_op jit(solution)/shard_map/ppermute | solution.py:190
  132.3 19.1 %collective-permute-start.39 = (bf16[4,88,512]{2,1,0:T(8,128)(2,1)S(1)}, bf16[4,88,512]{2,1,0:T(8,128)(2,1)S(1)}, u32[]{:S(2)}, u32[]{:S(2)}) collective-permute-start(bf16[4,88,512]{2,1,0:T(8,128)(2,1)S(1)} %get-tuple-element.255), channel_id=1, source_target_pairs={{0,17},{1,16},{2,19},{3,18},{4,21},{5,20},{6,23},{7,22},{8,25},{9,... | collective-permute-start | bytes 1081352 | tf_op jit(solution)/shard_map/ppermute | solution.py:190
  156.3 26.3 %collective-permute-start.41 = (bf16[4,144,512]{2,1,0:T(8,128)(2,1)}, bf16[4,144,512]{2,1,0:T(8,128)(2,1)S(1)}, u32[]{:S(2)}, u32[]{:S(2)}) collective-permute-start(bf16[4,144,512]{2,1,0:T(8,128)(2,1)} %get-tuple-element.285), channel_id=1, source_target_pairs={{0,1},{1,0},{2,3},{3,2},{4,5},{5,4},{6,7},{7,6},{8,9},{9,8},{10,11... | collective-permute-start | bytes 1769480 | tf_op jit(solution)/shard_map/ppermute | solution.py:190
  157.6 26.4 %collective-permute-start.42 = (bf16[4,144,512]{2,1,0:T(8,128)(2,1)}, bf16[4,144,512]{2,1,0:T(8,128)(2,1)S(1)}, u32[]{:S(2)}, u32[]{:S(2)}) collective-permute-start(bf16[4,144,512]{2,1,0:T(8,128)(2,1)} %get-tuple-element.286), channel_id=1, source_target_pairs={{0,16},{1,17},{2,18},{3,19},{4,20},{5,21},{6,22},{7,23},{8,24},{9,... | collective-permute-start | bytes 1769480 | tf_op jit(solution)/shard_map/ppermute | solution.py:190
  158.4 27.1 %collective-permute-start.43 = (bf16[4,144,512]{2,1,0:T(8,128)(2,1)S(1)}, bf16[4,144,512]{2,1,0:T(8,128)(2,1)S(1)}, u32[]{:S(2)}, u32[]{:S(2)}) collective-permute-start(bf16[4,144,512]{2,1,0:T(8,128)(2,1)S(1)} %get-tuple-element.287), channel_id=1, source_target_pairs={{0,17},{1,16},{2,19},{3,18},{4,21},{5,20},{6,23},{7,22},{8,25},{9,... | collective-permute-start | bytes 1769480 | tf_op jit(solution)/shard_map/ppermute | solution.py:190
  159.8 22.8 %collective-permute-start.44 = (bf16[2,88,512]{2,1,0:T(8,128)(2,1)}, bf16[2,88,512]{2,1,0:T(8,128)(2,1)S(1)}, u32[]{:S(2)}, u32[]{:S(2)}) collective-permute-start(bf16[2,88,512]{2,1,0:T(8,128)(2,1)} %get-tuple-element.288), channel_id=1, source_target_pairs={{0,2},{1,3},{2,0},{3,1},{4,6},{5,7},{6,4},{7,5},{8,10},{9,11},{10,... | collective-permute-start | bytes 540680 | tf_op jit(solution)/shard_map/ppermute | solution.py:190
  190.1 12.0 %collective-permute-start.50 = (bf16[4,56,512]{2,1,0:T(8,128)(2,1)S(1)}, bf16[4,56,512]{2,1,0:T(8,128)(2,1)S(1)}, u32[]{:S(2)}, u32[]{:S(2)}) collective-permute-start(bf16[4,56,512]{2,1,0:T(8,128)(2,1)S(1)} %get-tuple-element.345), channel_id=1, source_target_pairs={{0,16},{1,17},{2,18},{3,19},{4,20},{5,21},{6,22},{7,23},{8,24},{9,... | collective-permute-start | bytes 688136 | tf_op jit(solution)/shard_map/ppermute | solution.py:190
  (87 other events, 844.4 us)
